TPU v7x, 32 devices: a whole 2x2x4 slice. The times are simulated.
32 devices in a mesh: dp: 8 (over z, x), mp: 4 (over y, core).
Axes of the slice: x: 2, y: 2, z: 4, core: 2. Of those that a mesh axis runs over, the one named last changes fastest.
Arguments:
- inputs: float32 [8, 1024, 768], P('dp', None, 'mp'), may hold values from -6 to 6
- lengths: int32 [8], P('dp'), may hold values from 64 to 1024, as said below
- ln1_gain: float32 [768], P('mp'), may hold values from 0.5 to 1.5
- ln1_bias: float32 [768], P('mp'), may hold values from -3 to 3
- w_query: float32 [768, 768], P(None, 'mp'), may hold values from -0.21875 to 0.21875
- w_key: float32 [768, 768], P(None, 'mp'), may hold values from -0.21875 to 0.21875
- w_value: float32 [768, 768], P(None, 'mp'), may hold values from -0.21875 to 0.21875
- query_bias: float32 [768], P('mp'), may hold values from -3 to 3
- value_bias: float32 [768], P('mp'), may hold values from -3 to 3
- pair_bias: float32 [1024, 256], replicated, may hold values from -3 to 3
- w_out: float32 [768, 768], P('mp'), may hold values from -0.875 to 0.875
- out_bias: float32 [768], P('mp'), may hold values from -3 to 3
- ln2_gain: float32 [768], P('mp'), may hold values from 0.5 to 1.5
- ln2_bias: float32 [768], P('mp'), may hold values from -3 to 3
- w_up: float32 [768, 3072], P(None, 'mp'), may hold values from -0.21875 to 0.21875
- up_bias: float32 [3072], P('mp'), may hold values from -3 to 3
- w_down: float32 [3072, 768], P('mp'), may hold values from -0.109375 to 0.109375
- down_bias: float32 [768], P('mp'), may hold values from -3 to 3
- cotangent: float32 [8, 1024, 768], P('dp', None, 'mp'), may hold values from -6 to 6
Outputs:
- result: float32 [8, 1024, 768], P('dp', None, 'mp')
- d_inputs: float32 [8, 1024, 768], P('dp', None, 'mp')
- d_ln1_gain: float32 [768], P('mp')
- d_ln1_bias: float32 [768], P('mp')
- d_w_query: float32 [768, 768], P(None, 'mp')
- d_w_key: float32 [768, 768], P(None, 'mp')
- d_w_value: float32 [768, 768], P(None, 'mp')
- d_query_bias: float32 [768], P('mp')
- d_value_bias: float32 [768], P('mp')
- d_pair_bias: float32 [1024, 256], replicated
- d_w_out: float32 [768, 768], P('mp')
- d_out_bias: float32 [768], P('mp')
- d_ln2_gain: float32 [768], P('mp')
- d_ln2_bias: float32 [768], P('mp')
- d_w_up: float32 [768, 3072], P(None, 'mp')
- d_up_bias: float32 [3072], P('mp')
- d_w_down: float32 [3072, 768], P('mp')
- d_down_bias: float32 [768], P('mp')
Inputs may be any that keep to these rules, and one draw needn't show every extreme that they name: `lengths`: some row of every draw has exactly 1024 live positions.
All inputs are finite; a program needn't handle non-finite values.
Results may differ from a plain program's by a relative error of at most 0.0003.
Values sent between devices are 32-bit elements; how exact they have to be, the bound alone decides.
No kernel may reach another device: no remote copies, remote signals or barrier semaphores. Data moves between devices by JAX's collectives and lax.ppermute only.
A program may use at most 192 MiB of HBM per device.

v0:
```python
from functools import partial

import jax
import jax.numpy as jnp
from jax import lax
from jax.sharding import PartitionSpec as P

D = 768
WIN = 256
QB = 512


EXACT_MODE = lax.Precision.HIGHEST
EPSILON = 1e-05


def exact_dot(left_arr, right_arr):
    return jnp.dot(left_arr, right_arr, precision=EXACT_MODE, preferred_element_type=jnp.float32)


def exact_tdot(left_arr, right_arr):
    return lax.dot_general(
        left_arr,
        right_arr,
        (((0,), (0,)), ((), ())),
        precision=EXACT_MODE,
        preferred_element_type=jnp.float32,
    )


def exact_cdot(left_arr, right_arr):
    return lax.dot_general(
        left_arr,
        right_arr,
        (((1,), (1,)), ((), ())),
        precision=EXACT_MODE,
        preferred_element_type=jnp.float32,
    )


def row_norm(values_in):
    row_mean = jnp.mean(values_in, axis=-1, keepdims=True)
    row_var = jnp.mean(values_in * values_in, axis=-1, keepdims=True) - row_mean * row_mean
    row_scale = lax.rsqrt(row_var + EPSILON)
    return ((values_in - row_mean) * row_scale, row_scale)


def norm_back(d_normed, gain_vec, normal_rows, row_scale):
    scaled = d_normed * gain_vec
    centered = scaled - jnp.mean(scaled, axis=-1, keepdims=True)
    return row_scale * (
        centered - normal_rows * jnp.mean(scaled * normal_rows, axis=-1, keepdims=True)
    )


def smooth_gate(values_in):
    return jax.nn.gelu(values_in, approximate=True)


def band_matrix(band_exp, begin_at):
    block_rows, window = band_exp.shape
    skew_width = block_rows + window - 1
    flipped = band_exp[:, ::-1]
    widened = jnp.pad(flipped, ((0, 0), (0, skew_width + 1 - window)))
    skewed = widened.reshape(-1)[: block_rows * skew_width].reshape(block_rows, skew_width)
    placed = jnp.pad(skewed, ((0, 0), (begin_at, 0)))[:, window - 1 :]
    query_pos = begin_at + jnp.arange(block_rows, dtype=jnp.int32)[:, None]
    key_pos = jnp.arange(begin_at + block_rows, dtype=jnp.int32)[None, :]
    distant = (query_pos - key_pos >= window).astype(jnp.float32)
    return placed + distant


def band_values(grid, begin_at, window):
    block_rows = grid.shape[0]
    skew_width = block_rows + window - 1
    shifted = jnp.pad(grid, ((0, 0), (window - 1, 0)))[:, begin_at : begin_at + skew_width]
    flat_cells = jnp.pad(shifted.reshape(-1), (0, block_rows))
    return flat_cells.reshape(block_rows, skew_width + 1)[:, :window][:, ::-1]


def mix_forward(pieces, pair_exp, skipping):
    queries_row, keys_row, values_row, length_row = pieces
    span_len, channels = queries_row.shape
    exp_keys = jnp.exp(keys_row)
    carried = exp_keys * values_row
    blocks = []
    for begin_at in range(0, span_len, QB):
        finish = begin_at + QB

        def compute(begin_at=begin_at, finish=finish):
            weights = band_matrix(pair_exp[begin_at:finish], begin_at)
            numerator = exact_dot(weights, carried[:finish])
            denominator = exact_dot(weights, exp_keys[:finish])
            return jax.nn.sigmoid(queries_row[begin_at:finish]) * numerator / denominator

        block_out = compute()
        blocks.append(block_out)
    return jnp.concatenate(blocks, axis=0)


def mix_backward(pieces, pair_exp):
    queries_row, keys_row, values_row, length_row, grad_row = pieces
    span_len, channels = queries_row.shape
    exp_keys = jnp.exp(keys_row)
    carried = exp_keys * values_row
    back_num = jnp.zeros((span_len, channels), jnp.float32)
    back_den = jnp.zeros((span_len, channels), jnp.float32)
    query_blocks = []
    pair_blocks = []
    for begin_at in range(0, span_len, QB):
        finish = begin_at + QB

        def compute(begin_at=begin_at, finish=finish):
            weights = band_matrix(pair_exp[begin_at:finish], begin_at)
            numerator = exact_dot(weights, carried[:finish])
            denominator = exact_dot(weights, exp_keys[:finish])
            quotient = numerator / denominator
            gate_open = jax.nn.sigmoid(queries_row[begin_at:finish])
            grad_block = grad_row[begin_at:finish]
            d_queries = grad_block * quotient * gate_open * (1.0 - gate_open)
            d_numer = grad_block * gate_open / denominator
            d_denom = -d_numer * quotient
            into_num = exact_tdot(weights, d_numer)
            into_den = exact_tdot(weights, d_denom)
            d_weights = exact_cdot(d_numer, carried[:finish]) + exact_cdot(
                d_denom, exp_keys[:finish]
            )
            d_band = band_values(d_weights, begin_at, WIN) * pair_exp[begin_at:finish]
            return (d_queries, into_num, into_den, d_band)

        d_queries, into_num, into_den, d_band = compute()
        back_num = back_num + jnp.pad(into_num, ((0, span_len - finish), (0, 0)))
        back_den = back_den + jnp.pad(into_den, ((0, span_len - finish), (0, 0)))
        query_blocks.append(d_queries)
        pair_blocks.append(d_band)
    d_values = exp_keys * back_num
    d_keys = exp_keys * (values_row * back_num + back_den)
    return (
        jnp.concatenate(query_blocks, axis=0),
        d_keys,
        d_values,
        jnp.concatenate(pair_blocks, axis=0),
    )


def body(
    inputs,
    lengths,
    ln1_gain,
    ln1_bias,
    w_query,
    w_key,
    w_value,
    query_bias,
    value_bias,
    pair_bias,
    w_out,
    out_bias,
    ln2_gain,
    ln2_bias,
    w_up,
    up_bias,
    w_down,
    down_bias,
    cotangent,
):
    seq_rows, span_len, channels = inputs.shape
    token_count = seq_rows * span_len
    offset = lax.axis_index("mp") * channels
    live_mask = (jnp.arange(span_len, dtype=jnp.int32)[None, :] < lengths[:, None]).astype(
        jnp.float32
    )
    live_mask = live_mask.reshape(token_count, 1)
    whole_x, gain_one, bias_one, bias_out, gain_two, bias_two = (
        lax.all_gather(inputs, "mp", axis=2, tiled=True),
        lax.all_gather(ln1_gain, "mp", axis=0, tiled=True),
        lax.all_gather(ln1_bias, "mp", axis=0, tiled=True),
        lax.all_gather(out_bias, "mp", axis=0, tiled=True),
        lax.all_gather(ln2_gain, "mp", axis=0, tiled=True),
        lax.all_gather(ln2_bias, "mp", axis=0, tiled=True),
    )
    whole_x = whole_x.reshape(token_count, D)
    normal_one, scale_one = row_norm(whole_x)
    normed1 = normal_one * gain_one + bias_one
    queries = exact_dot(normed1, w_query) + query_bias
    key_proj = exact_dot(normed1, w_key)
    value_proj = exact_dot(normed1, w_value) + value_bias
    pair_exp = jnp.exp(pair_bias)
    shaped = (
        queries.reshape(seq_rows, span_len, channels),
        key_proj.reshape(seq_rows, span_len, channels),
        value_proj.reshape(seq_rows, span_len, channels),
        lengths,
    )
    mixed_rows = lax.map(partial(mix_forward, pair_exp=pair_exp, skipping=False), shaped)
    mixed_rows = mixed_rows.reshape(token_count, channels)
    out_terms = exact_dot(mixed_rows, w_out)
    attn_rows = lax.psum(out_terms, "mp")
    whole_inner = whole_x + live_mask * (attn_rows + bias_out)
    normal_two, scale_two = row_norm(whole_inner)
    inner_rows = lax.dynamic_slice_in_dim(whole_inner, offset, channels, 1)
    normed2 = normal_two * gain_two + bias_two
    hidden_pre = exact_dot(normed2, w_up) + up_bias
    hidden_act, gate_pull = jax.vjp(smooth_gate, hidden_pre)
    down_terms = exact_dot(hidden_act, w_down)
    result = inner_rows + live_mask * (
        lax.psum_scatter(down_terms, "mp", scatter_dimension=1, tiled=True) + down_bias
    )
    whole_cot = lax.all_gather(cotangent, "mp", axis=2, tiled=True).reshape(token_count, D)
    branch_two = live_mask * whole_cot
    d_down_bias = jnp.sum(live_mask * cotangent.reshape(token_count, channels), axis=0)
    d_w_down = exact_tdot(hidden_act, branch_two)
    (d_pre,) = gate_pull(exact_cdot(branch_two, w_down))
    d_up_bias = jnp.sum(d_pre, axis=0)
    d_w_up = exact_tdot(normed2, d_pre)
    d_normed2 = lax.psum(exact_cdot(d_pre, w_up), "mp")
    d_gain_two = lax.dynamic_slice_in_dim(
        jnp.sum(d_normed2 * normal_two, axis=0), offset, channels, 0
    )
    d_bias_two = lax.dynamic_slice_in_dim(jnp.sum(d_normed2, axis=0), offset, channels, 0)
    d_inner = whole_cot + norm_back(d_normed2, gain_two, normal_two, scale_two)
    branch_one = live_mask * d_inner
    d_out_bias = lax.dynamic_slice_in_dim(jnp.sum(branch_one, axis=0), offset, channels, 0)
    d_w_out = exact_tdot(mixed_rows, branch_one)
    d_mixed = exact_cdot(branch_one, w_out)

    def back_step(pair_total, pieces):
        d_queries, d_keys, d_values, d_band = mix_backward(pieces, pair_exp)
        return (pair_total + d_band, (d_queries, d_keys, d_values))

    pair_total, (d_queries, d_keys, d_values) = lax.scan(
        back_step,
        jnp.zeros((span_len, WIN), jnp.float32),
        shaped + (d_mixed.reshape(seq_rows, span_len, channels),),
    )
    d_queries = d_queries.reshape(token_count, channels)
    d_keys = d_keys.reshape(token_count, channels)
    d_values = d_values.reshape(token_count, channels)
    d_query_bias = jnp.sum(d_queries, axis=0)
    d_value_bias = jnp.sum(d_values, axis=0)
    d_w_query = exact_tdot(normed1, d_queries)
    d_w_key = exact_tdot(normed1, d_keys)
    d_w_value = exact_tdot(normed1, d_values)
    d_normed1 = lax.psum(
        exact_cdot(d_queries, w_query) + exact_cdot(d_keys, w_key) + exact_cdot(d_values, w_value),
        "mp",
    )
    d_gain_one = lax.dynamic_slice_in_dim(
        jnp.sum(d_normed1 * normal_one, axis=0), offset, channels, 0
    )
    d_bias_one = lax.dynamic_slice_in_dim(jnp.sum(d_normed1, axis=0), offset, channels, 0)
    d_whole = d_inner + norm_back(d_normed1, gain_one, normal_one, scale_one)
    d_inputs = lax.dynamic_slice_in_dim(d_whole, offset, channels, 1).reshape(
        seq_rows, span_len, channels
    )
    grad_sums = lax.psum(
        (
            d_gain_one,
            d_bias_one,
            d_w_query,
            d_w_key,
            d_w_value,
            d_query_bias,
            d_value_bias,
            d_w_out,
            d_out_bias,
            d_gain_two,
            d_bias_two,
            d_w_up,
            d_up_bias,
            d_w_down,
            d_down_bias,
        ),
        "dp",
    )
    d_pair_bias = lax.psum(pair_total, ("dp", "mp"))
    return (
        result.reshape(seq_rows, span_len, channels),
        d_inputs,
        grad_sums[0],
        grad_sums[1],
        grad_sums[2],
        grad_sums[3],
        grad_sums[4],
        grad_sums[5],
        grad_sums[6],
        d_pair_bias,
        grad_sums[7],
        grad_sums[8],
        grad_sums[9],
        grad_sums[10],
        grad_sums[11],
        grad_sums[12],
        grad_sums[13],
        grad_sums[14],
    )


def solution(mesh):
    return jax.shard_map(
        body,
        mesh=mesh,
        in_specs=(
            P("dp", None, "mp"),
            P("dp"),
            P("mp"),
            P("mp"),
            P(None, "mp"),
            P(None, "mp"),
            P(None, "mp"),
            P("mp"),
            P("mp"),
            P(),
            P("mp", None),
            P("mp"),
            P("mp"),
            P("mp"),
            P(None, "mp"),
            P("mp"),
            P("mp", None),
            P("mp"),
            P("dp", None, "mp"),
        ),
        out_specs=(
            P("dp", None, "mp"),
            P("dp", None, "mp"),
            P("mp"),
            P("mp"),
            P(None, "mp"),
            P(None, "mp"),
            P(None, "mp"),
            P("mp"),
            P("mp"),
            P(),
            P("mp", None),
            P("mp"),
            P("mp"),
            P("mp"),
            P(None, "mp"),
            P("mp"),
            P("mp", None),
            P("mp"),
        ),
        check_vma=False,
    )
```

profile of v0, /device:TPU:0, one launch (start us, length us, event | category | flops | bytes accessed | tf_op | source)
XLA Modules:
  0.0 803.8 jit_solution(12701246873645002920)
XLA Ops:
  23.7 4.1 reshape.195
  31.6 4.1 reshape.193
  38.2 12.6 %all-reduce.15 = (f32[768]{0:T(1024)S(1)}, f32[768]{0:T(1024)S(1)}, f32[768]{0:T(1024)S(1)}, f32[768]{0:T(1024)S(1)}, f32[768]{0:T(1024)S(1)}) all-reduce(f32[768]{0:T(1024)S(1)} %dynamic-update-slice.1, f32[768]{0:T(1024)S(1)} %dynamic-update-slice, f32[768]{0:T(1024)S(1)} %dynamic-update-slice.2, ...), channel_id=1, replica_groups=mesh['dp'=8,'mp'=4] {'mp'}, use_global_device_ids=true, to_apply=%add.9 | all-reduce | flops 3840 | bytes 30720
  50.8 9.0 %copy.49 = f32[1,1024,768]{2,1,0:T(8,128)} copy(f32[1,1024,768]{1,0,2:T(1,128)} %all-gather.3.cloned.1.call-done) | data formatting | bytes 6291456 | tf_op jit(solution)/shard_map/all_gather | solution.py:175
  88.7 4.4 fusion.38
  93.9 8.8 %copy.52 = f32[1,1024,768]{2,1,0:T(8,128)} copy(f32[1,1024,768]{1,0,2:T(1,128)} %all-gather.5.cloned.1.call-done) | data formatting | bytes 6291456 | tf_op jit(solution)/shard_map/all_gather | solution.py:209
  102.7 59.4 %all-reduce.22.cloned.1.call-done = f32[1024,768]{1,0:T(8,128)} async-done(((f32[1024,768]{1,0:T(8,128)}), f32[1024,768]{1,0:T(8,128)}) %all-reduce.22.cloned.1.call-update) | async-done | bytes 3145744 | tf_op jit(solution)/shard_map/psum | solution.py:198
  162.2 3.9 fusion.85
  166.2 8.4 %fusion.11 = f32[1024,768]{1,0:T(8,128)S(1)} fusion(f32[768,768]{1,0:T(8,128)S(1)} %copy-done.56, f32[1024,768]{1,0:T(8,128)S(1)} %get-tuple-element.157, f32[768]{0:T(1024)S(1)} %get-tuple-element.148, f32[768]{0:T(1024)S(1)} %get-tuple-element.149, f32[1024]{0:T(1024)S(1)} %get-tuple-element.172, f32[1024]{0:T(1024)S(1)} %get-tuple-element.171), kind=kOutput, calls=%fused_computation.28 | convolution fusion | flops 7250903040 | bytes 8665088 | tf_op jit(solution)/shard_map/dot_general | solution.py:18
  174.6 10.9 %fusion.90 = (f32[768]{0:T(1024)}, f32[1024,768]{1,0:T(8,128)S(1)}) fusion(f32[1024,768]{1,0:T(8,128)S(1)} %fusion.11, f32[768]{0:T(1024)S(1)} %copy-done.84, f32[768,768]{1,0:T(8,128)S(1)} %copy-done, f32[1,1024,768]{2,1,0:T(8,128)S(1)} %copy-done.14, f32[1024]{0:T(1024)S(1)} %fusion.55), kind=kOutput, calls=%fused_computation.149 | convolution fusion | flops 7265057792 | bytes 11806720 | tf_op jit(solution)/shard_map/dot_general | solution.py:32
  187.2 9.5 %fusion.91 = f32[1024,768]{1,0:T(8,128)} fusion(f32[1024,768]{1,0:T(8,128)S(1)} %get-tuple-element.181, f32[768,768]{1,0:T(8,128)S(1)} %copy-done.56), kind=kOutput, calls=%fused_computation.150 | convolution fusion | flops 7247757312 | bytes 8650752 | tf_op jit(solution)/shard_map/dot_general | solution.py:32
  196.8 68.6 %all-reduce.24.cloned.1.call-done = f32[1024,768]{1,0:T(8,128)} async-done(((f32[1024,768]{1,0:T(8,128)}), f32[1024,768]{1,0:T(8,128)}) %all-reduce.24.cloned.1.call-update) | async-done | bytes 3145744 | tf_op jit(solution)/shard_map/psum | solution.py:216
  265.5 4.5 multiply_reduce_fusion
  292.4 4.9 add_add_fusion
  298.0 11.2 %convolution_bitcast_fusion = f32[768,1024]{1,0:T(8,128)} fusion(f32[768,768]{1,0:T(8,128)S(1)} %copy-done, f32[1024,768]{1,0:T(8,128)} %copy-done.89, f32[768]{0:T(1024)S(1)} %copy-done.85), kind=kOutput, calls=%fused_computation.38 | convolution fusion | flops 7254835200 | bytes 8653824
  311.1 11.7 %fusion.10 = f32[768,768]{1,0:T(8,128)} fusion(f32[1024,768]{1,0:T(8,128)} %copy-done.43, f32[1024,768]{1,0:T(8,128)S(1)} %copy-done.8, f32[768]{0:T(1024)} %copy-done.87, f32[768]{0:T(1024)} %copy-done.71, f32[1024]{0:T(1024)} %copy-done.68, f32[1024]{0:T(1024)} %copy-done.67), kind=kOutput, calls=%fused_computation.27 | convolution fusion | flops 7250903040 | bytes 8665088 | tf_op jit(solution)/shard_map/dot_general | solution.py:22
  322.9 10.5 %fusion.8 = f32[768,768]{1,0:T(8,128)} fusion(f32[1,1024,768]{2,1,0:T(8,128)S(1)} %copy-done.16, f32[1024]{0:T(1024)S(1)} %fusion.55, f32[1024,768]{1,0:T(8,128)S(1)} %copy-done.90, f32[768]{0:T(1024)S(1)} %copy-done.86), kind=kOutput, calls=%fused_computation.24 | convolution fusion | flops 7255621632 | bytes 8657920 | tf_op jit(solution)/shard_map/dot_general | solution.py:22
  355.8 5.3 rev.23
  363.8 4.5 fusion.33
  372.1 5.7 fusion.12
  396.4 10.0 %reduce-scatter.4.cloned.1.call-done = f32[192,1024]{1,0:T(8,128)} async-done(((f32[768,1024]{1,0:T(8,128)}), f32[192,1024]{1,0:T(8,128)}) %reduce-scatter.4.cloned.1.call-update) | async-done | bytes 786448
  411.1 37.2 %all-reduce.13 = (f32[192]{0:T(256)}, f32[192]{0:T(256)}, f32[192]{0:T(256)}, f32[192]{0:T(256)}, f32[192]{0:T(256)}, /*index=5*/f32[192]{0:T(256)}, f32[192]{0:T(256)}, f32[768]{0:T(1024)}, f32[192]{0:T(256)}) all-reduce(f32[192]{0:T(256)S(1)} %dynamic_slice.38, f32[192]{0:T(256)S(1)} %dynamic_slice.39, ...), channel_id=1, replica_groups=mesh['dp'=8,'mp'=4] {'dp'}, use_global_device_ids=true, to_apply=%region_13.14 | all-reduce | flops 2304 | bytes 18432 | tf_op jit(solution)/shard_map/psum | solution.py:256
  448.3 94.2 %all-reduce.28.cloned.1.call-done = f32[1024,256]{1,0:T(8,128)} async-done(((f32[1024,256]{1,0:T(8,128)}), f32[1024,256]{1,0:T(8,128)}) %all-reduce.28.cloned.1.call-update) | async-done | bytes 1048592 | tf_op jit(solution)/shard_map/psum | solution.py:276
  542.5 243.2 %all-reduce.30.cloned.1.call-done = (f32[768,192]{0,1:T(8,128)}, f32[768,192]{0,1:T(8,128)}, f32[768,192]{0,1:T(8,128)}, f32[192,768]{1,0:T(8,128)}, f32[768,768]{1,0:T(8,128)}, /*index=5*/f32[768,768]{1,0:T(8,128)}) async-done(((f32[768,192]{0,1:T(8,128)}, f32[768,192]{0,1:T(8,128)}, f32[768,192]{0,1:T(8,128)}, f32[192,768]{1,0:T(8,128)}, f32[768,768]{1,0:T(8,128)}, /*index=5*/f32[768,768]{1,0:T(8,128)}), ...) | async-done | bytes 7077904 | tf_op jit(solution)/shard_map/psum | solution.py:256
  (287 shorter events, 140.1 us)
Async XLA Ops:
  7.2 167.4 %copy-start = (f32[768,768]{1,0:T(8,128)S(1)}, f32[768,768]{1,0:T(8,128)}, u32[]{:S(2)}) copy-start(f32[768,768]{1,0:T(8,128)} %param.35) | copy-start | bytes 7077892
  7.2 43.6 %all-gather.3.cloned.1.call-start = ((), (), s32[]{:S(2)}) async-start(), calls=%async_computation.1 | async-start | bytes 3932160 | tf_op jit(solution)/shard_map/all_gather | solution.py:175
  10.3 83.6 %all-gather.5.cloned.1.call-start = ((), (), s32[]{:S(2)}) async-start(), calls=%async_computation.3 | async-start | bytes 3932160 | tf_op jit(solution)/shard_map/all_gather | solution.py:209
  13.2 149.0 %all-reduce.22.cloned.1.call-start = ((), (), s32[]{:S(2)}) async-start(), calls=%async_computation.2 | async-start | bytes 6291456 | tf_op jit(solution)/shard_map/psum | solution.py:198
  50.7 115.4 %copy-start.87 = (f32[768]{0:T(1024)}, f32[768]{0:T(1024)S(1)}, u32[]{:S(2)}) copy-start(f32[768]{0:T(1024)S(1)} %get-tuple-element.148) | copy-start | bytes 9220
  50.7 219.2 %copy-start.71 = (f32[768]{0:T(1024)}, f32[768]{0:T(1024)S(1)}, u32[]{:S(2)}) copy-start(f32[768]{0:T(1024)S(1)} %get-tuple-element.149) | copy-start | bytes 9220
  50.8 26.8 %copy-start.69 = (s32[512]{0:T(512)}, s32[512]{0:T(512)S(1)}, u32[]{:S(2)}) copy-start(s32[512]{0:T(512)S(1)} %iota_add_fusion) | copy-start | bytes 6148
  66.7 15.2 %copy-start.2 = (f32[1024,768]{1,0:T(8,128)}, f32[1024,768]{1,0:T(8,128)S(1)}, u32[]{:S(2)}) copy-start(f32[1024,768]{1,0:T(8,128)S(1)} %fusion.6) | copy-start | bytes 9437188
  74.7 217.7 %copy-start.9 = (f32[1024,192]{0,1:T(8,128)}, f32[1024,192]{0,1:T(8,128)S(1)}, u32[]{:S(2)}) copy-start(f32[1024,192]{0,1:T(8,128)S(1)} %get-tuple-element.176) | copy-start | bytes 2359300
  93.2 172.3 %all-reduce.24.cloned.1.call-start = ((), (), s32[]{:S(2)}) async-start(), calls=%async_computation.4 | async-start | bytes 6291456 | tf_op jit(solution)/shard_map/psum | solution.py:216
  166.1 19.4 %copy-start.6 = (f32[1024,768]{1,0:T(8,128)}, f32[1024,768]{1,0:T(8,128)S(1)}, u32[]{:S(2)}) copy-start(f32[1024,768]{1,0:T(8,128)S(1)} %get-tuple-element.157) | copy-start | bytes 9437188
  166.1 103.8 %copy-start.67 = (f32[1024]{0:T(1024)}, f32[1024]{0:T(1024)S(1)}, u32[]{:S(2)}) copy-start(f32[1024]{0:T(1024)S(1)} %get-tuple-element.171) | copy-start | bytes 12292
  166.1 103.8 %copy-start.68 = (f32[1024]{0:T(1024)}, f32[1024]{0:T(1024)S(1)}, u32[]{:S(2)}) copy-start(f32[1024]{0:T(1024)S(1)} %get-tuple-element.172) | copy-start | bytes 12292
  196.8 189.4 %all-reduce.26.cloned.1.call-start = ((), (), s32[]{:S(2)}) async-start(), calls=%async_computation.5 | async-start | bytes 6291456 | tf_op jit(solution)/shard_map/psum | solution.py:244
  273.7 12.3 %copy-start.5 = (f32[1024,768]{1,0:T(8,128)}, f32[1024,768]{1,0:T(8,128)S(1)}, u32[]{:S(2)}) copy-start(f32[1024,768]{1,0:T(8,128)S(1)} %get-tuple-element.151) | copy-start | bytes 9437188
  297.3 109.2 %reduce-scatter.4.cloned.1.call-start = ((), (), s32[]{:S(2)}) async-start(), calls=%async_computation.7 | async-start | bytes 3932160
  309.2 233.3 %all-reduce.28.cloned.1.call-start = ((), (), s32[]{:S(2)}) async-start(), calls=%async_computation.6 | async-start | bytes 2097152 | tf_op jit(solution)/shard_map/psum | solution.py:276
  311.1 11.7 %copy-start.16 = (f32[1,1024,768]{2,1,0:T(8,128)S(1)}, f32[1,1024,768]{2,1,0:T(8,128)}, u32[]{:S(2)}) copy-start(f32[1,1024,768]{2,1,0:T(8,128)} %copy.52) | copy-start | bytes 9437188
  311.1 11.7 %copy-start.86 = (f32[768]{0:T(1024)S(1)}, f32[768]{0:T(1024)}, u32[]{:S(2)}) copy-start(f32[768]{0:T(1024)} %param.34) | copy-start | bytes 9220
  311.1 11.7 %copy-start.90 = (f32[1024,768]{1,0:T(8,128)S(1)}, f32[1024,768]{1,0:T(8,128)}, u32[]{:S(2)}) copy-start(f32[1024,768]{1,0:T(8,128)} %copy-done.89) | copy-start | bytes 9437188
  371.9 413.8 %all-reduce.30.cloned.1.call-start = ((), (), s32[]{:S(2)}) async-start(), calls=%async_computation.8 | async-start | bytes 14155776 | tf_op jit(solution)/shard_map/psum | solution.py:256
  390.2 17.8 %copy-start.78 = (f32[192]{0:T(256)S(1)}, f32[192]{0:T(256)}, u32[]{:S(2)}) copy-start(f32[192]{0:T(256)} %param.36) | copy-start | bytes 2308
  393.9 14.0 %copy-start.30 = (f32[1,1024,192]{2,1,0:T(8,128)S(1)}, f32[1,1024,192]{2,1,0:T(8,128)}, u32[]{:S(2)}) copy-start(f32[1,1024,192]{2,1,0:T(8,128)} %copy.54) | copy-start | bytes 2359300
  542.5 249.1 %copy-start.63 = (f32[1024,256]{1,0:T(8,128)S(1)}, f32[1024,256]{1,0:T(8,128)}, u32[]{:S(2)}) copy-start(f32[1024,256]{1,0:T(8,128)} %all-reduce.28.cloned.1.call-done) | copy-start | bytes 3145732
  (75 other events, 384.0 us)
Sparse Core Ops, SparseCore 0:
  10.4 31.2 all-gather.2
  43.8 28.5 all-gather.4
  93.3 68.8 all-reduce.21
  196.9 68.5 all-reduce.23
  297.4 68.5 all-reduce.25
  368.4 38.0 reduce-scatter.3
  412.5 129.9 all-reduce.27
  549.3 236.3 all-reduce.29
where the time goes:
time: 811 us; the launch traced here: 804 us
  waiting for transfers between devices  476 us (59%)
  matrix products  132 us (16%)
  local copies, waits for them, and re-layouts  95.3 us (12%)
  blocking collectives  49.8 us (6%)
  other arithmetic  33.5 us (4%)
  between operations  16.7 us (2%)
    psum x1, waiting for transfers between devices, body(): lax.psum((d_gain_one, d_bias_one, d_w_query, d_w_key, d_w_value, d_query_...  243 us
    psum x1, waiting for transfers between devices, body(): d_pair_bias = lax.psum(pair_total, ('dp', 'mp'))  94.2 us
    psum x1, waiting for transfers between devices, body(): d_normed2 = lax.psum(exact_cdot(d_pre, w_up), 'mp')  68.6 us
    psum x1, waiting for transfers between devices, body(): attn_rows = lax.psum(out_terms, 'mp')  59.4 us
    dot_general x10, matrix products, exact_tdot(): lax.dot_general(left_arr, right_arr, (((0,), (0,)), ((), ())), precision=...  46.7 us
    dot_general x10, matrix products, exact_cdot(): lax.dot_general(left_arr, right_arr, (((1,), (1,)), ((), ())), precision=...  41.3 us
    psum x1, blocking collectives, body(): lax.psum((d_gain_one, d_bias_one, d_w_query, d_w_key, d_w_value, d_query_...  37.2 us
    dot_general x9, matrix products, exact_dot(): jnp.dot(left_arr, right_arr, precision=EXACT_MODE, preferred_element_type...  32.9 us
  transfers between devices with their start and end apart: 8, of which 5 were waited for; matrix products, arithmetic and copies ran while one was open for 22% of the time, Pallas kernels for 0%

commit v1 on v0

v1 whole, which is shorter than its diff:
```python
import jax
import jax.numpy as jnp
from jax import lax
from jax.sharding import PartitionSpec as P

MODE = lax.Precision.HIGH
EPSILON = 1e-05


def dot_nn(left_arr, right_arr):
    return lax.dot_general(
        left_arr, right_arr, (((1,), (0,)), ((), ())), precision=MODE, preferred_element_type=jnp.float32
    )


def dot_nt(left_arr, right_arr):
    return lax.dot_general(
        left_arr, right_arr, (((1,), (1,)), ((), ())), precision=MODE, preferred_element_type=jnp.float32
    )


def dot_tn(left_arr, right_arr):
    return lax.dot_general(
        left_arr, right_arr, (((0,), (0,)), ((), ())), precision=MODE, preferred_element_type=jnp.float32
    )


def swap(block, bit):
    return lax.ppermute(block, "mp", [(i, i ^ bit) for i in range(4)])


def gather_rows(own):
    rows, width = own.shape
    place = lax.axis_index("mp")
    far = swap(own, 2)
    near = swap(own, 1)
    far_near = swap(far, 1)
    whole = jnp.zeros((4 * rows, width), own.dtype)
    for flip, part in enumerate((own, near, far, far_near)):
        whole = lax.dynamic_update_slice(whole, part, ((place ^ flip) * rows, 0))
    return whole


def halve(grid, axis, bit):
    mine = lax.dynamic_index_in_dim(grid, bit, axis, keepdims=False)
    other = lax.dynamic_index_in_dim(grid, 1 - bit, axis, keepdims=False)
    return mine, other


def reduce_core(terms):
    rows, width = terms.shape[0] // 4, terms.shape[1]
    place = lax.axis_index("mp")
    mine, other = halve(terms.reshape(2, 2, rows, width), 1, place & 1)
    return mine + swap(other, 1)


def scatter_sum(terms):
    place = lax.axis_index("mp")
    mine, other = halve(reduce_core(terms), 0, place >> 1)
    return mine + swap(other, 2)


def whole_sum(terms):
    place = lax.axis_index("mp")
    half = reduce_core(terms)
    half = half + swap(half, 2)
    other = swap(half, 1)
    odd = (place & 1) == 1
    both = jnp.stack([jnp.where(odd, other, half), jnp.where(odd, half, other)], axis=1)
    return both.reshape(terms.shape)


def column_norm(values_in):
    mean = jnp.mean(values_in, axis=0, keepdims=True)
    var = jnp.mean(values_in * values_in, axis=0, keepdims=True) - mean * mean
    scale = lax.rsqrt(var + EPSILON)
    return (values_in - mean) * scale, scale


def band_blocks(pair_exp):
    span, window = pair_exp.shape
    count = span // window
    flipped = pair_exp.reshape(count, window, window)[:, :, ::-1]
    wide = jnp.pad(flipped, ((0, 0), (0, 0), (1, window)))
    skewed = wide.reshape(count, -1)[:, : window * 2 * window].reshape(count, window, 2 * window)
    query = jnp.arange(window, dtype=jnp.int32)[:, None]
    key = jnp.arange(2 * window, dtype=jnp.int32)[None, :]
    return skewed + (key <= query).astype(jnp.float32)[None]


def band_values(grid):
    window, wide = grid.shape
    flat = jnp.pad(grid.reshape(-1), (0, window))
    return flat.reshape(window, wide + 1)[:, 1 : window + 1][:, ::-1]


def body(
    inputs,
    lengths,
    ln1_gain,
    ln1_bias,
    w_query,
    w_key,
    w_value,
    query_bias,
    value_bias,
    pair_bias,
    w_out,
    out_bias,
    ln2_gain,
    ln2_bias,
    w_up,
    up_bias,
    w_down,
    down_bias,
    cotangent,
):
    seq_rows, span, chans = inputs.shape
    assert seq_rows == 1
    window = pair_bias.shape[1]
    count = span // window
    model = 4 * chans
    place = lax.axis_index("mp")
    live = (jnp.arange(span, dtype=jnp.int32) < lengths[0]).astype(jnp.float32)[None, :]

    def own_rows(whole):
        return lax.dynamic_slice_in_dim(whole, place * chans, chans, 0)

    x_own = inputs[0].T
    cot_own = cotangent[0].T
    vectors = jnp.stack([ln1_gain, ln1_bias, out_bias, ln2_gain, ln2_bias], axis=1)
    vectors = jnp.pad(vectors, ((0, 0), (0, 128 - vectors.shape[1])))
    gathered = gather_rows(jnp.concatenate([x_own, vectors], axis=1))
    whole_x = gathered[:, :span]
    gain_one, bias_one, bias_out, gain_two, bias_two = (
        gathered[:, span + i : span + i + 1] for i in range(5)
    )
    pair_exp = jnp.exp(pair_bias)
    bands = band_blocks(pair_exp)

    normal_one, scale_one = column_norm(whole_x)
    normed1 = normal_one * gain_one + bias_one
    w_qkv = jnp.concatenate([w_query.T, w_key.T, w_value.T], axis=0)
    projected = dot_nn(w_qkv, normed1)
    queries = projected[:chans] + query_bias[:, None]
    exp_keys = jnp.exp(projected[chans : 2 * chans])
    values = projected[2 * chans :] + value_bias[:, None]
    pair = jnp.concatenate([exp_keys * values, exp_keys], axis=0)
    sums = []
    far = jnp.zeros((2 * chans, 1), jnp.float32)
    for i in range(count):
        here = slice(i * window, (i + 1) * window)
        if i == 0:
            sums.append(dot_nt(pair[:, here], bands[i, :, window:]))
        else:
            near = pair[:, (i - 1) * window : (i + 1) * window]
            sums.append(dot_nt(near, bands[i]) + far)
            far = far + jnp.sum(pair[:, (i - 1) * window : i * window], axis=1, keepdims=True)
    sums = jnp.concatenate(sums, axis=1)
    denominator = sums[chans:]
    quotient = sums[:chans] / denominator
    gate_open = jax.nn.sigmoid(queries)
    mixed = gate_open * quotient

    w_out_whole = gather_rows(w_out)
    whole_cot = gather_rows(cot_own)
    mixed_whole = gather_rows(mixed)
    inner = whole_x + live * (dot_tn(w_out_whole, mixed_whole) + bias_out)
    normal_two, scale_two = column_norm(inner)
    normed2 = normal_two * gain_two + bias_two
    hidden_pre = dot_tn(w_up, normed2) + up_bias[:, None]
    hidden_act, gate_pull = jax.vjp(lambda v: jax.nn.gelu(v, approximate=True), hidden_pre)
    branch_two = live * whole_cot
    d_w_down = dot_nt(hidden_act, branch_two)
    (d_pre,) = gate_pull(dot_nn(w_down, branch_two))
    d_w_up = dot_nt(normed2, d_pre)
    d_up_bias = jnp.sum(d_pre, axis=1)
    d_down_bias = jnp.sum(live * cot_own, axis=1)
    d_normed2 = whole_sum(dot_nn(w_up, d_pre))
    ffn_grads = lax.psum((d_w_down, d_w_up), "dp")
    down_own = scatter_sum(dot_tn(w_down, hidden_act))
    result = own_rows(inner) + live * (down_own + down_bias[:, None])

    scaled_two = d_normed2 * gain_two
    d_inner = whole_cot + scale_two * (
        scaled_two
        - jnp.mean(scaled_two, axis=0, keepdims=True)
        - normal_two * jnp.mean(scaled_two * normal_two, axis=0, keepdims=True)
    )
    d_gain_two = jnp.sum(own_rows(d_normed2) * own_rows(normal_two), axis=1)
    d_bias_two = jnp.sum(own_rows(d_normed2), axis=1)
    branch_one = live * d_inner
    d_out_bias = jnp.sum(own_rows(branch_one), axis=1)
    d_w_out = dot_nt(mixed, branch_one)
    d_mixed = dot_nn(w_out, branch_one)

    d_queries = d_mixed * quotient * gate_open * (1.0 - gate_open)
    d_numer = d_mixed * gate_open / denominator
    d_pairs = jnp.concatenate([d_numer, -d_numer * quotient], axis=0)
    back = [None] * count
    d_bands = [None] * count
    later = jnp.zeros((2 * chans, 1), jnp.float32)
    for i in reversed(range(count)):
        here = slice(i * window, (i + 1) * window)
        before = slice(max(i - 1, 0) * window, (i + 1) * window)
        band = bands[i] if i else bands[i, :, window:]
        into = dot_nn(d_pairs[:, here], band)
        grid = dot_tn(d_pairs[:, here], pair[:, before])
        if i == 0:
            grid = jnp.pad(grid, ((0, 0), (window, 0)))
        d_bands[i] = band_values(grid)
        own_part = into[:, -window:] + later
        back[i] = own_part if back[i] is None else back[i] + own_part
        if i:
            back[i - 1] = into[:, :window]
            if i + 1 < count:
                ahead = slice((i + 1) * window, (i + 2) * window)
                later = later + jnp.sum(d_pairs[:, ahead], axis=1, keepdims=True)
    back = jnp.concatenate(back, axis=1)
    d_pair_bias = jnp.concatenate(d_bands, axis=0) * pair_exp
    d_values = exp_keys * back[:chans]
    d_keys = exp_keys * (values * back[:chans] + back[chans:])
    d_qkv = jnp.concatenate([d_queries, d_keys, d_values], axis=0)
    d_w_qkv = dot_nt(d_qkv, normed1)
    terms = dot_tn(w_qkv, d_qkv)
    scaled_terms = terms * gain_one
    stats = jnp.concatenate(
        [
            jnp.sum(scaled_terms, axis=0, keepdims=True),
            jnp.sum(scaled_terms * normal_one, axis=0, keepdims=True),
        ],
        axis=0,
    )
    stats = jnp.pad(stats, ((0, 6), (0, 0)))
    stats = stats + swap(stats, 1)
    stats = (stats + swap(stats, 2)) / model
    d_normed1 = scatter_sum(terms)
    normal_own = own_rows(normal_one)
    d_gain_one = jnp.sum(d_normed1 * normal_own, axis=1)
    d_bias_one = jnp.sum(d_normed1, axis=1)
    d_inputs = own_rows(d_inner) + scale_one * (
        d_normed1 * own_rows(gain_one) - stats[0:1] - normal_own * stats[1:2]
    )
    small = jnp.concatenate(
        [
            d_gain_one,
            d_bias_one,
            jnp.sum(d_queries, axis=1),
            jnp.sum(d_values, axis=1),
            d_out_bias,
            d_gain_two,
            d_bias_two,
            d_down_bias,
            d_up_bias,
        ]
    )
    d_w_qkv, d_w_out, small = lax.psum((d_w_qkv, d_w_out, small), "dp")
    d_pair_bias = lax.psum(d_pair_bias, ("dp", "mp"))
    vecs = [small[i * chans : (i + 1) * chans] for i in range(8)]
    return (
        result.T[None],
        d_inputs.T[None],
        vecs[0],
        vecs[1],
        d_w_qkv[:chans].T,
        d_w_qkv[chans : 2 * chans].T,
        d_w_qkv[2 * chans :].T,
        vecs[2],
        vecs[3],
        d_pair_bias,
        d_w_out,
        vecs[4],
        vecs[5],
        vecs[6],
        ffn_grads[1],
        small[8 * chans :],
        ffn_grads[0],
        vecs[7],
    )


def solution(mesh):
    rows = P("dp", None, "mp")
    vec = P("mp")
    out_dim = P(None, "mp")
    in_dim = P("mp", None)
    return jax.shard_map(
        body,
        mesh=mesh,
        in_specs=(
            rows, P("dp"), vec, vec, out_dim, out_dim, out_dim, vec, vec, P(), in_dim, vec, vec, vec,
            out_dim, vec, in_dim, vec, rows,
        ),
        out_specs=(
            rows, rows, vec, vec, out_dim, out_dim, out_dim, vec, vec, P(), in_dim, vec, vec, vec,
            out_dim, vec, in_dim, vec,
        ),
        check_vma=False,
    )
```

time: 811 us -> 695 us (0.86)
  waiting for transfers between devices: 476 us -> 404 us
  matrix products: 132 us -> 77.3 us
  starting transfers between devices: 0.68 us -> 14.4 us
  blocking collectives: 49.8 us -> 39.3 us
    psum x5 -> x2, waiting for transfers between devices: 466 us -> 272 us  [the longest x1 139 us: body(): d_w_qkv, d_w_out, small = lax.psum((d_w_qkv, d_w_out, small), 'dp')]
    ppermute x0 -> x21, waiting for transfers between devices: none -> 133 us  [swap(): return lax.ppermute(block, 'mp', [(i, i ^ bit) for i in range(4)])]
    dot_general x29 -> x24, matrix products: 121 us -> 77.3 us  [the longest x8 29.2 us: dot_nt(): lax.dot_general(left_arr, right_arr, (((1,), (1,)), ((), ())), precision=...]
    dynamic_update_slice x0 -> x13, local copies, waits for them, and re-layouts: none -> 19.1 us  [gather_rows(): whole = lax.dynamic_update_slice(whole, part, ((place ^ flip) * rows, 0))]
    all_gather x2 -> x0, local copies, waits for them, and re-layouts: 17.9 us -> none  [the longest x1 9.04 us: body(): lax.all_gather(inputs, 'mp', axis=2, tiled=True)]
    ppermute x0 -> x21, starting transfers between devices: none -> 14.3 us  [swap(): return lax.ppermute(block, 'mp', [(i, i ^ bit) for i in range(4)])]
    unnamed x1 -> x0, blocking collectives: 12.6 us -> none
    reduce_sum x9 -> x10, other arithmetic: 24.6 us -> 12.4 us  [the longest x1 3.37 us: body(): d_down_bias = jnp.sum(live * cot_own, axis=1)]
  transfers between devices with their start and end apart: 8 -> 23, of which waited for: 5 -> 11; matrix products, arithmetic and copies ran while one was open for 22% -> 16% of each run, Pallas kernels for 0% -> 0%
where the time goes in v1:
time: 695 us; the launch traced here: 684 us
  waiting for transfers between devices  404 us (58%)
  local copies, waits for them, and re-layouts  96.7 us (14%)
  matrix products  77.3 us (11%)
  blocking collectives  39.3 us (6%)
  other arithmetic  35.8 us (5%)
  between operations  16.1 us (2%)
  starting transfers between devices  14.4 us (2%)
    psum x1, waiting for transfers between devices, body(): d_w_qkv, d_w_out, small = lax.psum((d_w_qkv, d_w_out, small), 'dp')  139 us
    ppermute x21, waiting for transfers between devices, swap(): return lax.ppermute(block, 'mp', [(i, i ^ bit) for i in range(4)])  133 us
    psum x1, waiting for transfers between devices, body(): d_pair_bias = lax.psum(d_pair_bias, ('dp', 'mp'))  133 us
    psum x1, blocking collectives, body(): d_w_qkv, d_w_out, small = lax.psum((d_w_qkv, d_w_out, small), 'dp')  39.3 us
    dot_general x8, matrix products, dot_nt(): lax.dot_general(left_arr, right_arr, (((1,), (1,)), ((), ())), precision=...  29.2 us
    dot_general x8, matrix products, dot_tn(): lax.dot_general(left_arr, right_arr, (((0,), (0,)), ((), ())), precision=...  25.7 us
    dot_general x8, matrix products, dot_nn(): lax.dot_general(left_arr, right_arr, (((1,), (0,)), ((), ())), precision=...  22.4 us
    unnamed x125, local copies, waits for them, and re-layouts  21.3 us
  transfers between devices with their start and end apart: 23, of which 11 were waited for; matrix products, arithmetic and copies ran while one was open for 16% of the time, Pallas kernels for 0%

profile of v1, /device:TPU:0, one launch (start us, length us, event | category | flops | bytes accessed | tf_op | source)
XLA Modules:
  0.0 684.1 jit_solution(1836574850174201471)
XLA Ops:
  14.7 20.0 %collective-permute-done.1 = f32[192,1152]{1,0:T(8,128)} collective-permute-done((f32[192,1152]{1,0:T(8,128)}, f32[192,1152]{1,0:T(8,128)}, u32[]{:S(2)}, u32[]{:S(2)}) %collective-permute-start.1) | collective-permute-done | bytes 884768 | tf_op jit(solution)/shard_map/ppermute | solution.py:29
  37.1 9.3 %rev.15 = f32[4,256,256]{2,1,0:T(8,128)} reverse(f32[4,256,256]{2,1,0:T(8,128)} %bitcast.164), dimensions={2} | reverse | bytes 2097152 | tf_op jit(solution)/shard_map/rev | solution.py:83
  49.6 5.6 reshape.167
  87.8 30.4 %collective-permute-done.4 = f32[192,768]{1,0:T(8,128)} collective-permute-done((f32[192,768]{1,0:T(8,128)}, f32[192,768]{1,0:T(8,128)}, u32[]{:S(2)}, u32[]{:S(2)}) %collective-permute-start.4) | collective-permute-done | bytes 589856 | tf_op jit(solution)/shard_map/ppermute | solution.py:29
  128.2 6.3 fusion.88
  137.7 5.1 fusion.16
  142.9 4.7 fusion.31
  160.2 11.0 %collective-permute-done.12 = f32[192,1024]{1,0:T(8,128)} collective-permute-done((f32[192,1024]{1,0:T(8,128)}, f32[192,1024]{1,0:T(8,128)}, u32[]{:S(2)}, u32[]{:S(2)}) %collective-permute-start.12) | collective-permute-done | bytes 786464 | tf_op jit(solution)/shard_map/ppermute | solution.py:29
  171.2 16.4 %collective-permute-done.10 = f32[192,1024]{1,0:T(8,128)} collective-permute-done((f32[192,1024]{1,0:T(8,128)}, f32[192,1024]{1,0:T(8,128)}, u32[]{:S(2)}, u32[]{:S(2)}) %collective-permute-start.10) | collective-permute-done | bytes 786464 | tf_op jit(solution)/shard_map/ppermute | solution.py:29
  195.2 10.0 %fusion.100 = (f32[768]{0:T(1024)}, f32[768,1024]{0,1:T(8,128)S(1)}) fusion(f32[1024,768]{1,0:T(8,128)S(1)} %copy-done.56, f32[768]{0:T(1024)S(1)} %copy-done.53, f32[768,768]{1,0:T(8,128)S(1)} %copy-done, f32[768,1024]{1,0:T(8,128)S(1)} %constant_dynamic-update-slice_fusion, f32[1024]{0:T(1024)S(1)} %fusion.63), kind=kOutput, calls=%fused_computation.206 | convolution fusion | flops 3641179392 | bytes 11806720 | tf_op jit(solution)/shard_map/dot_general | solution.py:11
  205.2 3.9 fusion.101
  209.3 3.4 collective-permute-done.14
  214.8 34.7 %collective-permute-done.15 = f32[2,192,1024]{2,1,0:T(8,128)S(1)} collective-permute-done((f32[2,192,1024]{2,1,0:T(8,128)S(1)}, f32[2,192,1024]{2,1,0:T(8,128)S(1)}, u32[]{:S(2)}, u32[]{:S(2)}) %collective-permute-start.15) | collective-permute-done | bytes 1572896 | tf_op jit(solution)/shard_map/ppermute | solution.py:29
  251.1 8.4 %fusion.15 = f32[768,768]{1,0:T(8,128)} fusion(f32[768,1024]{0,1:T(8,128)} %copy-done.31, f32[768,1024]{1,0:T(8,128)} %copy-done.24, f32[768]{0:T(1024)S(1)} %get-tuple-element.20, f32[768]{0:T(1024)S(1)} %get-tuple-element.18), kind=kOutput, calls=%fused_computation.33 | convolution fusion | flops 3625451520 | bytes 8656896 | tf_op jit(solution)/shard_map/dot_general | solution.py:17
  259.5 9.9 %fusion.9 = f32[768,768]{1,0:T(8,128)} fusion(f32[768,1024]{1,0:T(8,128)S(1)} %copy-done.16, f32[1024]{0:T(1024)S(1)} %fusion.63, f32[1024,768]{1,0:T(8,128)S(1)} %copy-done.57, f32[768]{0:T(1024)S(1)} %copy-done.53), kind=kOutput, calls=%fused_computation.27 | convolution fusion | flops 3631742976 | bytes 8657920 | tf_op jit(solution)/shard_map/dot_general | solution.py:17
  278.1 4.5 fusion.102
  282.6 3.4 fusion.91
  291.2 4.4 fusion.13
  295.6 7.2 %multiply_reduce_fusion.5 = (f32[1024]{0:T(1024)S(1)}, f32[1024]{0:T(1024)S(1)}, f32[768,1024]{1,0:T(8,128)S(1)}) fusion(f32[768]{0:T(1024)S(1)} %get-tuple-element.19, f32[768,1024]{1,0:T(8,128)} %copy-done.7, f32[192,1024]{1,0:T(8,128)S(1)} %get-tuple-element.38, f32[192,1024]{1,0:T(8,128)} %copy-done.40, f32[192,1024]{1,0:T(8,128)} %copy-done.54, ...), kind=kOutput, calls=%fused_computation.26 | convolution fusion | flops 2723117056 | bytes 10431488 | tf_op jit(solution)/shard_map/dot_general | solution.py:23
  335.4 14.7 %collective-permute-done.20 = f32[8,1024]{1,0:T(8,128)S(1)} collective-permute-done((f32[8,1024]{1,0:T(8,128)S(1)}, f32[8,1024]{1,0:T(8,128)S(1)}, u32[]{:S(2)}, u32[]{:S(2)}) %collective-permute-start.20) | collective-permute-done | bytes 32800 | tf_op jit(solution)/shard_map/ppermute | solution.py:29
  354.2 39.3 %psum.42 = f32[2304]{0:T(1024)S(1)} all-reduce(f32[2304]{0:T(1024)S(1)} %concatenate.38), channel_id=1, replica_groups=mesh['dp'=8,'mp'=4] {'dp'}, use_global_device_ids=true, to_apply=%region_21.22 | all-reduce | flops 2304 | bytes 18432 | tf_op jit(solution)/shard_map/psum | solution.py:257
  394.8 138.9 %all-reduce.14.cloned.1.call-done = (f32[576,768]{1,0:T(8,128)}, f32[192,768]{1,0:T(8,128)}, f32[768,768]{1,0:T(8,128)}, f32[768,768]{1,0:T(8,128)}) async-done(((f32[576,768]{1,0:T(8,128)}, f32[192,768]{1,0:T(8,128)}, f32[768,768]{1,0:T(8,128)}, f32[768,768]{1,0:T(8,128)}), (f32[576,768]{1,0:T(8,128)}, f32[192,768]{1,0:T(8,128)}, f32[768,768]{1,0:T(8,128)}, ...) | async-done | bytes 7077904 | tf_op jit(solution)/shard_map/psum | solution.py:257
  536.4 132.7 %all-reduce.12.cloned.1.call-done = f32[1024,256]{1,0:T(8,128)} async-done(((f32[1024,256]{1,0:T(8,128)}), f32[1024,256]{1,0:T(8,128)}) %all-reduce.12.cloned.1.call-update) | async-done | bytes 1048592 | tf_op jit(solution)/shard_map/psum | solution.py:258
  672.2 3.4 copy.101
  (264 shorter events, 140.3 us)
Async XLA Ops:
  7.2 526.5 %all-reduce.14.cloned.1.call-start = ((), (), s32[]{:S(2)}) async-start(), calls=%async_computation.1 | async-start | bytes 14155776 | tf_op jit(solution)/shard_map/psum | solution.py:257
  11.7 23.0 %collective-permute-start.1 = (f32[192,1152]{1,0:T(8,128)}, f32[192,1152]{1,0:T(8,128)}, u32[]{:S(2)}, u32[]{:S(2)}) collective-permute-start(f32[192,1152]{1,0:T(8,128)} %get-tuple-element.70), channel_id=1, source_target_pairs={{0,2},{1,3},{2,0},{3,1},{4,6},{5,7},{6,4},{7,5},{8,10},{9,11},{10,... | collective-permute-start | bytes 2654216 | tf_op jit(solution)/shard_map/ppermute | solution.py:29
  14.7 45.9 %collective-permute-start = (f32[192,1152]{1,0:T(8,128)}, f32[192,1152]{1,0:T(8,128)}, u32[]{:S(2)}, u32[]{:S(2)}) collective-permute-start(f32[192,1152]{1,0:T(8,128)} %get-tuple-element.70), channel_id=1, source_target_pairs={{0,1},{1,0},{2,3},{3,2},{4,5},{5,4},{6,7},{7,6},{8,9},{9,8},{10,11... | collective-permute-start | bytes 2654216 | tf_op jit(solution)/shard_map/ppermute | solution.py:29
  34.7 30.9 %collective-permute-start.2 = (f32[192,1152]{1,0:T(8,128)}, f32[192,1152]{1,0:T(8,128)}, u32[]{:S(2)}, u32[]{:S(2)}) collective-permute-start(f32[192,1152]{1,0:T(8,128)} %collective-permute-done.1), channel_id=1, source_target_pairs={{0,1},{1,0},{2,3},{3,2},{4,5},{5,4},{6,7},{7,6},{8,9},{9,8},{10,11... | collective-permute-start | bytes 2654216 | tf_op jit(solution)/shard_map/ppermute | solution.py:29
  85.2 33.6 %collective-permute-start.7 = (f32[192,1024]{1,0:T(8,128)}, f32[192,1024]{1,0:T(8,128)}, u32[]{:S(2)}, u32[]{:S(2)}) collective-permute-start(f32[192,1024]{1,0:T(8,128)} %get-tuple-element.51), channel_id=1, source_target_pairs={{0,2},{1,3},{2,0},{3,1},{4,6},{5,7},{6,4},{7,5},{8,10},{9,11},{10,... | collective-permute-start | bytes 2359304 | tf_op jit(solution)/shard_map/ppermute | solution.py:29
  87.0 31.2 %collective-permute-start.4 = (f32[192,768]{1,0:T(8,128)}, f32[192,768]{1,0:T(8,128)}, u32[]{:S(2)}, u32[]{:S(2)}) collective-permute-start(f32[192,768]{1,0:T(8,128)} %param.29), channel_id=1, source_target_pairs={{0,2},{1,3},{2,0},{3,1},{4,6},{5,7},{6,4},{7,5},{8,10},{9,11},{10,... | collective-permute-start | bytes 1769480 | tf_op jit(solution)/shard_map/ppermute | solution.py:29
  87.3 33.9 %collective-permute-start.3 = (f32[192,768]{1,0:T(8,128)}, f32[192,768]{1,0:T(8,128)}, u32[]{:S(2)}, u32[]{:S(2)}) collective-permute-start(f32[192,768]{1,0:T(8,128)} %param.29), channel_id=1, source_target_pairs={{0,1},{1,0},{2,3},{3,2},{4,5},{5,4},{6,7},{7,6},{8,9},{9,8},{10,11... | collective-permute-start | bytes 1769480 | tf_op jit(solution)/shard_map/ppermute | solution.py:29
  87.3 37.3 %collective-permute-start.6 = (f32[192,1024]{1,0:T(8,128)}, f32[192,1024]{1,0:T(8,128)}, u32[]{:S(2)}, u32[]{:S(2)}) collective-permute-start(f32[192,1024]{1,0:T(8,128)} %get-tuple-element.51), channel_id=1, source_target_pairs={{0,1},{1,0},{2,3},{3,2},{4,5},{5,4},{6,7},{7,6},{8,9},{9,8},{10,11... | collective-permute-start | bytes 2359304 | tf_op jit(solution)/shard_map/ppermute | solution.py:29
  118.1 5.2 collective-permute-start.5
  118.8 8.2 %collective-permute-start.8 = (f32[192,1024]{1,0:T(8,128)}, f32[192,1024]{1,0:T(8,128)}, u32[]{:S(2)}, u32[]{:S(2)}) collective-permute-start(f32[192,1024]{1,0:T(8,128)} %collective-permute-done.7), channel_id=1, source_target_pairs={{0,1},{1,0},{2,3},{3,2},{4,5},{5,4},{6,7},{7,6},{8,9},{9,8},{10,11... | collective-permute-start | bytes 2359304 | tf_op jit(solution)/shard_map/ppermute | solution.py:29
  150.5 3.8 collective-permute-start.9
  150.5 20.7 %collective-permute-start.12 = (f32[192,1024]{1,0:T(8,128)}, f32[192,1024]{1,0:T(8,128)}, u32[]{:S(2)}, u32[]{:S(2)}) collective-permute-start(f32[192,1024]{1,0:T(8,128)} %bitcast.27), channel_id=1, source_target_pairs={{0,2},{1,3},{2,0},{3,1},{4,6},{5,7},{6,4},{7,5},{8,10},{9,11},{10,... | collective-permute-start | bytes 2359304 | tf_op jit(solution)/shard_map/ppermute | solution.py:29
  158.5 29.2 %collective-permute-start.10 = (f32[192,1024]{1,0:T(8,128)}, f32[192,1024]{1,0:T(8,128)}, u32[]{:S(2)}, u32[]{:S(2)}) collective-permute-start(f32[192,1024]{1,0:T(8,128)} %dynamic-slice_bitcast_fusion.4), channel_id=1, source_target_pairs={{0,2},{1,3},{2,0},{3,1},{4,6},{5,7},{6,4},{7,5},{8,10},{9,11},{10,... | collective-permute-start | bytes 2359304 | tf_op jit(solution)/shard_map/ppermute | solution.py:29
  160.2 31.2 %collective-permute-start.11 = (f32[192,1024]{1,0:T(8,128)}, f32[192,1024]{1,0:T(8,128)}, u32[]{:S(2)}, u32[]{:S(2)}) collective-permute-start(f32[192,1024]{1,0:T(8,128)} %bitcast.27), channel_id=1, source_target_pairs={{0,1},{1,0},{2,3},{3,2},{4,5},{5,4},{6,7},{7,6},{8,9},{9,8},{10,11... | collective-permute-start | bytes 2359304 | tf_op jit(solution)/shard_map/ppermute | solution.py:29
  171.2 22.8 %collective-permute-start.13 = (f32[192,1024]{1,0:T(8,128)}, f32[192,1024]{1,0:T(8,128)}, u32[]{:S(2)}, u32[]{:S(2)}) collective-permute-start(f32[192,1024]{1,0:T(8,128)} %collective-permute-done.12), channel_id=1, source_target_pairs={{0,1},{1,0},{2,3},{3,2},{4,5},{5,4},{6,7},{7,6},{8,9},{9,8},{10,11... | collective-permute-start | bytes 2359304 | tf_op jit(solution)/shard_map/ppermute | solution.py:29
  209.3 3.5 collective-permute-start.14
  213.0 36.5 %collective-permute-start.15 = (f32[2,192,1024]{2,1,0:T(8,128)S(1)}, f32[2,192,1024]{2,1,0:T(8,128)S(1)}, u32[]{:S(2)}, u32[]{:S(2)}) collective-permute-start(f32[2,192,1024]{2,1,0:T(8,128)S(1)} %bitcast_add_fusion.2), channel_id=1, source_target_pairs={{0,2},{1,3},{2,0},{3,1},{4,6},{5,7},{6,4},{7,5},{8,10},{9,11},{10,... | collective-permute-start | bytes 4718600 | tf_op jit(solution)/shard_map/ppermute | solution.py:29
  251.0 18.4 %collective-permute-start.16 = (f32[2,192,1024]{2,1,0:T(8,128)}, f32[2,192,1024]{2,1,0:T(8,128)}, u32[]{:S(2)}, u32[]{:S(2)}) collective-permute-start(f32[2,192,1024]{2,1,0:T(8,128)} %add.320), channel_id=1, source_target_pairs={{0,1},{1,0},{2,3},{3,2},{4,5},{5,4},{6,7},{7,6},{8,9},{9,8},{10,11... | collective-permute-start | bytes 4718600 | tf_op jit(solution)/shard_map/ppermute | solution.py:29
  295.6 373.6 %all-reduce.12.cloned.1.call-start = ((), (), s32[]{:S(2)}) async-start(), calls=%async_computation | async-start | bytes 2097152 | tf_op jit(solution)/shard_map/psum | solution.py:258
  304.2 20.7 %collective-permute-start.17 = (f32[2,192,1024]{2,1,0:T(8,128)}, f32[2,192,1024]{2,1,0:T(8,128)}, u32[]{:S(2)}, u32[]{:S(2)}) collective-permute-start(f32[2,192,1024]{2,1,0:T(8,128)} %dynamic-slice_bitcast_fusion), channel_id=1, source_target_pairs={{0,1},{1,0},{2,3},{3,2},{4,5},{5,4},{6,7},{7,6},{8,9},{9,8},{10,11... | collective-permute-start | bytes 4718600 | tf_op jit(solution)/shard_map/ppermute | solution.py:29
  324.6 7.6 %collective-permute-start.19 = (f32[8,1024]{1,0:T(8,128)S(1)}, f32[8,1024]{1,0:T(8,128)S(1)}, u32[]{:S(2)}, u32[]{:S(2)}) collective-permute-start(f32[8,1024]{1,0:T(8,128)S(1)} %select_maximum_fusion.1), channel_id=1, source_target_pairs={{0,1},{1,0},{2,3},{3,2},{4,5},{5,4},{6,7},{7,6},{8,9},{9,8},{10,11... | collective-permute-start | bytes 98312 | tf_op jit(solution)/shard_map/ppermute | solution.py:29
  329.3 20.9 %collective-permute-start.18 = (f32[192,1024]{1,0:T(8,128)}, f32[192,1024]{1,0:T(8,128)}, u32[]{:S(2)}, u32[]{:S(2)}) collective-permute-start(f32[192,1024]{1,0:T(8,128)} %dynamic-slice_bitcast_fusion.3), channel_id=1, source_target_pairs={{0,2},{1,3},{2,0},{3,1},{4,6},{5,7},{6,4},{7,5},{8,10},{9,11},{10,... | collective-permute-start | bytes 2359304 | tf_op jit(solution)/shard_map/ppermute | solution.py:29
  332.3 17.8 %collective-permute-start.20 = (f32[8,1024]{1,0:T(8,128)S(1)}, f32[8,1024]{1,0:T(8,128)S(1)}, u32[]{:S(2)}, u32[]{:S(2)}) collective-permute-start(f32[8,1024]{1,0:T(8,128)S(1)} %fusion.64), channel_id=1, source_target_pairs={{0,2},{1,3},{2,0},{3,1},{4,6},{5,7},{6,4},{7,5},{8,10},{9,11},{10,... | collective-permute-start | bytes 98312 | tf_op jit(solution)/shard_map/ppermute | solution.py:29
  533.7 137.7 %copy-start.41 = (f32[192,768]{1,0:T(8,128)S(1)}, f32[192,768]{1,0:T(8,128)}, u32[]{:S(2)}) copy-start(f32[192,768]{1,0:T(8,128)} %get-tuple-element.108) | copy-start | bytes 1769476
  (57 other events, 432.9 us)
Sparse Core Ops, SparseCore 0:
  295.7 237.9 all-reduce.13
  540.3 128.8 all-reduce.11

commit v2 on v1

v2 whole, which is shorter than its diff:
```python
import math
from functools import partial

import jax
import jax.numpy as jnp
from jax import lax
from jax.experimental import pallas as pl
from jax.experimental.pallas import tpu as pltpu
from jax.sharding import PartitionSpec as P

EPSILON = 1e-05
TB = 256
WIDE = 512
NN = (((1,), (0,)), ((), ()))
NT = (((1,), (1,)), ((), ()))
F32 = jnp.float32
BF16 = jnp.bfloat16


def split(wide):
    high = wide.astype(BF16)
    return high, (wide - high.astype(F32)).astype(BF16)


def dot3(left, right, dims):
    def one(a, b):
        return lax.dot_general(a, b, dims, preferred_element_type=F32)

    return one(left[0], right[0]) + (one(left[0], right[1]) + one(left[1], right[0]))


def put(high_ref, low_ref, wide):
    high, low = split(wide)
    high_ref[...] = high
    low_ref[...] = low


def get(high_ref, low_ref):
    return high_ref[...], low_ref[...]


def reverse_lanes(wide):
    size = wide.shape[1]
    row = lax.broadcasted_iota(jnp.int32, (size, size), 0)
    col = lax.broadcasted_iota(jnp.int32, (size, size), 1)
    turn = (row + col == size - 1).astype(F32).astype(BF16)
    high, rest = split(wide)
    middle = wide - high.astype(F32)
    low = (middle - rest.astype(F32)).astype(BF16)

    def one(part):
        return lax.dot_general(part, turn, NN, preferred_element_type=F32)

    return one(high) + (one(rest) + one(low))


def live_row(length, start, width):
    return (lax.broadcasted_iota(jnp.int32, (1, width), 1) + start < length).astype(F32)


def whole(shape):
    return pl.BlockSpec(shape, lambda i: (0,) * len(shape))


def across(rows, width=WIDE):
    return pl.BlockSpec((rows, width), lambda i: (0, i))


SCALARS = pl.BlockSpec(memory_space=pltpu.SMEM)


def shaped(shape, dtype=F32):
    return jax.ShapeDtypeStruct(shape, dtype)


def call(kernel, grid, ins, outs, scratch=(), name=None, flops=0):
    held = sum(2 * math.prod(spec.block_shape) * array.dtype.itemsize for array, spec in ins if spec.block_shape)
    held += sum(2 * math.prod(spec.block_shape) * shape.dtype.itemsize for shape, spec in outs)
    held += sum(math.prod(ref.shape) * jnp.dtype(ref.dtype).itemsize for ref in scratch)
    moved = sum(array.size * array.dtype.itemsize for array, _ in ins)
    moved += sum(math.prod(shape.shape) * shape.dtype.itemsize for shape, _ in outs)
    run = pl.pallas_call(
        kernel,
        grid=(grid,),
        in_specs=[spec for _, spec in ins],
        out_specs=[spec for _, spec in outs],
        out_shape=[shape for shape, _ in outs],
        scratch_shapes=list(scratch),
        compiler_params=pltpu.CompilerParams(
            dimension_semantics=("arbitrary",), vmem_limit_bytes=min(held + 16 * 2**20, 58 * 2**20)
        ),
        cost_estimate=pl.CostEstimate(flops=int(flops), transcendentals=0, bytes_accessed=moved),
        name=name,
    )
    return run(*[array for array, _ in ins])


def place_rows(target, place, parts):
    for flip, part in enumerate(parts):
        rows = part.shape[0]
        target[pl.ds(pl.multiple_of((place ^ flip) * rows, rows), rows), :] = part[...]


def take_rows(source, index, rows):
    return source[pl.ds(pl.multiple_of(index * rows, rows), rows), :]


def fold(wide):
    total = wide[:, :128]
    for at in range(128, wide.shape[1], 128):
        total = total + wide[:, at : at + 128]
    return total


def band_kernel(bias, high, low):
    window = bias.shape[1]
    turned = reverse_lanes(jnp.exp(bias[...]))
    wide = jnp.concatenate([turned, jnp.zeros_like(turned)], axis=1)
    skewed = pltpu.roll(wide, 1, 1, stride=1, stride_axis=0)
    row = lax.broadcasted_iota(jnp.int32, wide.shape, 0)
    col = lax.broadcasted_iota(jnp.int32, wide.shape, 1)
    band = skewed + (col <= row).astype(F32)
    first = (pl.program_id(0) == 0) & (col < window)
    put(high, low, jnp.where(first, 0.0, band))


def qkv_weights_kernel(w_q, w_k, w_v, high, low, high_t, low_t):
    stacked = jnp.concatenate([w_q[...], w_k[...], w_v[...]], axis=0)
    put(high, low, stacked)
    put(high_t, low_t, stacked.T)


def weights_kernel(w, high, low, high_t, low_t):
    put(high, low, w[...])
    put(high_t, low_t, w[...].T)


def out_weights_kernel(own, near, far, far_near, high_own, low_own, high_t, low_t):
    put(high_own, low_own, own[...])
    stacked = jnp.concatenate([own[...], near[...], far[...], far_near[...]], axis=0)
    put(high_t, low_t, stacked.T)


def column_stats(values_in):
    mean = jnp.mean(values_in, axis=0, keepdims=True)
    var = jnp.mean(values_in * values_in, axis=0, keepdims=True) - mean * mean
    return mean, lax.rsqrt(var + EPSILON)


def attend_kernel(
    info, x0, x1, x2, x3, cols, w_hi, w_lo, band_hi, band_lo, biases,
    mixed, quotient, f_query, f_numer, pair_hi, pair_lo, n_hi, n_lo, stats,
    x_all, far, last_hi, last_lo,
):
    step = pl.program_id(0)
    chans = x0.shape[0]
    window = TB
    place_rows(x_all, info[0], (x0, x1, x2, x3))
    x = x_all[...]
    mean, scale = column_stats(x)
    stats[0:1, :] = mean
    stats[1:2, :] = scale
    normed = split((x - mean) * scale * cols[:, 0:1] + cols[:, 1:2])
    n_hi[...], n_lo[...] = normed
    projected = dot3(get(w_hi, w_lo), normed, NN)
    exp_keys = jnp.exp(projected[chans : 2 * chans])
    carried = exp_keys * (projected[2 * chans :] + biases[:, 1:2])
    pair = split(jnp.concatenate([carried, exp_keys], axis=0))
    pair_hi[...], pair_lo[...] = pair

    @pl.when(step == 0)
    def _():
        far[...] = jnp.zeros_like(far)
        last_hi[...] = jnp.zeros_like(last_hi)
        last_lo[...] = jnp.zeros_like(last_lo)

    last = get(last_hi, last_lo)
    total = far[:, 0:1]
    gates = jax.nn.sigmoid(projected[:chans] + biases[:, 0:1])
    for at in range(0, x.shape[1], window):
        here = slice(at, at + window)
        near = (band_hi[here, :], band_lo[here, :])
        block = (pair[0][:, here], pair[1][:, here])
        sums = dot3(block, (near[0][:, window:], near[1][:, window:]), NT)
        sums = sums + dot3(last, (near[0][:, :window], near[1][:, :window]), NT)
        sums = sums + total
        total = total + jnp.sum(last[0].astype(F32) + last[1].astype(F32), axis=1, keepdims=True)
        last = block
        inverse = 1.0 / sums[chans:]
        ratio = sums[:chans] * inverse
        gate = gates[:, here]
        quotient[:, here] = ratio
        mixed[:, here] = gate * ratio
        f_query[:, here] = ratio * gate * (1.0 - gate)
        f_numer[:, here] = gate * inverse
    far[...] = jnp.broadcast_to(total, far.shape)
    last_hi[...], last_lo[...] = last


def cotangent_kernel(info, c0, c1, c2, c3, hi, lo, own_sum, c_all):
    step = pl.program_id(0)
    place_rows(c_all, info[0], (c0, c1, c2, c3))
    live = live_row(info[1], step * WIDE, WIDE)
    put(hi, lo, c_all[...] * live)

    @pl.when(step == 0)
    def _():
        own_sum[...] = jnp.zeros_like(own_sum)

    own_sum[...] += fold(c0[...] * live)


def hidden_kernel(
    info, m0, m1, m2, m3, x0, x1, x2, x3, cols, wo_hi, wo_lo, wu_hi, wu_lo, up_bias,
    act_hi, act_lo, slope, normal, n_hi, n_lo, inner_own, stats,
    x_all,
):
    step = pl.program_id(0)
    place_rows(x_all, info[0], (x0, x1, x2, x3))
    live = live_row(info[1], step * WIDE, WIDE)
    parts = jnp.concatenate([m0[...], m1[...], m2[...], m3[...]], axis=0)
    out = dot3(get(wo_hi, wo_lo), split(parts), NN)
    inner = x_all[...] + live * (out + cols[:, 2:3])
    x_all[...] = inner
    inner_own[...] = take_rows(x_all, info[0], x0.shape[0])
    mean, scale = column_stats(inner)
    stats[0:1, :] = scale
    unit = (inner - mean) * scale
    normal[...] = unit
    normed = split(unit * cols[:, 3:4] + cols[:, 4:5])
    n_hi[...], n_lo[...] = normed
    pre = dot3(get(wu_hi, wu_lo), normed, NN) + up_bias[...]
    root = 0.7978845608028654
    cubic = 0.044715
    square = pre * pre
    bent = jnp.tanh(root * pre * (1.0 + cubic * square))
    put(act_hi, act_lo, 0.5 * pre * (1.0 + bent))
    slope[...] = 0.5 * (1.0 + bent) + 0.5 * pre * (1.0 - bent * bent) * (
        root * (1.0 + 3.0 * cubic * square)
    )


def outer_kernel(a_hi, a_lo, b_hi, b_lo, grad):
    grad[...] = dot3(get(a_hi, a_lo), get(b_hi, b_lo), NT)


def part_halves(grid, place, keep, send):
    rows = grid.shape[0] // 4
    core = place & 1
    for far in range(2):
        here = slice(far * rows, (far + 1) * rows)
        keep[here, :] = take_rows(grid, 2 * far + core, rows)
        send[here, :] = take_rows(grid, 2 * far + 1 - core, rows)


def hidden_back_kernel(
    info, c_hi, c_lo, wd_hi, wd_lo, slope, wu_hi, wu_lo, d_hi, d_lo, keep, send, bias_sum, grid
):
    d_pre = dot3(get(wd_hi, wd_lo), get(c_hi, c_lo), NN) * slope[...]

    @pl.when(pl.program_id(0) == 0)
    def _():
        bias_sum[...] = jnp.zeros_like(bias_sum)

    bias_sum[...] += fold(d_pre)
    parts = split(d_pre)
    d_hi[...], d_lo[...] = parts
    grid[...] = dot3(get(wu_hi, wu_lo), parts, NN)
    part_halves(grid, info[0], keep, send)


def down_kernel(info, wd_hi, wd_lo, act_hi, act_lo, keep, send, grid):
    grid[...] = dot3(get(wd_hi, wd_lo), get(act_hi, act_lo), NN)
    part_halves(grid, info[0], keep, send)


def inner_back_kernel(
    info, half, other, normal, stats, cols, c0, c1, c2, c3, wo_hi, wo_lo, f_query, f_numer, quotient,
    b_hi, b_lo, dq_hi, dq_lo, dp_hi, dp_lo, inner_own, sum_gain, sum_bias, sum_out, sum_query,
    c_all, d_all,
):
    step = pl.program_id(0)
    place = info[0]
    core = place & 1
    chans = c0.shape[0]
    place_rows(c_all, place, (c0, c1, c2, c3))
    for far in range(2):
        here = slice(far * chans, (far + 1) * chans)
        d_all[pl.ds(pl.multiple_of((2 * far + core) * chans, chans), chans), :] = half[here, :]
        d_all[pl.ds(pl.multiple_of((2 * far + 1 - core) * chans, chans), chans), :] = other[here, :]
    live = live_row(info[1], step * WIDE, WIDE)
    scaled = d_all[...] * cols[:, 3:4]
    unit = normal[...]
    mean_one = jnp.mean(scaled, axis=0, keepdims=True)
    mean_two = jnp.mean(scaled * unit, axis=0, keepdims=True)
    d_inner = c_all[...] + stats[0:1, :] * (scaled - mean_one - unit * mean_two)
    c_all[...] = d_inner
    own = take_rows(c_all, place, chans)
    inner_own[...] = own
    d_own = take_rows(d_all, place, chans)

    @pl.when(step == 0)
    def _():
        for total in (sum_gain, sum_bias, sum_out, sum_query):
            total[...] = jnp.zeros_like(total)

    sum_gain[...] += fold(d_own * take_rows(normal, place, chans))
    sum_bias[...] += fold(d_own)
    sum_out[...] += fold(own * live)
    branch = split(d_inner * live)
    b_hi[...], b_lo[...] = branch
    d_mixed = dot3(get(wo_hi, wo_lo), branch, NN)
    d_query = d_mixed * f_query[...]
    sum_query[...] += fold(d_query)
    put(dq_hi, dq_lo, d_query)
    d_numer = d_mixed * f_numer[...]
    put(dp_hi, dp_lo, jnp.concatenate([d_numer, -d_numer * quotient[...]], axis=0))


def outer_two_kernel(a, b_hi, b_lo, c_hi, c_lo, d_hi, d_lo, grad):
    rows = a.shape[0]
    grad[:rows, :] = dot3(split(a[...]), get(b_hi, b_lo), NT)
    grad[rows:, :] = dot3(get(c_hi, c_lo), get(d_hi, d_lo), NT)


def mix_back_kernel(
    d_hi, d_lo, before_hi, before_lo, here_hi, here_lo, band_hi, band_lo, bias,
    kv_hi, kv_lo, d_bias, sum_value,
    carry, later, ahead,
):
    step = pl.program_id(0)
    block = pl.num_programs(0) - 1 - step
    window = TB
    chans = d_hi.shape[0] // 2

    @pl.when(step == 0)
    def _():
        for total in (carry, later, ahead, sum_value):
            total[...] = jnp.zeros_like(total)

    d_pair = get(d_hi, d_lo)
    d_wide = d_pair[0].astype(F32) + d_pair[1].astype(F32)
    into = dot3(d_pair, get(band_hi, band_lo), NN)
    back = into[:, window:] + carry[...] + later[:, 0:1]
    carry[...] = into[:, :window]
    later[...] = later[...] + ahead[...]
    ahead[...] = jnp.broadcast_to(jnp.sum(d_wide, axis=1, keepdims=True), ahead.shape)
    turned = split(d_wide.T)
    right = dot3(turned, get(here_hi, here_lo), NN)
    left = dot3(turned, get(before_hi, before_lo), NN)
    left = jnp.where(block == 0, 0.0, left)
    wide = jnp.concatenate([reverse_lanes(right), reverse_lanes(left)], axis=1)
    placed = pltpu.roll(wide, window + 1, 1, stride=1, stride_axis=0)
    d_bias[...] = placed[:, :window] * jnp.exp(bias[...])
    pair = here_hi[...].astype(F32) + here_lo[...].astype(F32)
    d_value = pair[chans:] * back[:chans]
    d_key = pair[:chans] * back[:chans] + pair[chans:] * back[chans:]
    sum_value[...] += fold(d_value)
    put(kv_hi, kv_lo, jnp.concatenate([d_key, d_value], axis=0))


def project_back_kernel(
    info, dq_hi, dq_lo, kv_hi, kv_lo, w_hi, w_lo, x0, x1, x2, x3, stats, cols, keep, send, sums, x_all, grid
):
    place_rows(x_all, info[0], (x0, x1, x2, x3))
    d_all = (
        jnp.concatenate([dq_hi[...], kv_hi[...]], axis=0),
        jnp.concatenate([dq_lo[...], kv_lo[...]], axis=0),
    )
    terms = dot3(get(w_hi, w_lo), d_all, NN)
    grid[...] = terms
    part_halves(grid, info[0], keep, send)
    scaled = terms * cols[:, 0:1]
    unit = (x_all[...] - stats[0:1, :]) * stats[1:2, :]
    sums[...] = jnp.zeros_like(sums)
    sums[0:1, :] = jnp.sum(scaled, axis=0, keepdims=True)
    sums[1:2, :] = jnp.sum(scaled * unit, axis=0, keepdims=True)


def input_back_kernel(model, mine, come, inner_own, x_own, stats, sums, gain, d_in, sum_gain, sum_bias):
    d_normed = mine[...] + come[...]
    unit = (x_own[...] - stats[0:1, :]) * stats[1:2, :]

    @pl.when(pl.program_id(0) == 0)
    def _():
        for total in (sum_gain, sum_bias):
            total[...] = jnp.zeros_like(total)

    sum_gain[...] += fold(d_normed * unit)
    sum_bias[...] += fold(d_normed)
    d_in[...] = inner_own[...] + stats[1:2, :] * (
        d_normed * gain[...] - sums[0:1, :] / model - unit * (sums[1:2, :] / model)
    )


def swap(block, bit):
    return lax.ppermute(block, "mp", [(i, i ^ bit) for i in range(4)])


def gather_parts(own):
    far = swap(own, 2)
    near = swap(own, 1)
    return own, near, far, swap(far, 1)


def in_order(parts, place):
    stacked = jnp.stack(parts)
    return jnp.concatenate(
        [lax.dynamic_index_in_dim(stacked, place ^ i, 0, keepdims=False) for i in range(4)], axis=0
    )


def after(value, *earlier):
    return lax.optimization_barrier((value, earlier))[0]


def cut(grid, bit):
    rows = grid.shape[0] // 2
    mine = lax.dynamic_slice_in_dim(grid, bit * rows, rows, 0)
    other = lax.dynamic_slice_in_dim(grid, (1 - bit) * rows, rows, 0)
    return mine, other


def join(mine, other, bit):
    low = jnp.where(bit == 0, mine, other)
    high = jnp.where(bit == 0, other, mine)
    return jnp.concatenate([low, high], axis=0)


def trade(block, flip):
    size = lax.axis_size("dp")
    return lax.ppermute(block, "dp", [(i, i ^ flip) for i in range(size)])


def dp_bit(flip):
    return (lax.axis_index("dp") // flip) % 2


def dp_chains(grids, orders):
    first = [cut(g, dp_bit(o[0])) for g, o in zip(grids, orders)]
    come = [trade(send, o[0]) for (_, send), o in zip(first, orders)]
    held = [mine + c for (mine, _), c in zip(first, come)]
    second = [cut(h, dp_bit(o[1])) for h, o in zip(held, orders)]
    come = [trade(send, o[1]) for (_, send), o in zip(second, orders)]
    held = [mine + c for (mine, _), c in zip(second, come)]
    come = [trade(h, o[2]) for h, o in zip(held, orders)]
    held = [h + c for h, c in zip(held, come)]
    come = [trade(h, o[1]) for h, o in zip(held, orders)]
    held = [join(h, c, dp_bit(o[1])) for h, c, o in zip(held, come, orders)]
    come = [trade(h, o[0]) for h, o in zip(held, orders)]
    return [join(h, c, dp_bit(o[0])) for h, c, o in zip(held, come, orders)]


def dp_sum(grid):
    if lax.axis_size("dp") != 8:
        return lax.psum(grid, "dp")
    rows = grid.shape[0] // 2
    parts = dp_chains([grid[:rows], grid[rows:]], [(1, 2, 4), (2, 1, 4)])
    return jnp.concatenate(parts, axis=0)


def pair_sum(grid, place):
    core, far = place % 2, place // 2
    mine, send = cut(grid, core)
    mine, send = cut(mine + swap(send, 1), far)
    quarter = dp_sum(mine + swap(send, 2))
    half = join(quarter, swap(quarter, 2), far)
    return join(half, swap(half, 1), core)


def dp_sum_small(grid):
    if lax.axis_size("dp") != 8:
        return lax.psum(grid, "dp")
    for flip in (1, 2, 4):
        grid = grid + trade(grid, flip)
    return grid


def body(
    inputs,
    lengths,
    ln1_gain,
    ln1_bias,
    w_query,
    w_key,
    w_value,
    query_bias,
    value_bias,
    pair_bias,
    w_out,
    out_bias,
    ln2_gain,
    ln2_bias,
    w_up,
    up_bias,
    w_down,
    down_bias,
    cotangent,
):
    seq_rows, span, chans = inputs.shape
    window = pair_bias.shape[1]
    model = 4 * chans
    units = w_up.shape[1]
    steps = span // WIDE
    blocks = span // TB
    assert seq_rows == 1 and window == TB
    place = lax.axis_index("mp")
    info = jnp.stack([place.astype(jnp.int32), lengths[0]])

    unit = 6 * model * model * span

    x_own = inputs[0].T
    x_far = swap(x_own, 2)
    x_near = swap(x_own, 1)
    vectors = jnp.stack([ln1_gain, ln1_bias, out_bias, ln2_gain, ln2_bias])
    vectors = jnp.pad(vectors, ((0, 3), (0, 0)))
    cols = in_order([v.T for v in gather_parts(vectors)], place)

    band = call(
        band_kernel, blocks,
        [(pair_bias, pl.BlockSpec((TB, window), lambda i: (i, 0)))],
        [(shaped((span, 2 * window), BF16), pl.BlockSpec((TB, 2 * window), lambda i: (i, 0)))] * 2,
        name="band",
    )
    wide_qkv = (shaped((3 * chans, model), BF16), whole((3 * chans, model)))
    tall_qkv = (shaped((model, 3 * chans), BF16), whole((model, 3 * chans)))
    wq_hi, wq_lo, wqt_hi, wqt_lo = call(
        qkv_weights_kernel, 1,
        [(w.T, whole((chans, model))) for w in (w_query, w_key, w_value)],
        [wide_qkv, wide_qkv, tall_qkv, tall_qkv],
        name="qkv_weights",
    )
    up_out = (shaped((model, units), BF16), whole((model, units)))
    up_t_out = (shaped((units, model), BF16), whole((units, model)))
    wu_hi, wu_lo, wut_hi, wut_lo = call(
        weights_kernel, 1, [(w_up, whole((model, units)))], [up_out, up_out, up_t_out, up_t_out], name="up_weights"
    )
    wd_hi, wd_lo, wdt_hi, wdt_lo = call(
        weights_kernel, 1, [(w_down, whole((units, model)))], [up_t_out, up_t_out, up_out, up_out], name="down_weights"
    )

    x_far = after(x_far, band, wq_hi, wqt_hi, wu_hi, wut_hi, wd_hi, wdt_hi, cols)
    x_parts = (x_own, x_near, x_far, swap(x_far, 1))
    wo_own = after(w_out, x_far)
    wo_far = swap(wo_own, 2)
    wo_near = swap(w_out, 1)

    thin = (shaped((chans, span)), across(chans))
    tall = (shaped((model, span)), across(model))
    tall_half = (shaped((model, span), BF16), across(model))
    hid_half = (shaped((units, span), BF16), across(units))
    pair_half = (shaped((2 * chans, span), BF16), across(2 * chans))
    thin_half = (shaped((chans, span), BF16), across(chans))
    rows8 = (shaped((8, span)), across(8))
    x_ins = [(x, across(chans)) for x in x_parts]
    scalars = (info, SCALARS)
    cols_in = (cols, whole((model, 8)))

    mixed, quotient, f_query, f_numer, pair_hi, pair_lo, n1_hi, n1_lo, stats_one = call(
        attend_kernel, steps,
        [scalars, *x_ins, cols_in, (wq_hi, whole((3 * chans, model))), (wq_lo, whole((3 * chans, model)))]
        + [(b, pl.BlockSpec((WIDE, 2 * window), lambda i: (i, 0))) for b in band]
        + [(jnp.stack([query_bias, value_bias], axis=1), whole((chans, 2)))],
        [thin, thin, thin, thin, pair_half, pair_half, tall_half, tall_half, rows8],
        [
            pltpu.VMEM((model, WIDE), F32),
            pltpu.VMEM((2 * chans, 128), F32),
            pltpu.VMEM((2 * chans, TB), BF16),
            pltpu.VMEM((2 * chans, TB), BF16),
        ],
        name="attend",
        flops=1.25 * unit,
    )

    mixed_far = swap(mixed, 2)
    mixed_near = swap(mixed, 1)
    wo_parts = (w_out, wo_near, wo_far, swap(wo_far, 1))
    wo_hi, wo_lo, wot_hi, wot_lo = call(
        out_weights_kernel, 1,
        [(w, whole((chans, model))) for w in wo_parts],
        [(shaped((chans, model), BF16), whole((chans, model)))] * 2
        + [(shaped((model, model), BF16), whole((model, model)))] * 2,
        name="out_weights",
    )
    mixed_far = after(mixed_far, wo_hi, wot_hi)
    mixed_parts = (mixed, mixed_near, mixed_far, swap(mixed_far, 1))
    cot_own = cotangent[0].T
    cot_far = swap(after(cot_own, mixed_far), 2)
    cot_near = swap(cot_own, 1)
    lanes_own = (shaped((chans, 128)), whole((chans, 128)))

    act_hi, act_lo, slope, normal_two, n2_hi, n2_lo, inner_own, stats_two = call(
        hidden_kernel, steps,
        [scalars, *[(p, across(chans)) for p in mixed_parts], *x_ins, cols_in]
        + [(wot_hi, whole((model, model))), (wot_lo, whole((model, model)))]
        + [(wut_hi, whole((units, model))), (wut_lo, whole((units, model))), (up_bias[:, None], whole((units, 1)))],
        [hid_half, hid_half, (shaped((units, span)), across(units)), tall, tall_half, tall_half, thin, rows8],
        [pltpu.VMEM((model, WIDE), F32)],
        name="hidden",
        flops=2 * unit,
    )

    cot_far = after(cot_far, act_hi)
    cot_parts = (cot_own, cot_near, cot_far, swap(cot_far, 1))
    cot_ins = [(c, across(chans)) for c in cot_parts]
    c_hi, c_lo, s_down = call(
        cotangent_kernel, steps, [scalars, *cot_ins], [tall_half, tall_half, lanes_own],
        [pltpu.VMEM((model, WIDE), F32)], name="cotangent",
    )

    def outer(a_hi, a_lo, b_hi, b_lo, name):
        rows, inner_len = a_hi.shape
        deep = b_hi.shape[0]
        slab = pl.BlockSpec((rows // 2, inner_len), lambda i: (i, 0))
        return call(
            outer_kernel, 2,
            [(a_hi, slab), (a_lo, slab), (b_hi, whole((deep, inner_len))), (b_lo, whole((deep, inner_len)))],
            [(shaped((rows, deep)), pl.BlockSpec((rows // 2, deep), lambda i: (i, 0)))],
            name=name,
            flops=unit,
        )[0]

    d_w_down = outer(act_hi, act_lo, c_hi, c_lo, "down_grad")
    c_hi, c_lo = after((c_hi, c_lo), d_w_down)
    g_down = dp_sum(d_w_down)
    half_out = (shaped((2 * chans, span)), across(2 * chans))
    dpre_hi, dpre_lo, keep, send, s_up = call(
        hidden_back_kernel, steps,
        [scalars, (c_hi, across(model)), (c_lo, across(model))]
        + [(wd_hi, whole((units, model))), (wd_lo, whole((units, model))), (slope, across(units))]
        + [(wu_hi, whole((model, units))), (wu_lo, whole((model, units)))],
        [hid_half, hid_half, half_out, half_out, (shaped((units, 128)), whole((units, 128)))],
        [pltpu.VMEM((model, WIDE), F32)],
        name="hidden_back",
        flops=2 * unit,
    )
    half = keep + swap(send, 1)
    half_far = swap(half, 2)
    d_w_up = outer(n2_hi, n2_lo, dpre_hi, dpre_lo, "up_grad")
    g_up = dp_sum(d_w_up)
    keep_down, send_down = call(
        down_kernel, steps,
        [scalars, (wdt_hi, whole((model, units))), (wdt_lo, whole((model, units))), (act_hi, across(units)), (act_lo, across(units))],
        [half_out, half_out],
        [pltpu.VMEM((model, WIDE), F32)],
        name="down",
        flops=unit,
    )
    half_far = after(half_far, d_w_up, keep_down)
    half = half + half_far
    other = swap(half, 1)

    far_bit = place // 2
    mine_down, send_down = cut(keep_down + swap(send_down, 1), far_bit)
    come_down = swap(after(send_down, half_far), 2)
    live = (jnp.arange(span, dtype=jnp.int32) < lengths[0]).astype(F32)[None, :]
    result = inner_own + live * (mine_down + come_down + down_bias[:, None])

    b_hi, b_lo, dq_hi, dq_lo, dp_hi, dp_lo, d_inner_own, s_gain2, s_bias2, s_out, s_query = call(
        inner_back_kernel, steps,
        [scalars, (half, across(2 * chans)), (other, across(2 * chans)), (normal_two, across(model)), (stats_two, across(8)), cols_in]
        + cot_ins
        + [(wo_hi, whole((chans, model))), (wo_lo, whole((chans, model)))]
        + [(f_query, across(chans)), (f_numer, across(chans)), (quotient, across(chans))],
        [tall_half, tall_half, thin_half, thin_half, pair_half, pair_half, thin, lanes_own, lanes_own, lanes_own, lanes_own],
        [pltpu.VMEM((model, WIDE), F32), pltpu.VMEM((model, WIDE), F32)],
        name="inner_back",
        flops=0.25 * unit,
    )
    thin_all, tall_all = whole((chans, span)), whole((model, span))
    def back_at(i):
        return blocks - 1 - i

    pair_spec = pl.BlockSpec((2 * chans, TB), lambda i: (0, back_at(i)))
    prev_spec = pl.BlockSpec((2 * chans, TB), lambda i: (0, jnp.maximum(back_at(i) - 1, 0)))
    band_spec = pl.BlockSpec((TB, 2 * window), lambda i: (back_at(i), 0))
    row_spec = pl.BlockSpec((TB, window), lambda i: (back_at(i), 0))
    kv_hi, kv_lo, d_pair, s_value = call(
        mix_back_kernel, blocks,
        [(dp_hi, pair_spec), (dp_lo, pair_spec), (pair_hi, prev_spec), (pair_lo, prev_spec), (pair_hi, pair_spec), (pair_lo, pair_spec)]
        + [(band[0], band_spec), (band[1], band_spec), (pair_bias, row_spec)],
        [(shaped((2 * chans, span), BF16), pair_spec)] * 2 + [(shaped((span, window)), row_spec), lanes_own],
        [pltpu.VMEM((2 * chans, TB), F32), pltpu.VMEM((2 * chans, 128), F32), pltpu.VMEM((2 * chans, 128), F32)],
        name="mix_back",
        flops=0.7 * unit,
    )
    grad_kv = call(
        outer_kernel, 1,
        [(kv_hi, whole((2 * chans, span))), (kv_lo, whole((2 * chans, span))), (n1_hi, tall_all), (n1_lo, tall_all)],
        [(shaped((2 * chans, model)), whole((2 * chans, model)))],
        name="key_value_grad",
        flops=0.5 * unit,
    )[0]
    grad_oq = call(
        outer_two_kernel, 1,
        [(mixed, thin_all), (b_hi, tall_all), (b_lo, tall_all)]
        + [(dq_hi, thin_all), (dq_lo, thin_all), (n1_hi, tall_all), (n1_lo, tall_all)],
        [(shaped((2 * chans, model)), whole((2 * chans, model)))],
        name="out_query_grad",
        flops=0.5 * unit,
    )[0]

    dq_hi, kv_hi = after((dq_hi, kv_hi), grad_oq, grad_kv)
    g_kv = dp_sum(jnp.concatenate([grad_oq, grad_kv], axis=0))
    grad_oq, grad_kv = g_kv[: 2 * chans], g_kv[2 * chans :]
    d_pair = pair_sum(d_pair, place)
    keep, send, sums = call(
        project_back_kernel, steps,
        [scalars, (dq_hi, across(chans)), (dq_lo, across(chans)), (kv_hi, across(2 * chans)), (kv_lo, across(2 * chans))]
        + [(wqt_hi, whole((model, 3 * chans))), (wqt_lo, whole((model, 3 * chans))), *x_ins, (stats_one, across(8)), cols_in],
        [half_out, half_out, rows8],
        [pltpu.VMEM((model, WIDE), F32), pltpu.VMEM((model, WIDE), F32)],
        name="project_back",
        flops=0.75 * unit,
    )
    sums = sums + swap(sums, 1)
    sums = sums + swap(sums, 2)
    mine, send = cut(keep + swap(send, 1), far_bit)
    d_inputs, s_gain1, s_bias1 = call(
        partial(input_back_kernel, float(model)), steps,
        [(mine, across(chans)), (swap(send, 2), across(chans)), (d_inner_own, across(chans)), (x_parts[0], across(chans))]
        + [(stats_one, across(8)), (sums, across(8)), (ln1_gain[:, None], whole((chans, 1)))],
        [thin, lanes_own, lanes_own],
        name="input_back",
    )

    small = jnp.concatenate(
        [
            jnp.sum(s, axis=1)
            for s in (s_gain1, s_bias1, s_query, s_value, s_out, s_gain2, s_bias2, s_down, s_up)
        ]
    )
    small = dp_sum_small(small)
    vecs = [small[i * chans : (i + 1) * chans] for i in range(8)]
    return (
        result.T[None],
        d_inputs.T[None],
        vecs[0],
        vecs[1],
        grad_oq[chans:].T,
        grad_kv[:chans].T,
        grad_kv[chans:].T,
        vecs[2],
        vecs[3],
        d_pair,
        grad_oq[:chans],
        vecs[4],
        vecs[5],
        vecs[6],
        g_up,
        small[8 * chans :],
        g_down,
        vecs[7],
    )


def solution(mesh):
    rows = P("dp", None, "mp")
    vec = P("mp")
    out_dim = P(None, "mp")
    in_dim = P("mp", None)
    return jax.shard_map(
        body,
        mesh=mesh,
        in_specs=(
            rows, P("dp"), vec, vec, out_dim, out_dim, out_dim, vec, vec, P(), in_dim, vec, vec, vec,
            out_dim, vec, in_dim, vec, rows,
        ),
        out_specs=(
            rows, rows, vec, vec, out_dim, out_dim, out_dim, vec, vec, P(), in_dim, vec, vec, vec,
            out_dim, vec, in_dim, vec,
        ),
        check_vma=False,
    )
```

time: 695 us -> 429 us (0.62)
  waiting for transfers between devices: 404 us -> 179 us
  Pallas kernels: 0 us -> 83.9 us
  matrix products: 77.3 us -> 0 us
  starting transfers between devices: 14.4 us -> 70.6 us
  local copies, waits for them, and re-layouts: 96.7 us -> 49.1 us
  blocking collectives: 39.3 us -> 0 us
  between operations: 16.1 us -> 3.28 us
    psum x2 -> x0, waiting for transfers between devices: 272 us -> none  [the longest x1 139 us: body(): d_w_qkv, d_w_out, small = lax.psum((d_w_qkv, d_w_out, small), 'dp')]
    ppermute x0 -> x43, waiting for transfers between devices: none -> 132 us  [trade(): return lax.ppermute(block, 'dp', [(i, i ^ flip) for i in range(size)])]
    ppermute x21 -> x28, waiting for transfers between devices: 133 us -> 46.8 us  [swap(): return lax.ppermute(block, 'mp', [(i, i ^ bit) for i in range(4)])]
    pallas_call x0 -> x18, Pallas kernels: none -> 83.9 us  [call(): return run(*[array for array, _ in ins])]
    dot_general x24 -> x0, matrix products: 77.3 us -> none  [the longest x8 29.2 us: dot_nt(): lax.dot_general(left_arr, right_arr, (((1,), (1,)), ((), ())), precision=...]
    ppermute x0 -> x43, starting transfers between devices: none -> 53.7 us  [trade(): return lax.ppermute(block, 'dp', [(i, i ^ flip) for i in range(size)])]
    psum x1 -> x0, blocking collectives: 39.3 us -> none  [body(): d_w_qkv, d_w_out, small = lax.psum((d_w_qkv, d_w_out, small), 'dp')]
    unnamed x125 -> x202, local copies, waits for them, and re-layouts: 21.3 us -> 43.8 us
  transfers between devices with their start and end apart: 23 -> 71, of which waited for: 11 -> 33; matrix products, arithmetic and copies ran while one was open for 16% -> 9% of each run, Pallas kernels for 0% -> 20%
where the time goes in v2:
time: 429 us; the launch traced here: 422 us
  waiting for transfers between devices  179 us (42%)
  Pallas kernels  83.9 us (20%)
  starting transfers between devices  70.6 us (16%)
  local copies, waits for them, and re-layouts  49.1 us (11%)
  other arithmetic  35.7 us (8%)
    ppermute x43, waiting for transfers between devices, trade(): return lax.ppermute(block, 'dp', [(i, i ^ flip) for i in range(size)])  132 us
    pallas_call x18, Pallas kernels, call(): return run(*[array for array, _ in ins])  83.9 us
    ppermute x43, starting transfers between devices, trade(): return lax.ppermute(block, 'dp', [(i, i ^ flip) for i in range(size)])  53.7 us
    ppermute x28, waiting for transfers between devices, swap(): return lax.ppermute(block, 'mp', [(i, i ^ bit) for i in range(4)])  46.8 us
    unnamed x202, local copies, waits for them, and re-layouts  43.8 us
    ppermute x28, starting transfers between devices, swap(): return lax.ppermute(block, 'mp', [(i, i ^ bit) for i in range(4)])  16.9 us
  transfers between devices with their start and end apart: 71, of which 33 were waited for; matrix products, arithmetic and copies ran while one was open for 9% of the time, Pallas kernels for 20%

profile of v2, /device:TPU:0, one launch (start us, length us, event | category | flops | bytes accessed | tf_op | source)
XLA Modules:
  0.0 421.8 jit_solution(2359667218518096069)
XLA Ops:
  4.6 17.0 %collective-permute-done.3 = f32[8,192]{1,0:T(8,128)S(1)} collective-permute-done((f32[8,192]{1,0:T(8,128)S(1)}, f32[8,192]{1,0:T(8,128)S(1)}, u32[]{:S(2)}, u32[]{:S(2)}) %collective-permute-start.3) | collective-permute-done | bytes 6176 | tf_op jit(solution)/shard_map/ppermute | solution.py:397
  56.9 8.3 %attend.1 = (f32[192,1024]{1,0:T(8,128)S(1)}, f32[192,1024]{1,0:T(8,128)S(1)}, f32[192,1024]{1,0:T(8,128)S(1)}, f32[192,1024]{1,0:T(8,128)S(1)}, bf16[384,1024]{...) custom-call(s32[2]{0:T(128)S(1)} %pad_add_fusion.info, ...), custom_call_target="tpu_custom_call" | custom-call | flops 4529848320 | bytes 14935560 | tf_op jit(solution)/shard_map/attend/pallas_call | solution.py:95
  79.3 11.9 %collective-permute-done.7.m2 = f32[192,1024]{1,0:T(8,128)S(1)} collective-permute-done((f32[192,1024]{1,0:T(8,128)S(1)}, f32[192,1024]{1,0:T(8,128)S(1)}, u32[]{:S(2)}, u32[]{:S(2)}) %collective-permute-start.7) | collective-permute-done | bytes 786464 | tf_op jit(solution)/shard_map/ppermute | solution.py:397
  93.5 16.5 %hidden.1 = (bf16[768,1024]{1,0:T(8,128)(2,1)}, bf16[768,1024]{1,0:T(8,128)(2,1)}, f32[768,1024]{1,0:T(8,128)}, f32[768,1024]{1,0:T(8,128)}, bf16[768,1024]{1,0:...) custom-call(s32[2]{0:T(128)S(1)} %pad_add_fusion.info, ...), custom_call_target="tpu_custom_call" | custom-call | flops 7247757312 | bytes 24439816 | tf_op jit(solution)/shard_map/hidden/pallas_call | solution.py:95
  117.0 5.1 %down.1 = (f32[384,1024]{1,0:T(8,128)S(1)}, f32[384,1024]{1,0:T(8,128)S(1)}) custom-call(s32[2]{0:T(128)S(1)} %pad_add_fusion.info, bf16[768,768]{1,0:T(8,128)(2,1)S(1)} %copy-done.58, bf16[768,768]{1,0:T(8,128)(2,1)S(1)} %copy-done.60, bf16[768,1024]{1,0:T(8,128)(2,1)S(1)} %copy-done.89, bf16[768,1024]{1,0:T(8,128)(2,1)S(1)} %copy-done.91), custom_call_target="tpu_custom_call" | custom-call | flops 3623878656 | bytes 8650760 | tf_op jit(solution)/shard_map/down/pallas_call | solution.py:95
  125.5 4.1 down_grad.1
  129.7 10.9 %hidden_back.1 = (bf16[768,1024]{1,0:T(8,128)(2,1)S(1)}, bf16[768,1024]{1,0:T(8,128)(2,1)S(1)}, f32[384,1024]{1,0:T(8,128)S(1)}, f32[384,1024]{1,0:T(8,128)S(1)}, f32[768,128]{1,0:T(8,128)S(1)}) custom-call(s32[2]{0:T(128)S(1)} %pad_add_fusion.info, bf16[768,1024]{1,0:T(8,128)(2,1)S(1)} %get-tuple-element.122.b_hi.c_hi, ...), custom_call_target="tpu_custom_call" | custom-call | flops 7247757312 | bytes 17694728 | tf_op jit(solution)/shard_map/hidden_back/pallas_call | solution.py:95
  140.9 4.3 %up_grad.1 = f32[768,768]{1,0:T(8,128)S(1)} custom-call(bf16[768,1024]{1,0:T(8,128)(2,1)S(1)} %copy-done.87, bf16[768,1024]{1,0:T(8,128)(2,1)S(1)} %copy-done.88, bf16[768,1024]{1,0:T(8,128)(2,1)S(1)} %get-tuple-element.131.b_hi, bf16[768,1024]{1,0:T(8,128)(2,1)S(1)} %get-tuple-element.132.b_lo), custom_call_target="tpu_custom_call" | custom-call | flops 3623878656 | bytes 8650752 | tf_op jit(solution)/shard_map/up_grad/pallas_call | solution.py:95
  149.4 12.2 %collective-permute-done.56 = f32[192,768]{1,0:T(8,128)S(1)} collective-permute-done((f32[192,768]{1,0:T(8,128)S(1)}, f32[192,768]{1,0:T(8,128)S(1)}, u32[]{:S(2)}, u32[]{:S(2)}) %collective-permute-start.56) | collective-permute-done | bytes 589856 | tf_op jit(solution)/shard_map/ppermute | solution.py:432
  164.0 9.7 %collective-permute-done.66 = f32[192,768]{1,0:T(8,128)S(1)} collective-permute-done((f32[192,768]{1,0:T(8,128)S(1)}, f32[192,768]{1,0:T(8,128)S(1)}, u32[]{:S(2)}, u32[]{:S(2)}) %collective-permute-start.66) | collective-permute-done | bytes 589856 | tf_op jit(solution)/shard_map/ppermute | solution.py:432
  179.5 4.8 %collective-permute-done.57 = f32[96,768]{1,0:T(8,128)S(1)} collective-permute-done((f32[96,768]{1,0:T(8,128)S(1)}, f32[96,768]{1,0:T(8,128)S(1)}, u32[]{:S(2)}, u32[]{:S(2)}) %collective-permute-start.57) | collective-permute-done | bytes 294944 | tf_op jit(solution)/shard_map/ppermute | solution.py:432
  196.5 20.3 %collective-permute-done.58 = f32[96,768]{1,0:T(8,128)S(1)} collective-permute-done((f32[96,768]{1,0:T(8,128)S(1)}, f32[96,768]{1,0:T(8,128)S(1)}, u32[]{:S(2)}, u32[]{:S(2)}) %collective-permute-start.58) | collective-permute-done | bytes 294944 | tf_op jit(solution)/shard_map/ppermute | solution.py:432
  228.7 4.1 collective-permute-done.68
  249.2 11.3 %collective-permute-done.60 = f32[192,768]{1,0:T(8,128)S(1)} collective-permute-done((f32[192,768]{1,0:T(8,128)S(1)}, f32[192,768]{1,0:T(8,128)S(1)}, u32[]{:S(2)}, u32[]{:S(2)}) %collective-permute-start.60) | collective-permute-done | bytes 589856 | tf_op jit(solution)/shard_map/ppermute | solution.py:432
  262.2 8.5 %collective-permute-done.70 = f32[192,768]{1,0:T(8,128)S(1)} collective-permute-done((f32[192,768]{1,0:T(8,128)S(1)}, f32[192,768]{1,0:T(8,128)S(1)}, u32[]{:S(2)}, u32[]{:S(2)}) %collective-permute-start.70) | collective-permute-done | bytes 589856 | tf_op jit(solution)/shard_map/ppermute | solution.py:432
  273.7 6.6 %inner_back.1 = (bf16[768,1024]{1,0:T(8,128)(2,1)S(1)}, bf16[768,1024]{1,0:T(8,128)(2,1)S(1)}, bf16[192,1024]{1,0:T(8,128)(2,1)S(1)}, bf16[192,1024]{1,0:T(8,128...) custom-call(s32[2]{0:T(128)S(1)} %pad_add_fusion.info, ...), custom_call_target="tpu_custom_call" | custom-call | flops 905969664 | bytes 19128328 | tf_op jit(solution)/shard_map/inner_back/pallas_call | solution.py:95
  280.5 6.6 %mix_back.1 = (bf16[384,1024]{1,0:T(8,128)(2,1)S(1)}, bf16[384,1024]{1,0:T(8,128)(2,1)S(1)}, f32[1024,256]{1,0:T(8,128)S(1)}, f32[192,128]{1,0:T(8,128)S(1)}) custom-call(bf16[384,1024]{1,0:T(8,128)(2,1)S(1)} %get-tuple-element.142.d_hi, bf16[384,1024]{1,0:T(8,128)(2,1)S(1)} %get-tuple-element.143.d_lo, bf16[384,1024]{1,0:T(8,128)(2,1)S(1)} %copy-done.84, ...), custom_call_target="tpu_custom_call" | custom-call | flops 2536715008 | bytes 10584064 | tf_op jit(solution)/shard_map/mix_back/pallas_call | solution.py:95
  294.2 6.9 %project_back.1 = (f32[384,1024]{1,0:T(8,128)S(1)}, f32[384,1024]{1,0:T(8,128)}, f32[8,1024]{1,0:T(8,128)S(1)}) custom-call(s32[2]{0:T(128)S(1)} %pad_add_fusion.info, bf16[192,1024]{1,0:T(8,128)(2,1)S(1)} %get-tuple-element.153.c_hi.dq_hi, bf16[192,1024]{1,0:T(8,128)(2,1)S(1)} %get-tuple-element.149.c_lo.dq_lo, ...), custom_call_target="tpu_custom_call" | custom-call | flops 2717908992 | bytes 10510344 | tf_op jit(solution)/shard_map/project_back/pallas_call | solution.py:95
  303.5 5.0 %collective-permute-done.27 = f32[192,768]{1,0:T(8,128)S(1)} collective-permute-done((f32[192,768]{1,0:T(8,128)S(1)}, f32[192,768]{1,0:T(8,128)S(1)}, u32[]{:S(2)}, u32[]{:S(2)}) %collective-permute-start.27) | collective-permute-done | bytes 589856 | tf_op jit(solution)/shard_map/ppermute | solution.py:432
  309.5 8.3 %collective-permute-done.32 = f32[192,768]{1,0:T(8,128)S(1)} collective-permute-done((f32[192,768]{1,0:T(8,128)S(1)}, f32[192,768]{1,0:T(8,128)S(1)}, u32[]{:S(2)}, u32[]{:S(2)}) %collective-permute-start.32) | collective-permute-done | bytes 589856 | tf_op jit(solution)/shard_map/ppermute | solution.py:432
  320.1 7.4 %collective-permute-done.44 = f32[64,256]{1,0:T(8,128)S(1)} collective-permute-done((f32[64,256]{1,0:T(8,128)S(1)}, f32[64,256]{1,0:T(8,128)S(1)}, u32[]{:S(2)}, u32[]{:S(2)}) %collective-permute-start.44) | collective-permute-done | bytes 65568 | tf_op jit(solution)/shard_map/ppermute | solution.py:432
  334.1 4.9 %collective-permute-done.45 = f32[32,256]{1,0:T(8,128)S(1)} collective-permute-done((f32[32,256]{1,0:T(8,128)S(1)}, f32[32,256]{1,0:T(8,128)S(1)}, u32[]{:S(2)}, u32[]{:S(2)}) %collective-permute-start.45) | collective-permute-done | bytes 32800 | tf_op jit(solution)/shard_map/ppermute | solution.py:432
  376.9 4.5 %collective-permute-done.34 = f32[96,768]{1,0:T(8,128)} collective-permute-done((f32[96,768]{1,0:T(8,128)S(1)}, f32[96,768]{1,0:T(8,128)}, u32[]{:S(2)}, u32[]{:S(2)}) %collective-permute-start.34) | collective-permute-done | bytes 294944 | tf_op jit(solution)/shard_map/ppermute | solution.py:432
  391.5 14.4 %collective-permute-done.21.come = f32[192,1024]{1,0:T(8,128)S(1)} collective-permute-done((f32[192,1024]{1,0:T(8,128)S(1)}, f32[192,1024]{1,0:T(8,128)S(1)}, u32[]{:S(2)}, u32[]{:S(2)}) %collective-permute-start.21) | collective-permute-done | bytes 786464 | tf_op jit(solution)/shard_map/ppermute | solution.py:397
  (452 shorter events, 205.0 us)
Async XLA Ops:
  0.7 46.5 %collective-permute-start.1 = (f32[192,1024]{1,0:T(8,128)}, f32[192,1024]{1,0:T(8,128)}, u32[]{:S(2)}, u32[]{:S(2)}) collective-permute-start(f32[192,1024]{1,0:T(8,128)} %bitcast.58), channel_id=1, source_target_pairs={{0,2},{1,3},{2,0},{3,1},{4,6},{5,7},{6,4},{7,5},{8,10},{9,11},{10,... | collective-permute-start | bytes 2359304 | tf_op jit(solution)/shard_map/ppermute | solution.py:397
  4.5 42.5 %collective-permute-start.2 = (f32[8,192]{1,0:T(8,128)S(1)}, f32[8,192]{1,0:T(8,128)S(1)}, u32[]{:S(2)}, u32[]{:S(2)}) collective-permute-start(f32[8,192]{1,0:T(8,128)S(1)} %get-tuple-element.229), channel_id=1, source_target_pairs={{0,1},{1,0},{2,3},{3,2},{4,5},{5,4},{6,7},{7,6},{8,9},{9,8},{10,11... | collective-permute-start | bytes 18440 | tf_op jit(solution)/shard_map/ppermute | solution.py:397
  21.6 25.4 %collective-permute-start.4 = (f32[8,192]{1,0:T(8,128)S(1)}, f32[8,192]{1,0:T(8,128)S(1)}, u32[]{:S(2)}, u32[]{:S(2)}) collective-permute-start(f32[8,192]{1,0:T(8,128)S(1)} %collective-permute-done.3), channel_id=1, source_target_pairs={{0,1},{1,0},{2,3},{3,2},{4,5},{5,4},{6,7},{7,6},{8,9},{9,8},{10,11... | collective-permute-start | bytes 18440 | tf_op jit(solution)/shard_map/ppermute | solution.py:397
  21.6 28.4 %collective-permute-start = (f32[192,1024]{1,0:T(8,128)}, f32[192,1024]{1,0:T(8,128)}, u32[]{:S(2)}, u32[]{:S(2)}) collective-permute-start(f32[192,1024]{1,0:T(8,128)} %bitcast.59), channel_id=1, source_target_pairs={{0,1},{1,0},{2,3},{3,2},{4,5},{5,4},{6,7},{7,6},{8,9},{9,8},{10,11... | collective-permute-start | bytes 2359304 | tf_op jit(solution)/shard_map/ppermute | solution.py:397
  48.2 24.7 %collective-permute-start.9 = (f32[192,768]{1,0:T(8,128)}, f32[192,768]{1,0:T(8,128)S(1)}, u32[]{:S(2)}, u32[]{:S(2)}) collective-permute-start(f32[192,768]{1,0:T(8,128)} %own.1), channel_id=1, source_target_pairs={{0,2},{1,3},{2,0},{3,1},{4,6},{5,7},{6,4},{7,5},{8,10},{9,11},{10,... | collective-permute-start | bytes 1769480 | tf_op jit(solution)/shard_map/ppermute | solution.py:397
  92.6 30.0 %collective-permute-start.13 = (f32[192,1024]{1,0:T(8,128)S(1)}, f32[192,1024]{1,0:T(8,128)S(1)}, u32[]{:S(2)}, u32[]{:S(2)}) collective-permute-start(f32[192,1024]{1,0:T(8,128)S(1)} %bitcast.55), channel_id=1, source_target_pairs={{0,1},{1,0},{2,3},{3,2},{4,5},{5,4},{6,7},{7,6},{8,9},{9,8},{10,11... | collective-permute-start | bytes 2359304 | tf_op jit(solution)/shard_map/ppermute | solution.py:397
  122.2 95.4 %collective-permute-start.12 = (f32[384,1024]{1,0:T(8,128)S(1)}, f32[384,1024]{1,0:T(8,128)}, u32[]{:S(2)}, u32[]{:S(2)}) collective-permute-start(f32[384,1024]{1,0:T(8,128)S(1)} %get-tuple-element.117), channel_id=1, source_target_pairs={{0,1},{1,0},{2,3},{3,2},{4,5},{5,4},{6,7},{7,6},{8,9},{9,8},{10,11... | collective-permute-start | bytes 4718600 | tf_op jit(solution)/shard_map/ppermute | solution.py:397
  140.7 51.2 %collective-permute-start.16 = (f32[384,1024]{1,0:T(8,128)S(1)}, f32[384,1024]{1,0:T(8,128)S(1)}, u32[]{:S(2)}, u32[]{:S(2)}) collective-permute-start(f32[384,1024]{1,0:T(8,128)S(1)} %get-tuple-element.128), channel_id=1, source_target_pairs={{0,1},{1,0},{2,3},{3,2},{4,5},{5,4},{6,7},{7,6},{8,9},{9,8},{10,11... | collective-permute-start | bytes 4718600 | tf_op jit(solution)/shard_map/ppermute | solution.py:397
  148.8 24.9 %collective-permute-start.66 = (f32[192,768]{1,0:T(8,128)S(1)}, f32[192,768]{1,0:T(8,128)S(1)}, u32[]{:S(2)}, u32[]{:S(2)}) collective-permute-start(f32[192,768]{1,0:T(8,128)S(1)} %constant_dynamic-slice_fusion.1), channel_id=1, source_target_pairs={{0,8},{4,12},{8,0},{12,4},{16,24},{20,28},{24,16},{28,20},{1,9},{5... | collective-permute-start | bytes 1769480 | tf_op jit(solution)/shard_map/ppermute | solution.py:432
  163.2 21.0 %collective-permute-start.57 = (f32[96,768]{1,0:T(8,128)S(1)}, f32[96,768]{1,0:T(8,128)S(1)}, u32[]{:S(2)}, u32[]{:S(2)}) collective-permute-start(f32[96,768]{1,0:T(8,128)S(1)} %constant_dynamic-slice_fusion.4), channel_id=1, source_target_pairs={{0,4},{4,0},{8,12},{12,8},{16,20},{20,16},{24,28},{28,24},{1,5},{5... | collective-permute-start | bytes 884744 | tf_op jit(solution)/shard_map/ppermute | solution.py:432
  185.8 30.9 %collective-permute-start.58 = (f32[96,768]{1,0:T(8,128)S(1)}, f32[96,768]{1,0:T(8,128)S(1)}, u32[]{:S(2)}, u32[]{:S(2)}) collective-permute-start(f32[96,768]{1,0:T(8,128)S(1)} %dynamic-slice_add_fusion.9), channel_id=1, source_target_pairs={{0,16},{4,20},{8,24},{12,28},{16,0},{20,4},{24,8},{28,12},{1,17},{... | collective-permute-start | bytes 884744 | tf_op jit(solution)/shard_map/ppermute | solution.py:432
  189.2 37.2 %collective-permute-start.53 = (f32[96,768]{1,0:T(8,128)}, f32[96,768]{1,0:T(8,128)}, u32[]{:S(2)}, u32[]{:S(2)}) collective-permute-start(f32[96,768]{1,0:T(8,128)} %dynamic-slice_add_fusion.10), channel_id=1, source_target_pairs={{0,16},{4,20},{8,24},{12,28},{16,0},{20,4},{24,8},{28,12},{1,17},{... | collective-permute-start | bytes 884744 | tf_op jit(solution)/shard_map/ppermute | solution.py:432
  191.8 40.9 %collective-permute-start.68 = (f32[96,768]{1,0:T(8,128)}, f32[96,768]{1,0:T(8,128)}, u32[]{:S(2)}, u32[]{:S(2)}) collective-permute-start(f32[96,768]{1,0:T(8,128)} %dynamic-slice_add_fusion.7), channel_id=1, source_target_pairs={{0,16},{4,20},{8,24},{12,28},{16,0},{20,4},{24,8},{28,12},{1,17},{... | collective-permute-start | bytes 884744 | tf_op jit(solution)/shard_map/ppermute | solution.py:432
  194.4 48.6 %collective-permute-start.17 = (f32[384,1024]{1,0:T(8,128)}, f32[384,1024]{1,0:T(8,128)}, u32[]{:S(2)}, u32[]{:S(2)}) collective-permute-start(f32[384,1024]{1,0:T(8,128)} %add.268), channel_id=1, source_target_pairs={{0,2},{1,3},{2,0},{3,1},{4,6},{5,7},{6,4},{7,5},{8,10},{9,11},{10,... | collective-permute-start | bytes 4718600 | tf_op jit(solution)/shard_map/ppermute | solution.py:397
  238.3 22.2 %collective-permute-start.60 = (f32[192,768]{1,0:T(8,128)S(1)}, f32[192,768]{1,0:T(8,128)S(1)}, u32[]{:S(2)}, u32[]{:S(2)}) collective-permute-start(f32[192,768]{1,0:T(8,128)S(1)} %pad_maximum_fusion.6), channel_id=1, source_target_pairs={{0,8},{4,12},{8,0},{12,4},{16,24},{20,28},{24,16},{28,20},{1,9},{5... | collective-permute-start | bytes 1769480 | tf_op jit(solution)/shard_map/ppermute | solution.py:432
  243.0 27.7 %collective-permute-start.70 = (f32[192,768]{1,0:T(8,128)S(1)}, f32[192,768]{1,0:T(8,128)S(1)}, u32[]{:S(2)}, u32[]{:S(2)}) collective-permute-start(f32[192,768]{1,0:T(8,128)S(1)} %pad_maximum_fusion.8), channel_id=1, source_target_pairs={{0,8},{4,12},{8,0},{12,4},{16,24},{20,28},{24,16},{28,20},{1,9},{5... | collective-permute-start | bytes 1769480 | tf_op jit(solution)/shard_map/ppermute | solution.py:432
  245.2 28.4 %collective-permute-start.19 = (f32[384,1024]{1,0:T(8,128)S(1)}, f32[384,1024]{1,0:T(8,128)S(1)}, u32[]{:S(2)}, u32[]{:S(2)}) collective-permute-start(f32[384,1024]{1,0:T(8,128)S(1)} %add.273.half), channel_id=1, source_target_pairs={{0,1},{1,0},{2,3},{3,2},{4,5},{5,4},{6,7},{7,6},{8,9},{9,8},{10,11... | collective-permute-start | bytes 4718600 | tf_op jit(solution)/shard_map/ppermute | solution.py:397
  247.9 22.9 %collective-permute-start.65 = (f32[192,768]{1,0:T(8,128)S(1)}, f32[192,768]{1,0:T(8,128)S(1)}, u32[]{:S(2)}, u32[]{:S(2)}) collective-permute-start(f32[192,768]{1,0:T(8,128)S(1)} %pad_maximum_fusion.7), channel_id=1, source_target_pairs={{0,4},{4,0},{8,12},{12,8},{16,20},{20,16},{24,28},{28,24},{1,5},{5... | collective-permute-start | bytes 1769480 | tf_op jit(solution)/shard_map/ppermute | solution.py:432
  272.5 101.5 %collective-permute-start.18 = (f32[192,1024]{1,0:T(8,128)}, f32[192,1024]{1,0:T(8,128)S(1)}, u32[]{:S(2)}, u32[]{:S(2)}) collective-permute-start(f32[192,1024]{1,0:T(8,128)} %constant_dynamic-slice_fusion.20), channel_id=1, source_target_pairs={{0,2},{1,3},{2,0},{3,1},{4,6},{5,7},{6,4},{7,5},{8,10},{9,11},{10,... | collective-permute-start | bytes 2359304 | tf_op jit(solution)/shard_map/ppermute | solution.py:397
  301.4 82.7 %collective-permute-start.20 = (f32[384,1024]{1,0:T(8,128)}, f32[384,1024]{1,0:T(8,128)}, u32[]{:S(2)}, u32[]{:S(2)}) collective-permute-start(f32[384,1024]{1,0:T(8,128)} %get-tuple-element.158), channel_id=1, source_target_pairs={{0,1},{1,0},{2,3},{3,2},{4,5},{5,4},{6,7},{7,6},{8,9},{9,8},{10,11... | collective-permute-start | bytes 4718600 | tf_op jit(solution)/shard_map/ppermute | solution.py:397
  302.4 74.3 %collective-permute-start.23 = (f32[8,1024]{1,0:T(8,128)S(1)}, f32[8,1024]{1,0:T(8,128)S(1)}, u32[]{:S(2)}, u32[]{:S(2)}) collective-permute-start(f32[8,1024]{1,0:T(8,128)S(1)} %add.275), channel_id=1, source_target_pairs={{0,2},{1,3},{2,0},{3,1},{4,6},{5,7},{6,4},{7,5},{8,10},{9,11},{10,... | collective-permute-start | bytes 98312 | tf_op jit(solution)/shard_map/ppermute | solution.py:397
  355.0 21.8 %collective-permute-start.29 = (f32[96,768]{1,0:T(8,128)S(1)}, f32[96,768]{1,0:T(8,128)S(1)}, u32[]{:S(2)}, u32[]{:S(2)}) collective-permute-start(f32[96,768]{1,0:T(8,128)S(1)} %dynamic-slice_add_fusion.12), channel_id=1, source_target_pairs={{0,16},{4,20},{8,24},{12,28},{16,0},{20,4},{24,8},{28,12},{1,17},{... | collective-permute-start | bytes 884744 | tf_op jit(solution)/shard_map/ppermute | solution.py:432
  388.0 23.6 %collective-permute-start.31 = (f32[192,768]{1,0:T(8,128)}, f32[192,768]{1,0:T(8,128)}, u32[]{:S(2)}, u32[]{:S(2)}) collective-permute-start(f32[192,768]{1,0:T(8,128)} %pad_maximum_fusion.3), channel_id=1, source_target_pairs={{0,4},{4,0},{8,12},{12,8},{16,20},{20,16},{24,28},{28,24},{1,5},{5... | collective-permute-start | bytes 1769480 | tf_op jit(solution)/shard_map/ppermute | solution.py:432
  390.5 25.9 %collective-permute-start.36 = (f32[192,768]{1,0:T(8,128)}, f32[192,768]{1,0:T(8,128)}, u32[]{:S(2)}, u32[]{:S(2)}) collective-permute-start(f32[192,768]{1,0:T(8,128)} %pad_maximum_fusion.4), channel_id=1, source_target_pairs={{0,8},{4,12},{8,0},{12,4},{16,24},{20,28},{24,16},{28,20},{1,9},{5... | collective-permute-start | bytes 1769480 | tf_op jit(solution)/shard_map/ppermute | solution.py:432
  (148 other events, 1075.8 us)

commit v3 on v2

v3 whole, which is shorter than its diff:
```python
import math
from functools import partial

import jax
import jax.numpy as jnp
from jax import lax
from jax.experimental import pallas as pl
from jax.experimental.pallas import tpu as pltpu
from jax.sharding import PartitionSpec as P

EPSILON = 1e-05
TB = 256
WIDE = 512
SCALE = 0.0
PIN_MID = True
PIN_GLUE = False
PIN_ATT = True
PIN_HIN = True
PIN_DG = False
PIN_HID = False
NN = (((1,), (0,)), ((), ()))
NT = (((1,), (1,)), ((), ()))
F32 = jnp.float32
BF16 = jnp.bfloat16


def split(wide):
    high = wide.astype(BF16)
    return high, (wide - high.astype(F32)).astype(BF16)


def dot3(left, right, dims):
    def one(a, b):
        return lax.dot_general(a, b, dims, preferred_element_type=F32)

    return one(left[0], right[0]) + (one(left[0], right[1]) + one(left[1], right[0]))


def put(high_ref, low_ref, wide):
    high, low = split(wide)
    high_ref[...] = high
    low_ref[...] = low


def get(high_ref, low_ref):
    return high_ref[...], low_ref[...]


def reverse_lanes(wide):
    size = wide.shape[1]
    row = lax.broadcasted_iota(jnp.int32, (size, size), 0)
    col = lax.broadcasted_iota(jnp.int32, (size, size), 1)
    turn = (row + col == size - 1).astype(F32).astype(BF16)
    high, rest = split(wide)
    middle = wide - high.astype(F32)
    low = (middle - rest.astype(F32)).astype(BF16)

    def one(part):
        return lax.dot_general(part, turn, NN, preferred_element_type=F32)

    return one(high) + (one(rest) + one(low))


def live_row(length, start, width):
    return (lax.broadcasted_iota(jnp.int32, (1, width), 1) + start < length).astype(F32)


def whole(shape):
    return pl.BlockSpec(shape, lambda i: (0,) * len(shape))


def across(rows, width=WIDE):
    return pl.BlockSpec((rows, width), lambda i: (0, i))


SCALARS = pl.BlockSpec(memory_space=pltpu.SMEM)


def shaped(shape, dtype=F32):
    return jax.ShapeDtypeStruct(shape, dtype)


def to_hbm(array):
    return pltpu.with_memory_space_constraint(array, pltpu.HBM)


def call(kernel, grid, ins, outs, scratch=(), name=None, pin=True, pin_out=True):
    held = sum(2 * math.prod(spec.block_shape) * array.dtype.itemsize for array, spec in ins if spec.block_shape)
    held += sum(2 * math.prod(spec.block_shape) * shape.dtype.itemsize for shape, spec in outs)
    held += sum(math.prod(ref.shape) * jnp.dtype(ref.dtype).itemsize for ref in scratch)
    moved = sum(array.size * array.dtype.itemsize for array, _ in ins)
    moved += sum(math.prod(shape.shape) * shape.dtype.itemsize for shape, _ in outs)
    arrays = [array if spec is SCALARS or not pin else to_hbm(array) for array, spec in ins]
    run = pl.pallas_call(
        kernel,
        grid=(grid,),
        in_specs=[spec for _, spec in ins],
        out_specs=[spec for _, spec in outs],
        out_shape=[pltpu.HBM(shape.shape, shape.dtype) if pin_out else shape for shape, _ in outs],
        scratch_shapes=list(scratch),
        compiler_params=pltpu.CompilerParams(
            dimension_semantics=("arbitrary",), vmem_limit_bytes=min(held + 16 * 2**20, 58 * 2**20)
        ),
        cost_estimate=pl.CostEstimate(flops=0, transcendentals=0, bytes_accessed=int(moved * SCALE)),
        name=name,
    )
    return list(run(*arrays))


def place_rows(target, place, parts):
    for flip, part in enumerate(parts):
        rows = part.shape[0]
        target[pl.ds(pl.multiple_of((place ^ flip) * rows, rows), rows), :] = part[...]


def take_rows(source, index, rows):
    return source[pl.ds(pl.multiple_of(index * rows, rows), rows), :]


def fold(wide):
    total = wide[:, :128]
    for at in range(128, wide.shape[1], 128):
        total = total + wide[:, at : at + 128]
    return total


def band_kernel(bias, high, low):
    window = bias.shape[1]
    turned = reverse_lanes(jnp.exp(bias[...]))
    wide = jnp.concatenate([turned, jnp.zeros_like(turned)], axis=1)
    skewed = pltpu.roll(wide, 1, 1, stride=1, stride_axis=0)
    row = lax.broadcasted_iota(jnp.int32, wide.shape, 0)
    col = lax.broadcasted_iota(jnp.int32, wide.shape, 1)
    band = skewed + (col <= row).astype(F32)
    first = (pl.program_id(0) == 0) & (col < window)
    put(high, low, jnp.where(first, 0.0, band))


def qkv_weights_kernel(w_q, w_k, w_v, high, low, high_t, low_t):
    stacked = jnp.concatenate([w_q[...], w_k[...], w_v[...]], axis=0)
    put(high, low, stacked)
    put(high_t, low_t, stacked.T)


def weights_kernel(w, high, low, high_t, low_t):
    put(high, low, w[...])
    put(high_t, low_t, w[...].T)


def out_weights_kernel(own, near, far, far_near, high_t, low_t):
    stacked = jnp.concatenate([own[...], near[...], far[...], far_near[...]], axis=0)
    put(high_t, low_t, stacked.T)


def column_stats(values_in):
    mean = jnp.mean(values_in, axis=0, keepdims=True)
    var = jnp.mean(values_in * values_in, axis=0, keepdims=True) - mean * mean
    return mean, lax.rsqrt(var + EPSILON)


def attend_kernel(
    info, x0, x1, x2, x3, v0, v1, v2, v3, w_hi, w_lo, band_hi, band_lo,
    cols, mixed, quotient, f_query, f_numer, pair_hi, pair_lo, n_hi, n_lo, stats,
    x_all, far, last_hi, last_lo,
):
    step = pl.program_id(0)
    chans = x0.shape[0]
    window = TB

    @pl.when(step == 0)
    def _():
        for flip, part in enumerate((v0, v1, v2, v3)):
            start = pl.multiple_of((info[0] ^ flip) * chans, chans)
            cols[pl.ds(start, chans), :] = part[...].T[:chans]

    biases = v0[...].T[:chans]
    place_rows(x_all, info[0], (x0, x1, x2, x3))
    x = x_all[...]
    mean, scale = column_stats(x)
    stats[0:1, :] = mean
    stats[1:2, :] = scale
    normed = split((x - mean) * scale * cols[:, 0:1] + cols[:, 1:2])
    n_hi[...], n_lo[...] = normed
    projected = dot3(get(w_hi, w_lo), normed, NN)
    exp_keys = jnp.exp(projected[chans : 2 * chans])
    carried = exp_keys * (projected[2 * chans :] + biases[:, 6:7])
    pair = split(jnp.concatenate([carried, exp_keys], axis=0))
    pair_hi[...], pair_lo[...] = pair

    @pl.when(step == 0)
    def _():
        far[...] = jnp.zeros_like(far)
        last_hi[...] = jnp.zeros_like(last_hi)
        last_lo[...] = jnp.zeros_like(last_lo)

    last = get(last_hi, last_lo)
    total = far[:, 0:1]
    gates = jax.nn.sigmoid(projected[:chans] + biases[:, 5:6])
    for at in range(0, x.shape[1], window):
        here = slice(at, at + window)
        near = (band_hi[here, :], band_lo[here, :])
        block = (pair[0][:, here], pair[1][:, here])
        sums = dot3(block, (near[0][:, window:], near[1][:, window:]), NT)
        sums = sums + dot3(last, (near[0][:, :window], near[1][:, :window]), NT)
        sums = sums + total
        total = total + jnp.sum(last[0].astype(F32) + last[1].astype(F32), axis=1, keepdims=True)
        last = block
        inverse = 1.0 / sums[chans:]
        ratio = sums[:chans] * inverse
        gate = gates[:, here]
        quotient[:, here] = ratio
        mixed[:, here] = gate * ratio
        f_query[:, here] = ratio * gate * (1.0 - gate)
        f_numer[:, here] = gate * inverse
    far[...] = jnp.broadcast_to(total, far.shape)
    last_hi[...], last_lo[...] = last


def hidden_kernel(
    info, m0, m1, m2, m3, x0, x1, x2, x3, cols, wo_hi, wo_lo, wu_hi, wu_lo, up_bias,
    act_hi, act_lo, slope, n_hi, n_lo, inner_own, stats,
    x_all,
):
    step = pl.program_id(0)
    place_rows(x_all, info[0], (x0, x1, x2, x3))
    live = live_row(info[1], step * WIDE, WIDE)
    parts = jnp.concatenate([m0[...], m1[...], m2[...], m3[...]], axis=0)
    out = dot3(get(wo_hi, wo_lo), split(parts), NN)
    inner = x_all[...] + live * (out + cols[:, 2:3])
    x_all[...] = inner
    inner_own[...] = take_rows(x_all, info[0], x0.shape[0])
    mean, scale = column_stats(inner)
    stats[0:1, :] = scale
    unit = (inner - mean) * scale
    normed = split(unit * cols[:, 3:4] + cols[:, 4:5])
    n_hi[...], n_lo[...] = normed
    pre = dot3(get(wu_hi, wu_lo), normed, NN) + up_bias[...]
    root = 0.7978845608028654
    cubic = 0.044715
    square = pre * pre
    bent = jnp.tanh(root * pre * (1.0 + cubic * square))
    put(act_hi, act_lo, 0.5 * pre * (1.0 + bent))
    slope[...] = 0.5 * (1.0 + bent) + 0.5 * pre * (1.0 - bent * bent) * (
        root * (1.0 + 3.0 * cubic * square)
    )


def parted(rows, info):
    step = rows // 4
    for half in range(2):
        bit = info[2 + half]
        yield pl.multiple_of((2 * half + bit) * step, step)
        yield pl.multiple_of((2 * half + 1 - bit) * step, step)


def outer_kernel(info, a_hi, a_lo, b_hi, b_lo, *rest):
    outs, (s_hi, s_lo) = rest[:4], rest[4:]
    rows = a_hi.shape[0]
    step = rows // 4

    @pl.when(pl.program_id(0) == 0)
    def _():
        for at, start in enumerate(parted(rows, info)):
            here = slice(at * step, (at + 1) * step)
            s_hi[here, :] = a_hi[pl.ds(start, step), :]
            s_lo[here, :] = a_lo[pl.ds(start, step), :]

    grad = dot3(get(s_hi, s_lo), get(b_hi, b_lo), NT)
    for at, out in enumerate(outs):
        out[...] = grad[at * step : (at + 1) * step]


def down_grad_kernel(info, a_hi, a_lo, c0, c1, c2, c3, *rest):
    outs, (c_hi, c_lo, own_sum, s_hi, s_lo, c_all) = rest[:4], rest[4:]
    rows = a_hi.shape[0]
    step = rows // 4
    live = live_row(info[1], 0, c_all.shape[1])
    for at, start in enumerate(parted(rows, info)):
        here = slice(at * step, (at + 1) * step)
        s_hi[here, :] = a_hi[pl.ds(start, step), :]
        s_lo[here, :] = a_lo[pl.ds(start, step), :]
    place_rows(c_all, info[0], (c0, c1, c2, c3))
    put(c_hi, c_lo, c_all[...] * live)
    own_sum[...] = fold(c0[...] * live)
    grad = dot3(get(s_hi, s_lo), get(c_hi, c_lo), NT)
    for at, out in enumerate(outs):
        out[...] = grad[at * step : (at + 1) * step]


def order_pair(bit, first, second, keep, send):
    keep[...] = jnp.where(bit == 0, first, second)
    send[...] = jnp.where(bit == 0, second, first)


def projection_grads_kernel(
    info, mixed, b_hi, b_lo, q_hi, q_lo, kv_hi, kv_lo, n_hi, n_lo, keep_0, send_0, keep_1, send_1
):
    rows = mixed.shape[0]
    normed = get(n_hi, n_lo)
    d_out = dot3(split(mixed[...]), get(b_hi, b_lo), NT)
    d_query = dot3(get(q_hi, q_lo), normed, NT)
    order_pair(info[2], d_out, d_query, keep_0, send_0)
    d_kv = dot3(get(kv_hi, kv_lo), normed, NT)
    order_pair(info[3], d_kv[:rows], d_kv[rows:], keep_1, send_1)


def projection_done_kernel(info, h_0, c_0, h_1, c_1, d_out, d_query, d_key, d_value):
    order_pair(info[2], h_0[...], c_0[...], d_out, d_query)
    order_pair(info[3], h_1[...], c_1[...], d_key, d_value)


def halve_kernel(places, info, *refs):
    count = len(places)
    for i, at in enumerate(places):
        kept, come = refs[2 * i], refs[2 * i + 1]
        mine, send = refs[2 * count + 2 * i], refs[2 * count + 2 * i + 1]
        rows = mine.shape[0]
        mine[...] = take_rows(kept, info[at], rows) + take_rows(come, info[at], rows)
        send[...] = take_rows(kept, 1 - info[at], rows) + take_rows(come, 1 - info[at], rows)


def add_kernel(info, *refs):
    count = len(refs) // 3
    for i in range(count):
        refs[2 * count + i][...] = refs[2 * i][...] + refs[2 * i + 1][...]


def pack_kernel(info, *refs):
    rows = refs[0].shape[0]
    refs[4][:rows, :] = refs[0][...] + refs[1][...]
    refs[4][rows:, :] = refs[2][...] + refs[3][...]


def unpack_kernel(info, held, come, first, second):
    rows = first.shape[0]
    first[...] = held[:rows, :] + come[:rows, :]
    second[...] = held[rows:, :] + come[rows:, :]


def join_kernel(places, merged, info, *refs):
    count = len(places)
    for i, at in enumerate(places):
        held, come = refs[2 * i], refs[2 * i + 1]
        out = refs[2 * count] if merged else refs[2 * count + i]
        rows = held.shape[0]
        base = 2 * i if merged else 0
        out[pl.ds(pl.multiple_of((base + info[at]) * rows, rows), rows), :] = held[...]
        out[pl.ds(pl.multiple_of((base + 1 - info[at]) * rows, rows), rows), :] = come[...]


def lane_sums_kernel(*refs):
    ins, out = refs[:-1], refs[-1]
    wide = jnp.concatenate([ref[...] for ref in ins], axis=0)
    high, rest = split(wide)
    low = (wide - high.astype(F32) - rest.astype(F32)).astype(BF16)
    ones = jnp.ones((8, wide.shape[1]), BF16)

    def one(part):
        return lax.dot_general(ones, part, NT, preferred_element_type=F32)

    out[...] = one(high) + (one(rest) + one(low))


def part_halves(grid, place, keep, send):
    rows = grid.shape[0] // 4
    core = place & 1
    for far in range(2):
        here = slice(far * rows, (far + 1) * rows)
        keep[here, :] = take_rows(grid, 2 * far + core, rows)
        send[here, :] = take_rows(grid, 2 * far + 1 - core, rows)


def hidden_back_kernel(
    info, c_hi, c_lo, wd_hi, wd_lo, slope, wu_hi, wu_lo, d_hi, d_lo, keep, send, bias_sum, grid
):
    @pl.when(pl.program_id(0) == 0)
    def _():
        bias_sum[...] = jnp.zeros_like(bias_sum)

    d_pre = dot3(get(wd_hi, wd_lo), get(c_hi, c_lo), NN) * slope[...]
    bias_sum[...] += fold(d_pre)
    parts = split(d_pre)
    d_hi[...], d_lo[...] = parts
    grid[...] = dot3(get(wu_hi, wu_lo), parts, NN)
    part_halves(grid, info[0], keep, send)


def down_kernel(info, wd_hi, wd_lo, act_hi, act_lo, keep, send, grid):
    grid[...] = dot3(get(wd_hi, wd_lo), get(act_hi, act_lo), NN)
    part_halves(grid, info[0], keep, send)


def inner_back_kernel(
    info, half, other, n_hi, n_lo, stats, cols, c0, c1, c2, c3, w_out, f_query, f_numer, quotient,
    b_hi, b_lo, dq_hi, dq_lo, dp_hi, dp_lo, inner_own, sum_gain, sum_bias, sum_out, sum_query,
    c_all, d_all, normal, wo_hi, wo_lo,
):
    step = pl.program_id(0)
    place = info[0]
    core = place & 1
    chans = c0.shape[0]
    place_rows(c_all, place, (c0, c1, c2, c3))
    for far in range(2):
        here = slice(far * chans, (far + 1) * chans)
        d_all[pl.ds(pl.multiple_of((2 * far + core) * chans, chans), chans), :] = half[here, :]
        d_all[pl.ds(pl.multiple_of((2 * far + 1 - core) * chans, chans), chans), :] = other[here, :]
    live = live_row(info[1], step * WIDE, WIDE)
    scaled = d_all[...] * cols[:, 3:4]
    unit = (n_hi[...].astype(F32) + n_lo[...].astype(F32) - cols[:, 4:5]) / cols[:, 3:4]
    normal[...] = unit
    mean_one = jnp.mean(scaled, axis=0, keepdims=True)
    mean_two = jnp.mean(scaled * unit, axis=0, keepdims=True)
    d_inner = c_all[...] + stats[0:1, :] * (scaled - mean_one - unit * mean_two)
    c_all[...] = d_inner
    own = take_rows(c_all, place, chans)
    inner_own[...] = own
    d_own = take_rows(d_all, place, chans)

    @pl.when(step == 0)
    def _():
        put(wo_hi, wo_lo, w_out[...])
        for total in (sum_gain, sum_bias, sum_out, sum_query):
            total[...] = jnp.zeros_like(total)

    sum_gain[...] += fold(d_own * take_rows(normal, place, chans))
    sum_bias[...] += fold(d_own)
    sum_out[...] += fold(own * live)
    branch = split(d_inner * live)
    b_hi[...], b_lo[...] = branch
    d_mixed = dot3(get(wo_hi, wo_lo), branch, NN)
    d_query = d_mixed * f_query[...]
    sum_query[...] += fold(d_query)
    put(dq_hi, dq_lo, d_query)
    d_numer = d_mixed * f_numer[...]
    put(dp_hi, dp_lo, jnp.concatenate([d_numer, -d_numer * quotient[...]], axis=0))


def mix_back_kernel(
    d_hi, d_lo, before_hi, before_lo, here_hi, here_lo, band_hi, band_lo, bias,
    kv_hi, kv_lo, d_bias, sum_value,
    carry, later, ahead,
):
    step = pl.program_id(0)
    block = pl.num_programs(0) - 1 - step
    window = TB
    chans = d_hi.shape[0] // 2

    @pl.when(step == 0)
    def _():
        for total in (carry, later, ahead, sum_value):
            total[...] = jnp.zeros_like(total)

    d_pair = get(d_hi, d_lo)
    d_wide = d_pair[0].astype(F32) + d_pair[1].astype(F32)
    into = dot3(d_pair, get(band_hi, band_lo), NN)
    back = into[:, window:] + carry[...] + later[:, 0:1]
    carry[...] = into[:, :window]
    later[...] = later[...] + ahead[...]
    ahead[...] = jnp.broadcast_to(jnp.sum(d_wide, axis=1, keepdims=True), ahead.shape)
    turned = split(d_wide.T)
    right = dot3(turned, get(here_hi, here_lo), NN)
    left = dot3(turned, get(before_hi, before_lo), NN)
    left = jnp.where(block == 0, 0.0, left)
    wide = jnp.concatenate([reverse_lanes(right), reverse_lanes(left)], axis=1)
    placed = pltpu.roll(wide, window + 1, 1, stride=1, stride_axis=0)
    d_bias[...] = placed[:, :window] * jnp.exp(bias[...])
    pair = here_hi[...].astype(F32) + here_lo[...].astype(F32)
    d_value = pair[chans:] * back[:chans]
    d_key = pair[:chans] * back[:chans] + pair[chans:] * back[chans:]
    sum_value[...] += fold(d_value)
    put(kv_hi, kv_lo, jnp.concatenate([d_key, d_value], axis=0))


def project_back_kernel(
    info, dq_hi, dq_lo, kv_hi, kv_lo, w_hi, w_lo, x0, x1, x2, x3, stats, cols, d_pair, keep, send,
    x_all, grid,
):
    place_rows(x_all, info[0], (x0, x1, x2, x3))
    d_all = (
        jnp.concatenate([dq_hi[...], kv_hi[...]], axis=0),
        jnp.concatenate([dq_lo[...], kv_lo[...]], axis=0),
    )
    terms = dot3(get(w_hi, w_lo), d_all, NN)
    grid[...] = terms
    part_halves(grid, info[0], keep, send)
    scaled = terms * cols[:, 0:1]
    unit = (x_all[...] - stats[0:1, :]) * stats[1:2, :]
    at = grid.shape[0] // 2
    sums = (jnp.sum(scaled, axis=0, keepdims=True), jnp.sum(scaled * unit, axis=0, keepdims=True))
    sums = jnp.concatenate([*sums, jnp.zeros((6, grid.shape[1]), F32)], axis=0)
    rows, window = d_pair.shape[0] // 8, d_pair.shape[1]
    for out, core in ((keep, info[4]), (send, 1 - info[4])):
        out[at : at + 8, :] = sums
        for block in range(grid.shape[1] // window):
            start = 4 * rows * core + rows * (grid.shape[1] // window * pl.program_id(0) + block)
            lanes = slice(block * window, (block + 1) * window)
            out[at + 8 :, lanes] = d_pair[pl.ds(pl.multiple_of(start, rows), rows), :]


def core_halves_kernel(info, keep, come, mine, send):
    rows = (mine.shape[0] - 8) * 3 // 4
    for out, far in ((mine, info[5]), (send, 1 - info[5])):
        out[:rows, :] = take_rows(keep, far, rows) + take_rows(come, far, rows)
        out[rows : rows + 8, :] = keep[2 * rows : 2 * rows + 8, :] + come[2 * rows : 2 * rows + 8, :]
        half = keep[2 * rows + 8 :, :] + come[2 * rows + 8 :, :]
        wide = half.shape[1] // 2
        part = jnp.where(far == 0, half[:, :wide], half[:, wide:])
        tall = part.shape[0] // 2
        out[rows + 8 :, :wide] = part[:tall]
        out[rows + 8 :, wide:] = part[tall:]


def chip_sum_kernel(info, mine, come, pair, sums):
    rows = mine.shape[0] - pair.shape[0] - 8
    sums[...] = mine[rows : rows + 8, :] + come[rows : rows + 8, :]
    pair[...] = mine[rows + 8 :, :] + come[rows + 8 :, :]


def pair_chips_kernel(info, own, other, half):
    tall, wide = own.shape[0], own.shape[1] // 2
    for low, lanes in ((True, slice(0, wide)), (False, slice(wide, 2 * wide))):
        near = info[5] == (0 if low else 1)
        for top in range(2):
            here = slice(top * wide, (top + 1) * wide)
            half[top * tall : (top + 1) * tall, lanes] = jnp.where(near, own[:, here], other[:, here])


def pair_cores_kernel(info, own, other, d_pair):
    rows, window = own.shape[0], d_pair.shape[1]
    for half, core in ((own, info[4]), (other, 1 - info[4])):
        for block in range(4):
            start = 4 * rows * core + rows * block
            d_pair[pl.ds(pl.multiple_of(start, rows), rows), :] = half[:, block * window : (block + 1) * window]


def input_back_kernel(model, mine, come, inner_own, x_own, stats, sums, gain, d_in, sum_gain, sum_bias):
    rows = inner_own.shape[0]
    d_normed = mine[:rows, :] + come[:rows, :]
    unit = (x_own[...] - stats[0:1, :]) * stats[1:2, :]

    @pl.when(pl.program_id(0) == 0)
    def _():
        for total in (sum_gain, sum_bias):
            total[...] = jnp.zeros_like(total)

    sum_gain[...] += fold(d_normed * unit)
    sum_bias[...] += fold(d_normed)
    d_in[...] = inner_own[...] + stats[1:2, :] * (
        d_normed * gain[...] - sums[0:1, :] / model - unit * (sums[1:2, :] / model)
    )


def swap(block, bit):
    return lax.ppermute(block, "mp", [(i, i ^ bit) for i in range(4)])


def gather_parts(own):
    far = swap(own, 2)
    near = swap(own, 1)
    return own, near, far, swap(far, 1)


def in_order(parts, place):
    stacked = jnp.stack(parts)
    return jnp.concatenate(
        [lax.dynamic_index_in_dim(stacked, place ^ i, 0, keepdims=False) for i in range(4)], axis=0
    )


def after(value, *earlier):
    return lax.optimization_barrier((value, earlier))[0]


def trade(block, flip):
    size = lax.axis_size("dp")
    return lax.ppermute(block, "dp", [(i, i ^ flip) for i in range(size)])


def glue(kernel, scalars, ins, outs, name, steps=1):
    def columns(shape):
        return pl.BlockSpec((shape[0], shape[1] // steps), lambda i: (0, i))

    return call(
        kernel, steps,
        [scalars, *[(x, columns(x.shape)) for x in ins]],
        [(shaped(shape), columns(shape)) for shape in outs],
        name=name,
        pin=False,
        pin_out=PIN_GLUE,
    )


def add_trade(block, flip, *gate):
    if lax.axis_size("dp") != 8:
        return jnp.zeros_like(block)
    return trade(after(block, *gate), flip)


def settle(sums, arrived, *gates):
    comes = [s.come for s in sums]
    comes, arrived, _ = lax.optimization_barrier((comes, arrived, gates))
    for s, come in zip(sums, comes):
        s.come = come
        s.take()
    return arrived


class Sum:
    FLIPS = ((1, 2), (2, 1), (4,), (2, 1), (1, 2))

    def __init__(self, scalars, blocks, merged):
        self.merged = merged
        self.come = []
        self.scalars = scalars
        self.direct = lax.axis_size("dp") != 8
        self.stage = 0
        if self.direct:
            self.total = lax.psum(blocks, "dp")
            if merged:
                self.total = [jnp.concatenate(self.total, axis=0)]
            self.out = self.total
        else:
            self.mine, self.out = blocks[0::2], blocks[1::2]

    def send(self, *gate):
        if not self.direct:
            pairs = zip(self.out, self.FLIPS[self.stage])
            self.come = [trade(after(block, *gate), flip) for block, flip in pairs]

    def take(self):
        if self.direct:
            return
        ins = [x for pair in zip(self.mine, self.come) for x in pair]
        rows, width = self.mine[0].shape
        name = f"sum_stage_{self.stage}"
        if self.stage == 0:
            half = (rows // 2, width)
            got = glue(partial(halve_kernel, (3, 2)), self.scalars, ins, [half] * 4, name, 2)
            self.mine, self.out = got[0::2], got[1::2]
        elif self.stage == 1:
            self.mine = self.out = glue(pack_kernel, self.scalars, ins, [(2 * rows, width)], name)
        elif self.stage == 2:
            self.mine = self.out = glue(unpack_kernel, self.scalars, ins, [(rows // 2, width)] * 2, name)
        elif self.stage == 3:
            kernel = partial(join_kernel, (3, 2), False)
            self.mine = self.out = glue(kernel, self.scalars, ins, [(2 * rows, width)] * 2, name)
        else:
            shapes = [(4 * rows, width)] if self.merged else [(rows, width)] * 4
            kernel = partial(join_kernel, (2, 3), True) if self.merged else projection_done_kernel
            self.out = self.total = glue(kernel, self.scalars, ins, shapes, name, 2)
        self.stage += 1


def body(
    inputs,
    lengths,
    ln1_gain,
    ln1_bias,
    w_query,
    w_key,
    w_value,
    query_bias,
    value_bias,
    pair_bias,
    w_out,
    out_bias,
    ln2_gain,
    ln2_bias,
    w_up,
    up_bias,
    w_down,
    down_bias,
    cotangent,
):
    seq_rows, span, chans = inputs.shape
    window = pair_bias.shape[1]
    model = 4 * chans
    units = w_up.shape[1]
    steps = span // WIDE
    blocks = span // TB
    assert seq_rows == 1 and window == TB
    place = lax.axis_index("mp")
    row = lax.axis_index("dp")
    halving = lax.axis_size("dp") == 8
    bits = [row % 2, (row // 2) % 2] if halving else [jnp.int32(0)] * 2
    info = jnp.stack([place.astype(jnp.int32), lengths[0], *bits, place % 2, place // 2])

    x_own = inputs[0].T
    x_far = swap(x_own, 2)
    x_near = swap(x_own, 1)
    vectors = jnp.stack([ln1_gain, ln1_bias, out_bias, ln2_gain, ln2_bias, query_bias, value_bias])
    vectors = jnp.pad(vectors, ((0, 1), (0, 256 - chans)))
    v_far = swap(vectors, 2)
    v_near = swap(vectors, 1)

    band = call(
        band_kernel, blocks,
        [(pair_bias, pl.BlockSpec((TB, window), lambda i: (i, 0)))],
        [(shaped((span, 2 * window), BF16), pl.BlockSpec((TB, 2 * window), lambda i: (i, 0)))] * 2,
        name="band",
    )
    wide_qkv, tall_qkv = (3 * chans, model), (model, 3 * chans)
    up_dims, down_dims = (model, units), (units, model)

    def prepare(kernel, ins, dims, name):
        return call(
            kernel, 1, [(w, whole(w.shape)) for w in ins], [(shaped(d, BF16), whole(d)) for d in dims for _ in range(2)], name=name
        )

    wq_hi, wq_lo, wqt_hi, wqt_lo = prepare(
        qkv_weights_kernel, [w_query.T, w_key.T, w_value.T], [wide_qkv, tall_qkv], "qkv_weights"
    )
    wu_hi, wu_lo, wut_hi, wut_lo = prepare(weights_kernel, [w_up], [up_dims, down_dims], "up_weights")
    up_column, gain_column = up_bias[:, None], ln1_gain[:, None]
    v_far, x_far, up_column, gain_column = lax.optimization_barrier(
        (v_far, x_far, up_column, gain_column, band, wq_hi, wu_hi)
    )[:4]
    x_parts = (x_own, x_near, x_far, swap(x_far, 1))
    v_parts = (vectors, v_near, v_far, swap(v_far, 1))
    wo_own = after(w_out, x_far, v_far)
    wo_far = swap(wo_own, 2)
    wo_near = swap(w_out, 1)

    thin = (shaped((chans, span)), across(chans))
    tall_half = (shaped((model, span), BF16), across(model))
    hid_half = (shaped((units, span), BF16), across(units))
    pair_half = (shaped((2 * chans, span), BF16), across(2 * chans))
    thin_half = (shaped((chans, span), BF16), across(chans))
    rows8 = (shaped((8, span)), across(8))
    x_ins = [(x, across(chans)) for x in x_parts]
    scalars = (info, SCALARS)

    cols_out = (shaped((model, 8)), whole((model, 8)))
    cols, mixed, quotient, f_query, f_numer, pair_hi, pair_lo, n1_hi, n1_lo, stats_one = call(
        attend_kernel, steps,
        [scalars, *x_ins, *[(v, whole((8, 256))) for v in v_parts], (wq_hi, whole(wide_qkv)), (wq_lo, whole(wide_qkv))]
        + [(b, pl.BlockSpec((WIDE, 2 * window), lambda i: (i, 0))) for b in band],
        [cols_out, thin, thin, thin, thin, pair_half, pair_half, tall_half, tall_half, rows8],
        [
            pltpu.VMEM((model, WIDE), F32),
            pltpu.VMEM((2 * chans, 128), F32),
            pltpu.VMEM((2 * chans, TB), BF16),
            pltpu.VMEM((2 * chans, TB), BF16),
        ],
        name="attend",
        pin=PIN_ATT,
    )

    cols_in = (cols, whole((model, 8)))
    mixed_far = swap(mixed, 2)
    mixed_near = swap(mixed, 1)
    wo_parts = (w_out, wo_near, wo_far, swap(wo_far, 1))
    wot_hi, wot_lo = prepare(out_weights_kernel, wo_parts, [(model, model)], "out_weights")
    wd_hi, wd_lo, wdt_hi, wdt_lo = prepare(weights_kernel, [w_down], [down_dims, up_dims], "down_weights")
    mixed_far = after(mixed_far, wot_hi, wd_hi)
    mixed_parts = (mixed, mixed_near, mixed_far, swap(mixed_far, 1))
    cot_own = cotangent[0].T
    cot_far = swap(after(cot_own, mixed_far), 2)
    cot_near = swap(cot_own, 1)
    lanes_own = (shaped((chans, 128)), whole((chans, 128)))

    act_hi, act_lo, slope, n2_hi, n2_lo, inner_own, stats_two = call(
        hidden_kernel, steps,
        [scalars, *[(p, across(chans)) for p in mixed_parts], *x_ins, cols_in]
        + [(wot_hi, whole((model, model))), (wot_lo, whole((model, model)))]
        + [(wut_hi, whole(down_dims)), (wut_lo, whole(down_dims)), (up_column, whole((units, 1)))],
        [hid_half, hid_half, (shaped((units, span)), across(units)), tall_half, tall_half, thin, rows8],
        [pltpu.VMEM((model, WIDE), F32)],
        name="hidden",
        pin=PIN_HIN,
        pin_out=PIN_HID,
    )

    cot_far = after(cot_far, act_hi)
    cot_parts = (cot_own, cot_near, cot_far, swap(cot_far, 1))
    cot_ins = [(c, across(chans)) for c in cot_parts]
    def outer(a_hi, a_lo, b_hi, b_lo, name, steps=2):
        rows, inner_len = a_hi.shape
        deep = b_hi.shape[0]
        left = whole((rows, inner_len))
        right = pl.BlockSpec((deep // steps, inner_len), lambda i: (i, 0))
        part = (shaped((rows // 4, deep)), across(rows // 4, deep // steps))
        grads = call(
            outer_kernel, steps,
            [scalars, (a_hi, left), (a_lo, left), (b_hi, right), (b_lo, right)],
            [part] * 4,
            [pltpu.VMEM((rows, inner_len), BF16)] * 2,
            name=name,
            pin=False,
        )
        return Sum(scalars, grads, True)

    whole_half = (shaped((model, span), BF16), whole((model, span)))
    block = (shaped((units // 4, model)), whole((units // 4, model)))
    *grads, c_hi, c_lo, s_down = call(
        down_grad_kernel, 1,
        [scalars, (act_hi, whole((units, span))), (act_lo, whole((units, span))), *[(c, whole((chans, span))) for c in cot_parts]],
        [block] * 4 + [whole_half, whole_half, lanes_own],
        [pltpu.VMEM((units, span), BF16)] * 2 + [pltpu.VMEM((model, span), F32)],
        name="down_grad",
        pin=PIN_DG,
    )
    g_down = Sum(scalars, grads, True)
    g_down.send()
    c_hi, c_lo = after((c_hi, c_lo), g_down.out)
    half_out = (shaped((2 * chans, span)), across(2 * chans))
    half_shape = (2 * chans, span)
    dpre_hi, dpre_lo, keep, send, s_up = call(
        hidden_back_kernel, steps,
        [scalars, (c_hi, across(model)), (c_lo, across(model)), (wd_hi, whole(down_dims)), (wd_lo, whole(down_dims))]
        + [(slope, across(units)), (wu_hi, whole(up_dims)), (wu_lo, whole(up_dims))],
        [hid_half, hid_half, half_out, half_out, (shaped((units, 128)), whole((units, 128)))],
        [pltpu.VMEM((model, WIDE), F32)],
        name="hidden_back",
        pin=False,
        pin_out=PIN_MID,
    )
    send = settle([g_down], send, keep)
    half = glue(add_kernel, scalars, [keep, swap(after(send, g_down.out), 1)], [half_shape], "core_sum", 2)[0]
    half_far = swap(half, 2)
    g_down.send(half)
    g_up = outer(after(n2_hi, half), n2_lo, dpre_hi, dpre_lo, "up_grad")
    settle([g_down], [], g_up.out)
    g_down.send()
    g_up.send(g_down.out)
    keep_down, send_down = call(
        down_kernel, steps,
        [scalars, (wdt_hi, whole(up_dims)), (wdt_lo, whole(up_dims)), (after(act_hi, g_down.out), across(units)), (act_lo, across(units))],
        [half_out, half_out],
        [pltpu.VMEM((model, WIDE), F32)],
        name="down",
        pin=False,
        pin_out=PIN_MID,
    )
    half_far, send_down = settle([g_down, g_up], (half_far, send_down), keep_down)
    half = glue(add_kernel, scalars, [half, half_far], [half_shape], "chip_sum", 2)[0]
    half = after(half, g_down.out, g_up.out)
    other = swap(half, 1)
    come = swap(after(send_down, half), 1)
    other, come = lax.optimization_barrier((other, come))
    own_shape = (chans, span)
    mine_down, send_down = glue(
        partial(halve_kernel, (5,)), scalars, [keep_down, come], [own_shape] * 2, "down_halves", 2
    )
    other = after(other, send_down)
    g_down.send(other)
    g_up.send(other)

    b_hi, b_lo, dq_hi, dq_lo, dp_hi, dp_lo, d_inner_own, s_gain2, s_bias2, s_out, s_query = call(
        inner_back_kernel, steps,
        [scalars, (half, across(2 * chans)), (other, across(2 * chans)), (n2_hi, across(model)), (n2_lo, across(model)), (stats_two, across(8)), cols_in]
        + cot_ins
        + [(w_out, whole((chans, model)))]
        + [(f_query, across(chans)), (f_numer, across(chans)), (quotient, across(chans))],
        [tall_half, tall_half, thin_half, thin_half, pair_half, pair_half, thin, lanes_own, lanes_own, lanes_own, lanes_own],
        [pltpu.VMEM((model, WIDE), F32)] * 3 + [pltpu.VMEM((chans, model), BF16)] * 2,
        name="inner_back",
        pin=False,
        pin_out=PIN_MID,
    )
    dp_hi = settle([g_down, g_up], dp_hi, b_hi)
    g_down.send()
    g_up.send()
    come_down = swap(after(send_down, g_down.out, g_up.out), 2)
    dp_hi = after(dp_hi, g_down.out, g_up.out)
    thin_all, tall_all = whole((chans, span)), whole((model, span))

    def back_at(i):
        return blocks - 1 - i

    pair_spec = pl.BlockSpec((2 * chans, TB), lambda i: (0, back_at(i)))
    prev_spec = pl.BlockSpec((2 * chans, TB), lambda i: (0, jnp.maximum(back_at(i) - 1, 0)))
    band_spec = pl.BlockSpec((TB, 2 * window), lambda i: (back_at(i), 0))
    row_spec = pl.BlockSpec((TB, window), lambda i: (back_at(i), 0))
    kv_hi, kv_lo, d_pair, s_value = call(
        mix_back_kernel, blocks,
        [(dp_hi, pair_spec), (dp_lo, pair_spec), (pair_hi, prev_spec), (pair_lo, prev_spec), (pair_hi, pair_spec), (pair_lo, pair_spec)]
        + [(band[0], band_spec), (band[1], band_spec), (pair_bias, row_spec)],
        [(shaped((2 * chans, span), BF16), pair_spec)] * 2 + [(shaped((span, window)), row_spec), lanes_own],
        [pltpu.VMEM((2 * chans, TB), F32), pltpu.VMEM((2 * chans, 128), F32), pltpu.VMEM((2 * chans, 128), F32)],
        name="mix_back",
        pin=False,
        pin_out=PIN_MID,
    )
    slab = pl.BlockSpec((model // 2, span), lambda i: (i, 0))
    grads = call(
        projection_grads_kernel, 2,
        [scalars, (mixed, thin_all), (b_hi, slab), (b_lo, slab), (dq_hi, thin_all), (dq_lo, thin_all)]
        + [(kv_hi, whole((2 * chans, span))), (kv_lo, whole((2 * chans, span))), (n1_hi, slab), (n1_lo, slab)],
        [(shaped((chans, model)), across(chans, model // 2))] * 4,
        name="projection_grads", pin=False,
    )
    g_mix = Sum(scalars, grads, False)
    dq_hi, kv_hi = after((dq_hi, kv_hi), grads)
    payload_rows = 2 * chans + 8 + span // 8
    payload = (shaped((payload_rows, span)), across(payload_rows))
    keep, send = call(
        project_back_kernel, steps,
        [scalars, (dq_hi, across(chans)), (dq_lo, across(chans)), (kv_hi, across(2 * chans)), (kv_lo, across(2 * chans))]
        + [(wqt_hi, whole(tall_qkv)), (wqt_lo, whole(tall_qkv)), *x_ins, (stats_one, across(8)), cols_in, (d_pair, whole((span, window)))],
        [payload, payload],
        [pltpu.VMEM((model, WIDE), F32)] * 2,
        name="project_back",
        pin=False,
        pin_out=PIN_MID,
    )
    send, come_down = settle([g_down, g_up], (send, come_down), keep, grads)
    live = (jnp.arange(span, dtype=jnp.int32) < lengths[0]).astype(F32)[None, :]
    result = inner_own + live * (mine_down + come_down + down_bias[:, None])
    come = swap(after(send, g_up.out, g_down.out, result), 1)
    mine, send = glue(core_halves_kernel, scalars, [keep, come], [(chans + 8 + span // 16, span)] * 2, "core_halves")
    g_mix.send(send)
    g_up.send(send)
    come = settle([g_mix, g_up], swap(send, 2))
    quarter = (span // 16, span)
    pair_sum, sums = glue(chip_sum_kernel, scalars, [mine, come], [quarter, (8, span)], "chip_sums")
    come, sums, pair_sum = after((come, sums, pair_sum), g_mix.out, g_up.out)
    come, sums, pair_sum = lax.optimization_barrier((come, sums, pair_sum))
    g_mix.send(pair_sum)
    pair_come = add_trade(pair_sum, 4)
    d_inputs, s_gain1, s_bias1 = call(
        partial(input_back_kernel, float(model)), steps,
        [(mine, across(mine.shape[0])), (come, across(mine.shape[0])), (d_inner_own, across(chans)), (x_parts[0], across(chans))]
        + [(stats_one, across(8)), (sums, across(8)), (gain_column, whole((chans, 1)))],
        [thin, lanes_own, lanes_own],
        name="input_back",
        pin=False,
        pin_out=PIN_MID,
    )

    lanes = (s_gain1, s_bias1, s_query, s_value, s_out, s_gain2, s_bias2, s_down, s_up)
    count = sum(x.shape[0] for x in lanes)
    small = call(
        lane_sums_kernel, 1, [(x, whole(x.shape)) for x in lanes], [(shaped((8, count)), whole((8, count)))],
        name="lane_sums", pin=False,
    )[0]
    small, pair_come = settle([g_mix], (small, pair_come))
    pair_sum = glue(add_kernel, scalars, [pair_sum, pair_come], [quarter], "pair_far")[0]
    small, pair_sum = after((small, pair_sum), g_mix.out)
    g_mix.send(small, pair_sum)
    g_up.send(small, pair_sum)
    small_come, pair_come = settle([g_mix, g_up], (add_trade(small, 1), add_trade(pair_sum, 1)))
    pair_sum = glue(add_kernel, scalars, [pair_sum, pair_come], [quarter], "pair_x")[0]
    small = glue(add_kernel, scalars, [small, small_come], [(8, count)], "small_x")[0]
    small, pair_sum = after((small, pair_sum), g_mix.out, g_up.out)
    g_mix.send(small, pair_sum)
    small_come, pair_come = settle([g_mix], (add_trade(small, 2), add_trade(pair_sum, 2)))
    pair_sum = glue(add_kernel, scalars, [pair_sum, pair_come], [quarter], "pair_z")[0]
    small = glue(add_kernel, scalars, [small, small_come], [(8, count)], "small_z")[0]
    small, pair_sum = after((small, pair_sum), g_mix.out)
    g_mix.send(small, pair_sum)
    small_come, pair_come = settle([g_mix], (add_trade(small, 4), swap(pair_sum, 2)))
    pair_half = glue(pair_chips_kernel, scalars, [pair_sum, pair_come], [(span // 8, span)], "pair_chips")[0]
    small = (small + small_come)[0]
    pair_come = swap(pair_half, 1)
    d_pair = glue(pair_cores_kernel, scalars, [pair_half, pair_come], [(span, window)], "pair_cores")[0]
    if not halving:
        d_pair = lax.psum(d_pair, "dp")
        small = lax.psum(small, "dp")
    d_w_out, d_w_query, d_w_key, d_w_value = g_mix.total
    vecs = [small[i * chans : (i + 1) * chans] for i in range(8)]
    return (
        result.T[None],
        d_inputs.T[None],
        vecs[0],
        vecs[1],
        d_w_query.T,
        d_w_key.T,
        d_w_value.T,
        vecs[2],
        vecs[3],
        d_pair,
        d_w_out,
        vecs[4],
        vecs[5],
        vecs[6],
        g_up.total[0],
        small[8 * chans :],
        g_down.total[0],
        vecs[7],
    )


def solution(mesh):
    rows = P("dp", None, "mp")
    vec = P("mp")
    out_dim = P(None, "mp")
    in_dim = P("mp", None)
    return jax.shard_map(
        body,
        mesh=mesh,
        in_specs=(
            rows, P("dp"), vec, vec, out_dim, out_dim, out_dim, vec, vec, P(), in_dim, vec, vec, vec,
            out_dim, vec, in_dim, vec, rows,
        ),
        out_specs=(
            rows, rows, vec, vec, out_dim, out_dim, out_dim, vec, vec, P(), in_dim, vec, vec, vec,
            out_dim, vec, in_dim, vec,
        ),
        check_vma=False,
    )
```

time: 429 us -> 340 us (0.79)
  waiting for transfers between devices: 179 us -> 120 us
  Pallas kernels: 83.9 us -> 137 us
  other arithmetic: 35.7 us -> 1.07 us
  local copies, waits for them, and re-layouts: 49.1 us -> 23.9 us
  starting transfers between devices: 70.6 us -> 48.2 us
    pallas_call x18 -> x44, Pallas kernels: 83.9 us -> 137 us  [call(): return list(run(*arrays))]
    ppermute x43 -> x33, waiting for transfers between devices: 132 us -> 89.6 us  [trade(): return lax.ppermute(block, 'dp', [(i, i ^ flip) for i in range(size)])]
    unnamed x202 -> x174, local copies, waits for them, and re-layouts: 43.8 us -> 20.1 us
    ppermute x43 -> x33, starting transfers between devices: 53.7 us -> 35.1 us  [trade(): return lax.ppermute(block, 'dp', [(i, i ^ flip) for i in range(size)])]
    ppermute x28 -> x24, waiting for transfers between devices: 46.8 us -> 30.8 us  [swap(): return lax.ppermute(block, 'mp', [(i, i ^ bit) for i in range(4)])]
    add x35 -> x2, other arithmetic: 15.4 us -> 1.07 us  [the longest x1 1.06 us: body(): result = inner_own + live * (mine_down + come_down + down_bias[:, None])]
    concatenate x14 -> x0, other arithmetic: 8.15 us -> none  [the longest x10 4.24 us: join(): return jnp.concatenate([low, high], axis=0)]
    select_n x17 -> x0, other arithmetic: 5.89 us -> none  [join(): low = jnp.where(bit == 0, mine, other)]
  transfers between devices with their start and end apart: 71 -> 57, of which waited for: 33 -> 25; matrix products, arithmetic and copies ran while one was open for 9% -> 1% of each run, Pallas kernels for 20% -> 32%
where the time goes in v3:
time: 340 us; the launch traced here: 334 us
  Pallas kernels  137 us (40%)
  waiting for transfers between devices  120 us (35%)
  starting transfers between devices  48.2 us (14%)
  local copies, waits for them, and re-layouts  23.9 us (7%)
    pallas_call x44, Pallas kernels, call(): return list(run(*arrays))  137 us
    ppermute x33, waiting for transfers between devices, trade(): return lax.ppermute(block, 'dp', [(i, i ^ flip) for i in range(size)])  89.6 us
    ppermute x33, starting transfers between devices, trade(): return lax.ppermute(block, 'dp', [(i, i ^ flip) for i in range(size)])  35.1 us
    ppermute x24, waiting for transfers between devices, swap(): return lax.ppermute(block, 'mp', [(i, i ^ bit) for i in range(4)])  30.8 us
    unnamed x174, local copies, waits for them, and re-layouts  20.1 us
    ppermute x24, starting transfers between devices, swap(): return lax.ppermute(block, 'mp', [(i, i ^ bit) for i in range(4)])  13.1 us
  transfers between devices with their start and end apart: 57, of which 25 were waited for; matrix products, arithmetic and copies ran while one was open for 1% of the time, Pallas kernels for 32%

profile of v3, /device:TPU:0, one launch (start us, length us, event | category | flops | bytes accessed | tf_op | source)
XLA Modules:
  0.0 333.8 jit_solution(5167158337401738796)
XLA Ops:
  5.4 4.2 %band.1 = (bf16[1024,512]{1,0:T(8,128)(2,1)}, bf16[1024,512]{1,0:T(8,128)(2,1)}) custom-call(f32[1024,256]{1,0:T(8,128)} %bias.3), custom_call_target="tpu_custom_call" | custom-call | tf_op jit(solution)/shard_map/band/pallas_call | solution.py:107
  9.6 4.6 %up_weights.1 = (bf16[768,768]{1,0:T(8,128)(2,1)}, bf16[768,768]{1,0:T(8,128)(2,1)}, bf16[768,768]{1,0:T(8,128)(2,1)}, bf16[768,768]{1,0:T(8,128)(2,1)}) custom-call(f32[768,768]{1,0:T(8,128)} %w.2), custom_call_target="tpu_custom_call" | custom-call | tf_op jit(solution)/shard_map/up_weights/pallas_call | solution.py:107
  14.3 3.7 %qkv_weights.1 = (bf16[576,768]{1,0:T(8,128)(2,1)}, bf16[576,768]{1,0:T(8,128)(2,1)}, bf16[768,576]{1,0:T(8,128)(2,1)}, bf16[768,576]{1,0:T(8,128)(2,1)}) custom-call(f32[192,768]{1,0:T(8,128)} %bitcast.52, f32[192,768]{1,0:T(8,128)} %bitcast.53, f32[192,768]{1,0:T(8,128)} %bitcast.54), custom_call_target="tpu_custom_call" | custom-call | tf_op jit(solution)/shard_map/qkv_weights/pallas_call | solution.py:107
  26.0 10.5 %attend.1 = (f32[768,8]{1,0:T(8,128)}, f32[192,1024]{1,0:T(8,128)}, f32[192,1024]{1,0:T(8,128)}, f32[192,1024]{1,0:T(8,128)}, f32[192,1024]{1,0:T(8,128)}, /*ind...) custom-call(s32[6]{0:T(128)S(1)} %stack.47.info, ...), custom_call_target="tpu_custom_call" | custom-call | tf_op jit(solution)/shard_map/attend/pallas_call | solution.py:107
  38.0 4.6 %down_weights.1 = (bf16[768,768]{1,0:T(8,128)(2,1)}, bf16[768,768]{1,0:T(8,128)(2,1)}, bf16[768,768]{1,0:T(8,128)(2,1)}, bf16[768,768]{1,0:T(8,128)(2,1)}) custom-call(f32[768,768]{1,0:T(8,128)} %w.3), custom_call_target="tpu_custom_call" | custom-call | tf_op jit(solution)/shard_map/down_weights/pallas_call | solution.py:107
  44.6 3.7 %out_weights.1 = (bf16[768,768]{1,0:T(8,128)(2,1)}, bf16[768,768]{1,0:T(8,128)(2,1)}) custom-call(f32[192,768]{1,0:T(8,128)} %w_out.1, f32[192,768]{1,0:T(8,128)} %copy-done.74, f32[192,768]{1,0:T(8,128)} %collective-permute-done.9.far, f32[192,768]{1,0:T(8,128)} %copy-done.75), custom_call_target="tpu_custom_call" | custom-call | tf_op jit(solution)/shard_map/out_weights/pallas_call | solution.py:107
  48.3 8.2 %collective-permute-done.7.m2 = f32[192,1024]{1,0:T(8,128)} collective-permute-done((f32[192,1024]{1,0:T(8,128)}, f32[192,1024]{1,0:T(8,128)}, u32[]{:S(2)}, u32[]{:S(2)}) %collective-permute-start.7) | collective-permute-done | bytes 786464 | tf_op jit(solution)/shard_map/ppermute | solution.py:554
  59.1 16.2 %hidden.1 = (bf16[768,1024]{1,0:T(8,128)(2,1)S(1)}, bf16[768,1024]{1,0:T(8,128)(2,1)S(1)}, f32[768,1024]{1,0:T(8,128)S(1)}, bf16[768,1024]{1,0:T(8,128)(2,1)S(1)...) custom-call(s32[6]{0:T(128)S(1)} %stack.47.info, ...), custom_call_target="tpu_custom_call" | custom-call | tf_op jit(solution)/shard_map/hidden/pallas_call | solution.py:107
  80.2 7.0 %down_grad.1 = (f32[192,768]{1,0:T(8,128)}, f32[192,768]{1,0:T(8,128)}, f32[192,768]{1,0:T(8,128)}, f32[192,768]{1,0:T(8,128)}, bf16[768,1024]{1,0:T(8,128)(2,1)...) custom-call(s32[6]{0:T(128)S(1)} %stack.47.info, bf16[768,1024]{1,0:T(8,128)(2,1)S(1)} %get-tuple-element.281.a_hi.act_hi, ...), custom_call_target="tpu_custom_call" | custom-call | tf_op jit(solution)/shard_map/down_grad/pallas_call | solution.py:107
  95.1 10.7 %hidden_back.1 = (bf16[768,1024]{1,0:T(8,128)(2,1)}, bf16[768,1024]{1,0:T(8,128)(2,1)}, f32[384,1024]{1,0:T(8,128)}, f32[384,1024]{1,0:T(8,128)}, f32[768,128]{1,0:T(8,128)}) custom-call(s32[6]{0:T(128)S(1)} %stack.47.info, bf16[768,1024]{1,0:T(8,128)(2,1)S(1)} %copy-done.32, bf16[768,1024]{1,0:T(8,128)(2,1)S(1)} %copy-done.33, ...), custom_call_target="tpu_custom_call" | custom-call | tf_op jit(solution)/shard_map/hidden_back/pallas_call | solution.py:107
  113.3 7.2 %up_grad.1 = (f32[192,768]{1,0:T(8,128)}, f32[192,768]{1,0:T(8,128)}, f32[192,768]{1,0:T(8,128)}, f32[192,768]{1,0:T(8,128)}) custom-call(s32[6]{0:T(128)S(1)} %stack.47.info, bf16[768,1024]{1,0:T(8,128)(2,1)S(1)} %get-tuple-element.272.a_hi.n_hi, bf16[768,1024]{1,0:T(8,128)(2,1)S(1)} %get-tuple-element.273.a_lo.n_lo, bf16[768,1024]{1,0:T(8,128)(2,1)S(1)} %copy-done.30, ...), custom_call_target="tpu_custom_call" | custom-call | tf_op jit(solution)/shard_map/up_grad/pallas_call | solution.py:107
  126.9 6.1 %down.1 = (f32[384,1024]{1,0:T(8,128)}, f32[384,1024]{1,0:T(8,128)}) custom-call(s32[6]{0:T(128)S(1)} %stack.47.info, bf16[768,768]{1,0:T(8,128)(2,1)S(1)} %copy-done.36, bf16[768,768]{1,0:T(8,128)(2,1)S(1)} %copy-done.37, bf16[768,1024]{1,0:T(8,128)(2,1)S(1)} %get-tuple-element.281.a_hi.act_hi, bf16[768,1024]{1,0:T(8,128)(2,1)S(1)} %get-tuple-element.246.a_lo.act_lo), custom_call_target="tpu_custom_call" | custom-call | tf_op jit(solution)/shard_map/down/pallas_call | solution.py:107
  133.0 16.7 %collective-permute-done.20.come = f32[192,768]{1,0:T(8,128)S(1)} collective-permute-done((f32[192,768]{1,0:T(8,128)S(1)}, f32[192,768]{1,0:T(8,128)S(1)}, u32[]{:S(2)}, u32[]{:S(2)}) %collective-permute-start.20) | collective-permute-done | bytes 589856 | tf_op jit(solution)/shard_map/ppermute | solution.py:576
  164.4 8.1 %inner_back.1 = (bf16[768,1024]{1,0:T(8,128)(2,1)}, bf16[768,1024]{1,0:T(8,128)(2,1)}, bf16[192,1024]{1,0:T(8,128)(2,1)}, bf16[192,1024]{1,0:T(8,128)(2,1)}, bf1...) custom-call(s32[6]{0:T(128)S(1)} %stack.47.info, ...), custom_call_target="tpu_custom_call" | custom-call | tf_op jit(solution)/shard_map/inner_back/pallas_call | solution.py:107
  184.5 7.0 %mix_back.1 = (bf16[384,1024]{1,0:T(8,128)(2,1)}, bf16[384,1024]{1,0:T(8,128)(2,1)}, f32[1024,256]{1,0:T(8,128)}, f32[192,128]{1,0:T(8,128)}) custom-call(bf16[384,1024]{1,0:T(8,128)(2,1)S(1)} %copy-done.49, bf16[384,1024]{1,0:T(8,128)(2,1)S(1)} %copy-done.50, bf16[384,1024]{1,0:T(8,128)(2,1)S(1)} %copy-done.19, bf16[384,1024]{1,0:T(8,128)(2,1)S(1)} %copy-done.20, ...), custom_call_target="tpu_custom_call" | custom-call | tf_op jit(solution)/shard_map/mix_back/pallas_call | solution.py:107
  193.9 7.5 %projection_grads.1 = (f32[192,768]{1,0:T(8,128)}, f32[192,768]{1,0:T(8,128)}, f32[192,768]{1,0:T(8,128)}, f32[192,768]{1,0:T(8,128)}) custom-call(s32[6]{0:T(128)S(1)} %stack.47.info, f32[192,1024]{1,0:T(8,128)S(1)} %copy-done.13, bf16[768,1024]{1,0:T(8,128)(2,1)S(1)} %copy-done.26, bf16[768,1024]{1,0:T(8,128)(2,1)S(1)} %copy-done.27, ...), custom_call_target="tpu_custom_call" | custom-call | tf_op jit(solution)/shard_map/projection_grads/pallas_call | solution.py:107
  201.4 7.0 %project_back.1 = (f32[520,1024]{1,0:T(8,128)}, f32[520,1024]{1,0:T(8,128)}) custom-call(s32[6]{0:T(128)S(1)} %stack.47.info, bf16[192,1024]{1,0:T(8,128)(2,1)S(1)} %copy-done.22, bf16[192,1024]{1,0:T(8,128)(2,1)S(1)} %copy-done.23, bf16[384,1024]{1,0:T(8,128)(2,1)S(1)} %copy-done.14, bf16[384,1024]{1,0:T(8,128)(2,1)S(1)} %copy-done.16, ...), custom_call_target="tpu_custom_call" | custom-call | tf_op jit(solution)/shard_map/project_back/pallas_call | solution.py:107
  212.3 4.2 %collective-permute-done.34.come = f32[520,1024]{1,0:T(8,128)S(1)} collective-permute-done((f32[520,1024]{1,0:T(8,128)S(1)}, f32[520,1024]{1,0:T(8,128)S(1)}, u32[]{:S(2)}, u32[]{:S(2)}) %collective-permute-start.34) | collective-permute-done | bytes 2129952 | tf_op jit(solution)/shard_map/ppermute | solution.py:554
  222.3 18.0 %collective-permute-done.37.refs_1_ = f32[96,768]{1,0:T(8,128)S(1)} collective-permute-done((f32[96,768]{1,0:T(8,128)S(1)}, f32[96,768]{1,0:T(8,128)S(1)}, u32[]{:S(2)}, u32[]{:S(2)}) %collective-permute-start.37) | collective-permute-done | bytes 294944 | tf_op jit(solution)/shard_map/ppermute | solution.py:576
  258.5 7.0 %collective-permute-done.42.refs_1_ = f32[64,1024]{1,0:T(8,128)} collective-permute-done((f32[64,1024]{1,0:T(8,128)}, f32[64,1024]{1,0:T(8,128)}, u32[]{:S(2)}, u32[]{:S(2)}) %collective-permute-start.42) | collective-permute-done | bytes 262176 | tf_op jit(solution)/shard_map/ppermute | solution.py:576
  272.6 16.0 %collective-permute-done.46.refs_1_ = f32[8,2304]{1,0:T(8,128)S(1)} collective-permute-done((f32[8,2304]{1,0:T(8,128)S(1)}, f32[8,2304]{1,0:T(8,128)S(1)}, u32[]{:S(2)}, u32[]{:S(2)}) %collective-permute-start.46) | collective-permute-done | bytes 73760 | tf_op jit(solution)/shard_map/ppermute | solution.py:576
  288.7 4.1 %collective-permute-done.43.come = f32[192,768]{1,0:T(8,128)S(1)} collective-permute-done((f32[192,768]{1,0:T(8,128)S(1)}, f32[192,768]{1,0:T(8,128)S(1)}, u32[]{:S(2)}, u32[]{:S(2)}) %collective-permute-start.43) | collective-permute-done | bytes 589856 | tf_op jit(solution)/shard_map/ppermute | solution.py:576
  301.2 10.6 %collective-permute-done.50.refs_1_ = f32[8,2304]{1,0:T(8,128)S(1)} collective-permute-done((f32[8,2304]{1,0:T(8,128)S(1)}, f32[8,2304]{1,0:T(8,128)S(1)}, u32[]{:S(2)}, u32[]{:S(2)}) %collective-permute-start.50) | collective-permute-done | bytes 73760 | tf_op jit(solution)/shard_map/ppermute | solution.py:576
  316.8 8.7 %collective-permute-done.54 = f32[8,2304]{1,0:T(8,128)S(1)} collective-permute-done((f32[8,2304]{1,0:T(8,128)S(1)}, f32[8,2304]{1,0:T(8,128)S(1)}, u32[]{:S(2)}, u32[]{:S(2)}) %collective-permute-start.54) | collective-permute-done | bytes 73760 | tf_op jit(solution)/shard_map/ppermute | solution.py:576
  (319 shorter events, 129.5 us)
Async XLA Ops:
  0.7 21.0 %collective-permute-start.2 = (f32[192,1024]{1,0:T(8,128)}, f32[192,1024]{1,0:T(8,128)S(1)}, u32[]{:S(2)}, u32[]{:S(2)}) collective-permute-start(f32[192,1024]{1,0:T(8,128)} %bitcast.41), channel_id=1, source_target_pairs={{0,2},{1,3},{2,0},{3,1},{4,6},{5,7},{6,4},{7,5},{8,10},{9,11},{10,... | collective-permute-start | bytes 2359304 | tf_op jit(solution)/shard_map/ppermute | solution.py:554
  4.5 17.1 %collective-permute-start.1 = (f32[8,256]{1,0:T(8,128)S(1)}, f32[8,256]{1,0:T(8,128)S(1)}, u32[]{:S(2)}, u32[]{:S(2)}) collective-permute-start(f32[8,256]{1,0:T(8,128)S(1)} %pad.4.v0), channel_id=1, source_target_pairs={{0,2},{1,3},{2,0},{3,1},{4,6},{5,7},{6,4},{7,5},{8,10},{9,11},{10,... | collective-permute-start | bytes 24584 | tf_op jit(solution)/shard_map/ppermute | solution.py:554
  4.6 20.2 %collective-permute-start = (f32[192,1024]{1,0:T(8,128)}, f32[192,1024]{1,0:T(8,128)S(1)}, u32[]{:S(2)}, u32[]{:S(2)}) collective-permute-start(f32[192,1024]{1,0:T(8,128)} %bitcast.42), channel_id=1, source_target_pairs={{0,1},{1,0},{2,3},{3,2},{4,5},{5,4},{6,7},{7,6},{8,9},{9,8},{10,11... | collective-permute-start | bytes 2359304 | tf_op jit(solution)/shard_map/ppermute | solution.py:554
  36.5 20.0 %collective-permute-start.7 = (f32[192,1024]{1,0:T(8,128)}, f32[192,1024]{1,0:T(8,128)}, u32[]{:S(2)}, u32[]{:S(2)}) collective-permute-start(f32[192,1024]{1,0:T(8,128)} %get-tuple-element.232.m0.mixed), channel_id=1, source_target_pairs={{0,2},{1,3},{2,0},{3,1},{4,6},{5,7},{6,4},{7,5},{8,10},{9,11},{10,... | collective-permute-start | bytes 2359304 | tf_op jit(solution)/shard_map/ppermute | solution.py:554
  56.5 21.5 %collective-permute-start.13 = (f32[192,1024]{1,0:T(8,128)S(1)}, f32[192,1024]{1,0:T(8,128)S(1)}, u32[]{:S(2)}, u32[]{:S(2)}) collective-permute-start(f32[192,1024]{1,0:T(8,128)S(1)} %bitcast.47), channel_id=1, source_target_pairs={{0,2},{1,3},{2,0},{3,1},{4,6},{5,7},{6,4},{7,5},{8,10},{9,11},{10,... | collective-permute-start | bytes 2359304 | tf_op jit(solution)/shard_map/ppermute | solution.py:554
  57.4 20.7 %collective-permute-start.12 = (f32[192,1024]{1,0:T(8,128)S(1)}, f32[192,1024]{1,0:T(8,128)S(1)}, u32[]{:S(2)}, u32[]{:S(2)}) collective-permute-start(f32[192,1024]{1,0:T(8,128)S(1)} %bitcast.48), channel_id=1, source_target_pairs={{0,1},{1,0},{2,3},{3,2},{4,5},{5,4},{6,7},{7,6},{8,9},{9,8},{10,11... | collective-permute-start | bytes 2359304 | tf_op jit(solution)/shard_map/ppermute | solution.py:554
  87.3 18.5 %collective-permute-start.15 = (f32[192,768]{1,0:T(8,128)}, f32[192,768]{1,0:T(8,128)S(1)}, u32[]{:S(2)}, u32[]{:S(2)}) collective-permute-start(f32[192,768]{1,0:T(8,128)} %get-tuple-element.250), channel_id=1, source_target_pairs={{0,4},{4,0},{8,12},{12,8},{16,20},{20,16},{24,28},{28,24},{1,5},{5... | collective-permute-start | bytes 1769480 | tf_op jit(solution)/shard_map/ppermute | solution.py:576
  111.4 39.6 %collective-permute-start.23 = (f32[384,1024]{1,0:T(8,128)S(1)}, f32[384,1024]{1,0:T(8,128)S(1)}, u32[]{:S(2)}, u32[]{:S(2)}) collective-permute-start(f32[384,1024]{1,0:T(8,128)S(1)} %core_sum.1.refs_0_), channel_id=1, source_target_pairs={{0,2},{1,3},{2,0},{3,1},{4,6},{5,7},{6,4},{7,5},{8,10},{9,11},{10,... | collective-permute-start | bytes 4718600 | tf_op jit(solution)/shard_map/ppermute | solution.py:554
  121.9 27.8 %collective-permute-start.20 = (f32[192,768]{1,0:T(8,128)S(1)}, f32[192,768]{1,0:T(8,128)S(1)}, u32[]{:S(2)}, u32[]{:S(2)}) collective-permute-start(f32[192,768]{1,0:T(8,128)S(1)} %sum_stage_1.3.held), channel_id=1, source_target_pairs={{0,16},{4,20},{8,24},{12,28},{16,0},{20,4},{24,8},{28,12},{1,17},{... | collective-permute-start | bytes 1769480 | tf_op jit(solution)/shard_map/ppermute | solution.py:576
  124.6 25.1 %collective-permute-start.21 = (f32[192,768]{1,0:T(8,128)}, f32[192,768]{1,0:T(8,128)S(1)}, u32[]{:S(2)}, u32[]{:S(2)}) collective-permute-start(f32[192,768]{1,0:T(8,128)} %get-tuple-element.283), channel_id=1, source_target_pairs={{0,4},{4,0},{8,12},{12,8},{16,20},{20,16},{24,28},{28,24},{1,5},{5... | collective-permute-start | bytes 1769480 | tf_op jit(solution)/shard_map/ppermute | solution.py:576
  125.3 25.7 %collective-permute-start.22 = (f32[192,768]{1,0:T(8,128)S(1)}, f32[192,768]{1,0:T(8,128)S(1)}, u32[]{:S(2)}, u32[]{:S(2)}) collective-permute-start(f32[192,768]{1,0:T(8,128)S(1)} %copy-done.86), channel_id=1, source_target_pairs={{0,8},{4,12},{8,0},{12,4},{16,24},{20,28},{24,16},{28,20},{1,9},{5... | collective-permute-start | bytes 1769480 | tf_op jit(solution)/shard_map/ppermute | solution.py:576
  177.0 31.4 %collective-permute-start.33 = (f32[192,1024]{1,0:T(8,128)S(1)}, f32[192,1024]{1,0:T(8,128)S(1)}, u32[]{:S(2)}, u32[]{:S(2)}) collective-permute-start(f32[192,1024]{1,0:T(8,128)S(1)} %get-tuple-element.345), channel_id=1, source_target_pairs={{0,2},{1,3},{2,0},{3,1},{4,6},{5,7},{6,4},{7,5},{8,10},{9,11},{10,... | collective-permute-start | bytes 2359304 | tf_op jit(solution)/shard_map/ppermute | solution.py:554
  178.2 30.2 %collective-permute-start.30 = (f32[192,768]{1,0:T(8,128)S(1)}, f32[192,768]{1,0:T(8,128)S(1)}, u32[]{:S(2)}, u32[]{:S(2)}) collective-permute-start(f32[192,768]{1,0:T(8,128)S(1)} %get-tuple-element.316.refs_0_), channel_id=1, source_target_pairs={{0,4},{4,0},{8,12},{12,8},{16,20},{20,16},{24,28},{28,24},{1,5},{5... | collective-permute-start | bytes 1769480 | tf_op jit(solution)/shard_map/ppermute | solution.py:576
  179.4 29.0 %collective-permute-start.31 = (f32[192,768]{1,0:T(8,128)S(1)}, f32[192,768]{1,0:T(8,128)S(1)}, u32[]{:S(2)}, u32[]{:S(2)}) collective-permute-start(f32[192,768]{1,0:T(8,128)S(1)} %get-tuple-element.317.refs_2_), channel_id=1, source_target_pairs={{0,8},{4,12},{8,0},{12,4},{16,24},{20,28},{24,16},{28,20},{1,9},{5... | collective-permute-start | bytes 1769480 | tf_op jit(solution)/shard_map/ppermute | solution.py:576
  180.5 27.9 %collective-permute-start.32 = (f32[192,768]{1,0:T(8,128)S(1)}, f32[192,768]{1,0:T(8,128)S(1)}, u32[]{:S(2)}, u32[]{:S(2)}) collective-permute-start(f32[192,768]{1,0:T(8,128)S(1)} %sum_stage_1.4.held), channel_id=1, source_target_pairs={{0,16},{4,20},{8,24},{12,28},{16,0},{20,4},{24,8},{28,12},{1,17},{... | collective-permute-start | bytes 1769480 | tf_op jit(solution)/shard_map/ppermute | solution.py:576
  217.3 26.0 %collective-permute-start.39 = (f32[264,1024]{1,0:T(8,128)S(1)}, f32[264,1024]{1,0:T(8,128)S(1)}, u32[]{:S(2)}, u32[]{:S(2)}) collective-permute-start(f32[264,1024]{1,0:T(8,128)S(1)} %get-tuple-element.356), channel_id=1, source_target_pairs={{0,2},{1,3},{2,0},{3,1},{4,6},{5,7},{6,4},{7,5},{8,10},{9,11},{10,... | collective-permute-start | bytes 3244040 | tf_op jit(solution)/shard_map/ppermute | solution.py:554
  218.3 22.0 %collective-permute-start.35 = (f32[192,768]{1,0:T(8,128)S(1)}, f32[192,768]{1,0:T(8,128)S(1)}, u32[]{:S(2)}, u32[]{:S(2)}) collective-permute-start(f32[192,768]{1,0:T(8,128)S(1)} %copy-done.85), channel_id=1, source_target_pairs={{0,4},{4,0},{8,12},{12,8},{16,20},{20,16},{24,28},{28,24},{1,5},{5... | collective-permute-start | bytes 1769480 | tf_op jit(solution)/shard_map/ppermute | solution.py:576
  219.2 21.1 %collective-permute-start.36 = (f32[192,768]{1,0:T(8,128)S(1)}, f32[192,768]{1,0:T(8,128)S(1)}, u32[]{:S(2)}, u32[]{:S(2)}) collective-permute-start(f32[192,768]{1,0:T(8,128)S(1)} %copy-done.84), channel_id=1, source_target_pairs={{0,8},{4,12},{8,0},{12,4},{16,24},{20,28},{24,16},{28,20},{1,9},{5... | collective-permute-start | bytes 1769480 | tf_op jit(solution)/shard_map/ppermute | solution.py:576
  220.8 19.5 %collective-permute-start.37 = (f32[96,768]{1,0:T(8,128)S(1)}, f32[96,768]{1,0:T(8,128)S(1)}, u32[]{:S(2)}, u32[]{:S(2)}) collective-permute-start(f32[96,768]{1,0:T(8,128)S(1)} %get-tuple-element.359.refs_0_), channel_id=1, source_target_pairs={{0,8},{4,12},{8,0},{12,4},{16,24},{20,28},{24,16},{28,20},{1,9},{5... | collective-permute-start | bytes 884744 | tf_op jit(solution)/shard_map/ppermute | solution.py:576
  221.2 19.1 %collective-permute-start.38 = (f32[96,768]{1,0:T(8,128)S(1)}, f32[96,768]{1,0:T(8,128)S(1)}, u32[]{:S(2)}, u32[]{:S(2)}) collective-permute-start(f32[96,768]{1,0:T(8,128)S(1)} %get-tuple-element.360.refs_2_), channel_id=1, source_target_pairs={{0,4},{4,0},{8,12},{12,8},{16,20},{20,16},{24,28},{28,24},{1,5},{5... | collective-permute-start | bytes 884744 | tf_op jit(solution)/shard_map/ppermute | solution.py:576
  267.7 25.1 %collective-permute-start.43 = (f32[192,768]{1,0:T(8,128)S(1)}, f32[192,768]{1,0:T(8,128)S(1)}, u32[]{:S(2)}, u32[]{:S(2)}) collective-permute-start(f32[192,768]{1,0:T(8,128)S(1)} %sum_stage_1.5.held), channel_id=1, source_target_pairs={{0,16},{4,20},{8,24},{12,28},{16,0},{20,4},{24,8},{28,12},{1,17},{... | collective-permute-start | bytes 1769480 | tf_op jit(solution)/shard_map/ppermute | solution.py:576
  268.2 24.6 %collective-permute-start.44 = (f32[192,768]{1,0:T(8,128)S(1)}, f32[192,768]{1,0:T(8,128)S(1)}, u32[]{:S(2)}, u32[]{:S(2)}) collective-permute-start(f32[192,768]{1,0:T(8,128)S(1)} %copy-done.52), channel_id=1, source_target_pairs={{0,4},{4,0},{8,12},{12,8},{16,20},{20,16},{24,28},{28,24},{1,5},{5... | collective-permute-start | bytes 1769480 | tf_op jit(solution)/shard_map/ppermute | solution.py:576
  269.1 24.7 %collective-permute-start.45 = (f32[192,768]{1,0:T(8,128)S(1)}, f32[192,768]{1,0:T(8,128)S(1)}, u32[]{:S(2)}, u32[]{:S(2)}) collective-permute-start(f32[192,768]{1,0:T(8,128)S(1)} %copy-done.54), channel_id=1, source_target_pairs={{0,8},{4,12},{8,0},{12,4},{16,24},{20,28},{24,16},{28,20},{1,9},{5... | collective-permute-start | bytes 1769480 | tf_op jit(solution)/shard_map/ppermute | solution.py:576
  270.6 18.1 %collective-permute-start.47 = (f32[64,1024]{1,0:T(8,128)S(1)}, f32[64,1024]{1,0:T(8,128)S(1)}, u32[]{:S(2)}, u32[]{:S(2)}) collective-permute-start(f32[64,1024]{1,0:T(8,128)S(1)} %pair_far.1.refs_0_), channel_id=1, source_target_pairs={{0,4},{4,0},{8,12},{12,8},{16,20},{20,16},{24,28},{28,24},{1,5},{5... | collective-permute-start | bytes 786440 | tf_op jit(solution)/shard_map/ppermute | solution.py:576
  (120 other events, 873.8 us)
